TPU v7x, 128 devices: a whole 4x4x4 slice. The times are simulated.
128 devices in a mesh: gx: 8 (over x_hi, z), yz: 16 (over x_lo, y, core).
Axes of the slice: x: 4 (x_hi: 2, x_lo: 2; x = x_hi * 2 + x_lo), y: 4, z: 4, core: 2. Of those that a mesh axis runs over, the one named last changes fastest.
Arguments:
- positions: bfloat16 [3, 32768], P(None, ('gx', 'yz')), may hold values from 0 to 1
- species: int32 [32768], P(('gx', 'yz')), may hold values from 0 to 5
- features: bfloat16 [32768, 512], P(('gx', 'yz')), may hold values from -6 to 6
- move_dest: int32 [256], P(('gx', 'yz')), may hold values from 0 to 15, as said below
- move_slot: int32 [256], P(('gx', 'yz')), may hold values from 0 to 1, as said below
- halo_list: int32 [4096], P(('gx', 'yz')), may hold values from 0 to 255
- neighbours: int32 [32768, 64], P(('gx', 'yz')), may hold values from 0 to 383, as said below
- neighbour_count: int32 [32768], P(('gx', 'yz')), may hold values from 16 to 64
- wave_index: int32 [3, 4096], replicated, may hold values from -32 to 32, as said below
- radial_in: bfloat16 [8, 64], replicated, may hold values from -2 to 2
- radial_mid: bfloat16 [2, 64, 64], replicated, may hold values from -0.75 to 0.75
- radial_out: bfloat16 [64, 512], replicated, may hold values from -0.75 to 0.75
- up_weight: bfloat16 [2, 128, 128], replicated, may hold values from -0.5 to 0.5
- prod_weight: float32 [6, 640], replicated, may hold values from -4 to 4
- out_weight: bfloat16 [2, 128, 128], replicated, may hold values from -0.5 to 0.5
- skip_weight: bfloat16 [2, 128, 128], replicated, may hold values from -0.5 to 0.5
- charge_weight: bfloat16 [128, 8], replicated, may hold values from -0.5 to 0.5
- field_weight: float32 [8, 128], replicated, may hold values from -2 to 2
- read_weight: bfloat16 [128, 16], replicated, may hold values from -0.5 to 0.5
- read_vector: float32 [16], replicated, may hold values from -1.5 to 1.5
- force_weight: float32 [128], replicated, may hold values from -0.5 to 0.5
Outputs:
- forces: float32 [3, 32768], P(None, ('gx', 'yz'))
- energies: float32 [32768], P(('gx', 'yz'))
Inputs may be any that keep to these rules, and one draw needn't show every extreme that they name: `move_dest`: the destination lies in the same gx row. Exactly 2 blocks of each device go to other devices, at most one to any one device, and each device receives exactly 2 blocks; the others stay. `move_slot`: the 2 blocks that a device holds after the move take its 2 slots once each. `neighbours`: row of the device's table: its working atoms, then the ghosts from gx - 1, gx + 1, yz - 1, yz + 1. Never the atom itself; slots from neighbour_count on are padding. `wave_index`: row 0 runs from 1 to 16, row 1 from -32 to 32, row 2 from -2 to 2.
All inputs are finite; a program needn't handle non-finite values.
Results may differ from a plain program's by a relative error of at most 0.0028.
Values may be sent and summed in bfloat16 or wider, within the bound.
No kernel may reach another device: no remote copies, remote signals or barrier semaphores. Data moves between devices by JAX's collectives and lax.ppermute only.
A program may use at most 64 MiB of HBM per device.

v0:
```python
import math

import jax
import jax.numpy as jnp
from jax import lax
from jax.sharding import PartitionSpec as P

MOVES = 2


highest = lax.Precision.HIGHEST
two_pi = 2.0 * math.pi
cutoff_radius = 3.5
basis_sharpness = 4.0
ewald_width = 0.1
ewald_scale = 0.01
atom_step = 64
wave_step = 512


def side_by_side(arrays, axis, dim, along):
    columns = [a.reshape(*a.shape[:along], -1) for a in arrays]
    both = jnp.concatenate(columns, axis=along)
    out, at, outs = (lax.all_gather(both, axis, axis=dim, tiled=True), 0, [])
    for a, column in zip(arrays, columns):
        piece = out[..., at : at + column.shape[along]]
        outs.append(piece.reshape(*piece.shape[:along], *a.shape[along:]))
        at += column.shape[along]
    return tuple(outs)


def padded(value, sides, width):
    edges = {}
    for axis, dim in sides:
        count, length = (lax.axis_size(axis), value.shape[dim])
        up = [(i, (i + 1) % count) for i in range(count)]
        last = lax.slice_in_dim(value, length - width, length, axis=dim)
        leading = lax.slice_in_dim(value, 0, width, axis=dim)
        edges[dim] = (
            lax.ppermute(last, axis, up),
            lax.ppermute(leading, axis, [(b, a) for a, b in up]),
        )
    done = []
    for _, dim in sides:
        low, high = edges[dim]
        around = [(width, width) if d in done else (0, 0) for d in range(value.ndim)]
        value = jnp.concatenate([jnp.pad(low, around), value, jnp.pad(high, around)], axis=dim)
        done.append(dim)
    return value


def joined_along(tiles, dim):
    lengths = list(tiles.shape[1:])
    lengths[dim] *= tiles.shape[0]
    return jnp.moveaxis(tiles, 0, dim).reshape(lengths)


def from_everyone(value, axis):
    copies = jnp.broadcast_to(value, (lax.axis_size(axis), *value.shape))
    return lax.all_to_all(copies, axis, split_axis=0, concat_axis=0, tiled=True)


def collect_2(value, axis, dim):
    return joined_along(from_everyone(value, axis), dim)


def wave_vectors(wave_index, domains_x, domains_y):
    scales = jnp.array([two_pi / domains_x, two_pi / domains_y, two_pi], jnp.float32)
    wavevectors = wave_index.astype(jnp.float32) * scales[:, None]
    squared = jnp.sum(wavevectors * wavevectors, axis=0)
    prefactor = 8.0 * math.pi * ewald_scale / (domains_x * domains_y)
    weights = prefactor * jnp.exp(-0.5 * ewald_width * ewald_width * squared) / squared
    return (wavevectors, weights)


def phase_of(absolute, wavevectors):
    return (
        absolute[0][:, None] * wavevectors[0][None, :]
        + absolute[1][:, None] * wavevectors[1][None, :]
        + absolute[2][:, None] * wavevectors[2][None, :]
    )


def structure_terms(absolute, charges, wavevectors):
    stride = math.gcd(wavevectors.shape[1], wave_step)
    block_count = wavevectors.shape[1] // stride

    def one_block(block_index):
        wave_block = lax.dynamic_slice_in_dim(wavevectors, block_index * stride, stride, 1)
        phases = phase_of(absolute, wave_block)
        real_part = jnp.einsum("ak,aq->kq", jnp.cos(phases), charges, precision=highest)
        imag_part = jnp.einsum("ak,aq->kq", jnp.sin(phases), charges, precision=highest)
        return (real_part, imag_part)

    real_part, imag_part = lax.map(one_block, jnp.arange(block_count, dtype=jnp.int32))
    latent = charges.shape[1]
    return (real_part.reshape(-1, latent), imag_part.reshape(-1, latent))


def field_terms(absolute, wavevectors, weights, total_real, total_imag):
    scaled_real = weights[:, None] * total_real
    scaled_imag = weights[:, None] * total_imag
    right_cos = jnp.concatenate(
        [scaled_real] + [-wavevectors[direction][:, None] * scaled_imag for direction in range(3)],
        axis=1,
    )
    right_sin = jnp.concatenate(
        [scaled_imag] + [wavevectors[direction][:, None] * scaled_real for direction in range(3)],
        axis=1,
    )
    stride = math.gcd(wavevectors.shape[1], wave_step)
    block_count = wavevectors.shape[1] // stride

    def accumulate(block_index, running):
        wave_block = lax.dynamic_slice_in_dim(wavevectors, block_index * stride, stride, 1)
        phases = phase_of(absolute, wave_block)
        cos_right = lax.dynamic_slice_in_dim(right_cos, block_index * stride, stride, 0)
        sin_right = lax.dynamic_slice_in_dim(right_sin, block_index * stride, stride, 0)
        running = running + jnp.dot(jnp.cos(phases), cos_right, precision=highest)
        return running + jnp.dot(jnp.sin(phases), sin_right, precision=highest)

    initial = jnp.zeros((absolute.shape[1], right_cos.shape[1]), jnp.float32)
    return lax.fori_loop(0, block_count, accumulate, initial)


def project_pair(feature, weights):
    channels = weights.shape[1]
    row_count = feature.shape[0]
    scalar = jnp.dot(feature[:, :channels], weights[0], preferred_element_type=jnp.float32)
    vector = jnp.dot(
        feature[:, channels:].reshape(row_count * 3, channels),
        weights[1],
        preferred_element_type=jnp.float32,
    )
    return jnp.concatenate([scalar, vector.reshape(row_count, 3 * channels)], axis=1)


def edge_products(
    table_pos, table_up, centre_pos, nbr_rows, nbr_live, coeffs, radial_in, radial_mid, radial_out
):
    atom_count, slot_count = nbr_rows.shape
    edge_count = atom_count * slot_count
    table_size = table_up.shape[0]
    flat_rows = nbr_rows.reshape(edge_count)
    row_onehot = (flat_rows[:, None] == jnp.arange(table_size, dtype=jnp.int32)[None, :]).astype(
        jnp.bfloat16
    )
    picked_pos = jnp.dot(row_onehot.astype(jnp.float32), table_pos.T, precision=highest)
    offset = (picked_pos.T.reshape(3, atom_count, slot_count) - centre_pos[:, :, None]).reshape(
        3, edge_count
    )
    distance = jnp.sqrt(jnp.sum(offset * offset, axis=0))
    scaled_dist = distance / cutoff_radius
    envelope = 1.0 - 28.0 * scaled_dist**6 + 48.0 * scaled_dist**7 - 21.0 * scaled_dist**8
    alive_mask = (
        (jnp.arange(slot_count, dtype=jnp.int32)[None, :] < nbr_live[:, None])
        .astype(jnp.float32)
        .reshape(edge_count)
    )
    basis_count = radial_in.shape[0]
    centres = jnp.arange(basis_count, dtype=jnp.float32) * (cutoff_radius / (basis_count - 1))
    radial_basis = jnp.exp(-basis_sharpness * (distance[:, None] - centres[None, :]) ** 2).astype(
        jnp.bfloat16
    )
    hidden = jax.nn.silu(
        jnp.dot(radial_basis, radial_in, preferred_element_type=jnp.float32)
    ).astype(jnp.bfloat16)
    hidden = jax.nn.silu(jnp.dot(hidden, radial_mid[0], preferred_element_type=jnp.float32)).astype(
        jnp.bfloat16
    )
    hidden = jax.nn.silu(jnp.dot(hidden, radial_mid[1], preferred_element_type=jnp.float32)).astype(
        jnp.bfloat16
    )
    radial = (
        jnp.dot(hidden, radial_out, preferred_element_type=jnp.float32)
        * (envelope * alive_mask)[:, None]
    ).astype(jnp.bfloat16)
    channels = radial.shape[1] // 4
    gathered = jnp.dot(row_onehot, table_up, preferred_element_type=jnp.float32)

    def column_block(source, number):
        return source[:, number * channels : (number + 1) * channels].astype(jnp.float32)

    norm_factor = 1.0 / math.sqrt(slot_count)

    def neighbour_sum(values):
        return jnp.sum(values.reshape(atom_count, slot_count, channels), axis=1) * norm_factor

    up_scalar = column_block(gathered, 0)
    up_vector = [column_block(gathered, 1 + direction) for direction in range(3)]
    along = (
        up_vector[0] * offset[0][:, None]
        + up_vector[1] * offset[1][:, None]
        + up_vector[2] * offset[2][:, None]
    )
    scalar_msg = neighbour_sum(
        column_block(radial, 0) * up_scalar + column_block(radial, 1) * along
    )
    radial_scalar = column_block(radial, 2) * up_scalar
    radial_vector = column_block(radial, 3)
    vector_msg = [
        neighbour_sum(
            radial_scalar * offset[direction][:, None] + radial_vector * up_vector[direction]
        )
        for direction in range(3)
    ]
    square_sum = (
        vector_msg[0] * vector_msg[0]
        + vector_msg[1] * vector_msg[1]
        + vector_msg[2] * vector_msg[2]
    )
    path_weights = [coeffs[:, number * channels : (number + 1) * channels] for number in range(5)]
    scalar_prod = (
        path_weights[0] * scalar_msg
        + path_weights[1] * scalar_msg * scalar_msg
        + path_weights[2] * square_sum
    )
    vector_prod = [
        path_weights[3] * vector_msg[direction]
        + path_weights[4] * scalar_msg * vector_msg[direction]
        for direction in range(3)
    ]
    return jnp.concatenate([scalar_prod] + vector_prod, axis=1).astype(jnp.bfloat16)


def atom_results(
    work_feat,
    products,
    charges,
    efield,
    out_weight,
    skip_weight,
    field_weight,
    read_weight,
    read_vector,
    force_weight,
):
    channels = out_weight.shape[1]
    latent = charges.shape[1]
    mixed_feat = project_pair(products, out_weight) + project_pair(work_feat, skip_weight)
    potential = efield[:, :latent]
    scalars = mixed_feat[:, :channels] + jnp.dot(potential, field_weight, precision=highest)
    readout = jax.nn.silu(
        jnp.dot(scalars.astype(jnp.bfloat16), read_weight, preferred_element_type=jnp.float32)
    )
    energy = jnp.dot(readout, read_vector, precision=highest) + 0.5 * jnp.sum(
        charges * potential, axis=1
    )
    forces = [
        jnp.dot(
            mixed_feat[:, (1 + direction) * channels : (2 + direction) * channels],
            force_weight,
            precision=highest,
        )
        + jnp.sum(charges * efield[:, (1 + direction) * latent : (2 + direction) * latent], axis=1)
        for direction in range(3)
    ]
    return jnp.stack(forces + [energy])


def pick_float(chosen, source):
    return jnp.einsum("ab,bij->aij", chosen, source, precision=highest)


def pick_half(chosen, source):
    return jnp.einsum(
        "ab,bij->aij", chosen.astype(jnp.bfloat16), source, preferred_element_type=jnp.float32
    )


def on_device(
    positions,
    species,
    features,
    move_dest,
    move_slot,
    halo_list,
    neighbours,
    neighbour_count,
    wave_index,
    radial_in,
    radial_mid,
    radial_out,
    up_weight,
    prod_weight,
    out_weight,
    skip_weight,
    charge_weight,
    field_weight,
    read_weight,
    read_vector,
    force_weight,
):
    blocks = move_dest.shape[0]
    atom_count = positions.shape[1]
    block_size = atom_count // blocks
    channels = up_weight.shape[1]
    domains_x = lax.axis_size("gx")
    domains_y = lax.axis_size("yz")
    column = lax.axis_index("yz")
    layer_row = lax.axis_index("gx")
    column_f = column.astype(jnp.float32)
    slot_iota = jnp.arange(blocks, dtype=jnp.int32)
    slot_float = slot_iota.astype(jnp.float32)
    moving = move_dest != column
    meta_rows = jnp.stack(
        [
            move_slot.astype(jnp.float32) + 1.0,
            slot_float,
            jnp.zeros((blocks,), jnp.float32) + column_f + 1.0,
            move_dest.astype(jnp.float32) + 1.0,
        ],
        axis=1,
    )
    home_geo = jnp.concatenate(
        [
            positions.reshape(3, blocks, block_size).transpose(1, 0, 2),
            species.astype(jnp.bfloat16).reshape(blocks, 1, block_size),
            jnp.broadcast_to(meta_rows[:, :, None], (blocks, 4, block_size)).astype(jnp.bfloat16),
        ],
        axis=1,
    )
    home_feat = features.reshape(blocks, block_size, 4 * channels)
    stay_pick = ((move_slot[None, :] == slot_iota[:, None]) & ~moving[None, :]).astype(jnp.float32)
    move_rank = jnp.cumsum(moving.astype(jnp.int32)) - 1
    out_pick = (
        moving[None, :] & (move_rank[None, :] == jnp.arange(MOVES, dtype=jnp.int32)[:, None])
    ).astype(jnp.float32)
    out_geo = pick_half(out_pick, home_geo).astype(jnp.bfloat16)
    out_feat = pick_half(out_pick, home_feat).astype(jnp.bfloat16)
    piece_geo, piece_feat = side_by_side((out_geo, out_feat), "yz", 0, 1)
    addressed = piece_geo[:, 7, 0].astype(jnp.float32) == column_f + 1.0
    chosen = (
        addressed[None, :]
        & (piece_geo[:, 4, 0].astype(jnp.float32)[None, :] == slot_float[:, None] + 1.0)
    ).astype(jnp.float32)
    arrive_geo = pick_half(chosen, piece_geo)
    arrive_feat = pick_half(chosen, piece_feat)
    work_geo = pick_half(stay_pick, home_geo) + arrive_geo
    work_feat = (
        (pick_half(stay_pick, home_feat) + arrive_feat)
        .astype(jnp.bfloat16)
        .reshape(atom_count, 4 * channels)
    )
    work_pos = work_geo[:, :3].transpose(1, 0, 2).reshape(3, atom_count)
    work_species = work_geo[:, 3].reshape(atom_count)
    home_of_slot = work_geo[:, 6, 0] - 1.0
    block_of_slot = work_geo[:, 5, 0]
    arrived = home_of_slot != column_f
    list_pick = (halo_list[:, None] == jnp.arange(atom_count, dtype=jnp.int32)[None, :]).astype(
        jnp.float32
    )
    send_pos = jnp.dot(work_pos, list_pick.T, precision=highest).astype(jnp.bfloat16)
    send_feat = jnp.dot(
        list_pick.astype(jnp.bfloat16), work_feat, preferred_element_type=jnp.float32
    ).astype(jnp.bfloat16)
    ext_pos, ext_feat = (
        padded(send_pos[None, None], (("gx", 0), ("yz", 1)), 1),
        padded(send_feat[None, None], (("gx", 0), ("yz", 1)), 1),
    )
    unit_axes = jnp.eye(3, dtype=jnp.float32)
    ghost_pos = [
        ext_pos[0, 1].astype(jnp.float32) - unit_axes[0][:, None],
        ext_pos[2, 1].astype(jnp.float32) + unit_axes[0][:, None],
        ext_pos[1, 0].astype(jnp.float32) - unit_axes[1][:, None],
        ext_pos[1, 2].astype(jnp.float32) + unit_axes[1][:, None],
    ]
    table_pos = jnp.concatenate([work_pos] + ghost_pos, axis=1)
    table_feat = jnp.concatenate(
        [work_feat, ext_feat[0, 1], ext_feat[2, 1], ext_feat[1, 0], ext_feat[1, 2]], axis=0
    )
    anchor = jnp.stack([layer_row.astype(jnp.float32), column_f, jnp.zeros((), jnp.float32)])
    absolute = work_pos + anchor[:, None]
    charges = jnp.dot(work_feat[:, :channels], charge_weight, preferred_element_type=jnp.float32)
    wavevectors, weights = wave_vectors(wave_index, domains_x, domains_y)
    part_real, part_imag = structure_terms(absolute, charges, wavevectors)
    total_real, total_imag = lax.psum((part_real, part_imag), ("gx", "yz"))
    table_up = project_pair(table_feat, up_weight).astype(jnp.bfloat16)
    onehot = (
        work_species[:, None] == jnp.arange(prod_weight.shape[0], dtype=jnp.float32)[None, :]
    ).astype(jnp.float32)
    coeffs = jnp.dot(onehot, prod_weight, precision=highest)
    block_count = atom_count // atom_step

    def edge_block(pieces):
        return edge_products(
            table_pos,
            table_up,
            pieces[2],
            pieces[0],
            pieces[1],
            pieces[3],
            radial_in,
            radial_mid,
            radial_out,
        )

    products = lax.map(
        edge_block,
        (
            neighbours.reshape(block_count, atom_step, -1),
            neighbour_count.reshape(block_count, atom_step),
            work_pos.reshape(3, block_count, atom_step).transpose(1, 0, 2),
            coeffs.reshape(block_count, atom_step, -1),
        ),
    ).reshape(atom_count, 4 * channels)
    efield = field_terms(absolute, wavevectors, weights, total_real, total_imag)
    results = atom_results(
        work_feat,
        products,
        charges,
        efield,
        out_weight,
        skip_weight,
        field_weight,
        read_weight,
        read_vector,
        force_weight,
    )
    res_blocks = results.reshape(4, blocks, block_size).transpose(1, 0, 2)
    arrive_rank = jnp.cumsum(arrived.astype(jnp.int32)) - 1
    return_pick = (
        arrived[None, :] & (arrive_rank[None, :] == jnp.arange(MOVES, dtype=jnp.int32)[:, None])
    ).astype(jnp.float32)
    labels = jnp.stack([block_of_slot, home_of_slot + 1.0], axis=1)
    payload = jnp.concatenate(
        [res_blocks, jnp.broadcast_to(labels[:, :, None], (blocks, 2, block_size))], axis=1
    )
    outgoing = pick_float(return_pick, payload)
    piece = collect_2(outgoing, "yz", 0)
    chosen = (
        (piece[:, 5, 0][None, :] == column_f + 1.0)
        & (piece[:, 4, 0][None, :] == slot_float[:, None])
    ).astype(jnp.float32)
    remote = pick_float(chosen, piece[:, :4])
    home_res = pick_float(stay_pick.T, res_blocks) + remote
    flat_res = home_res.transpose(1, 0, 2).reshape(4, atom_count)
    return (flat_res[:3], flat_res[3])


def solution(mesh):
    in_specs = (
        P(None, ("gx", "yz")),
        P(("gx", "yz")),
        P(("gx", "yz"), None),
        P(("gx", "yz")),
        P(("gx", "yz")),
        P(("gx", "yz")),
        P(("gx", "yz"), None),
        P(("gx", "yz")),
        P(),
        P(),
        P(),
        P(),
        P(),
        P(),
        P(),
        P(),
        P(),
        P(),
        P(),
        P(),
        P(),
    )
    out_specs = (P(None, ("gx", "yz")), P(("gx", "yz")))
    return jax.shard_map(
        on_device, mesh=mesh, in_specs=in_specs, out_specs=out_specs, check_vma=False
    )
```

profile of v0, /device:TPU:1, one launch (start us, length us, event | category | flops | bytes accessed | tf_op | source)
XLA Modules:
  0.0 331.0 jit_solution(17151193566446055851)
XLA Ops:
  12.9 40.2 %all-gather.3.cloned.1.call-done = bf16[16,2,66560]{2,1,0:T(2,128)(2,1)} async-done(((bf16[1,2,66560]{2,1,0:T(2,128)(2,1)}), bf16[16,2,66560]{2,1,0:T(2,128)(2,1)}) %all-gather.3.cloned.1.call-update) | async-done | bytes 4259856 | tf_op jit(solution)/shard_map/all_gather | solution.py:24
  53.2 5.5 %reshape.419 = bf16[32,66560]{1,0:T(8,128)(2,1)} reshape(bf16[16,2,66560]{2,1,0:T(2,128)(2,1)} %all-gather.3.cloned.1.call-done) | data formatting | bytes 8519680
  64.6 3.8 %collective-permute-start.5 = (bf16[1,1,32,512]{3,2,1,0:T(8,128)(2,1)S(1)}, bf16[1,1,32,512]{3,2,1,0:T(8,128)(2,1)S(1)}, u32[]{:S(2)}, u32[]{:S(2)}) collective-permute-start(bf16[1,1,32,512]{3,2,1,0:T(8,128)(2,1)S(1)} %fusion.87), channel_id=1, source_target_pairs={{16,0},{32,16},{48,32},{64,48},{80,64},{96,80},{112,96},{0,112},{1... | collective-permute-start | bytes 98312 | tf_op jit(solution)/shard_map/ppermute | solution.py:41
  71.4 56.7 %while.37 = (s32[]{:T(128)}, f32[8,512,8]{1,2,0:T(8,128)}, f32[8,512,8]{1,2,0:T(8,128)}, f32[3,256]{1,0:T(4,128)S(1)}, s32[8]{0:T(128)S(1)}, /*index=5*/f32[3,40...) while((s32[]{:T(128)}, f32[8,512,8]{1,2,0:T(8,128)}, ...), condition=%wide.region_10.11_spmd, body=%wide.region_9.10_spmd.sunk | while | flops 26476552 | bytes 87259 | solution.py:95
  122.4 2.9 fusion.242
  130.1 5.1 %collective-permute-start.1 = (bf16[1,1,3,32]{3,2,1,0:T(4,128)(2,1)S(1)}, bf16[1,1,3,32]{3,2,1,0:T(4,128)(2,1)S(1)}, u32[]{:S(2)}, u32[]{:S(2)}) collective-permute-start(bf16[1,1,3,32]{3,2,1,0:T(4,128)(2,1)S(1)} %fusion.90), channel_id=1, source_target_pairs={{16,0},{32,16},{48,32},{64,48},{80,64},{96,80},{112,96},{0,112},{1... | collective-permute-start | bytes 584 | tf_op jit(solution)/shard_map/ppermute | solution.py:41
  136.1 3.7 %collective-permute-start.7 = (bf16[1,1,32,512]{3,2,1,0:T(8,128)(2,1)S(1)}, bf16[1,1,32,512]{3,2,1,0:T(8,128)(2,1)S(1)}, u32[]{:S(2)}, u32[]{:S(2)}) collective-permute-start(bf16[1,1,32,512]{3,2,1,0:T(8,128)(2,1)S(1)} %fusion.87), channel_id=1, source_target_pairs={{1,0},{2,1},{3,2},{4,3},{5,4},{6,5},{7,6},{8,7},{9,8},{10,9},{11,1... | collective-permute-start | bytes 98312 | tf_op jit(solution)/shard_map/ppermute | solution.py:41
  141.7 57.3 %while.36 = (s32[]{:T(128)}, bf16[4,64,512]{2,1,0:T(8,128)(2,1)S(1)}, f32[4,64,640]{2,1,0:T(8,128)S(1)}, s32[4,64,64]{2,1,0:T(8,128)S(1)}, f32[3,384]{1,0:T(4,12...) while((s32[]{:T(128)}, ...), condition=%wide.region_7.8_spmd, body=%wide.region_1.7_spmd.sunk | while | flops 2032549888 | bytes 45546492 | solution.py:398
  142.1 3.1 multiply_reduce_fusion.7
  146.3 3.3 %multiply_convert_fusion.13 = bf16[4096,512]{1,0:T(8,128)(2,1)} fusion(bf16[64,512]{1,0:T(8,128)(2,1)S(1)} %get-tuple-element.591, f32[4096]{0:T(1024)S(1)} %get-tuple-element.521, bf16[4096,64]{0,1:T(8,128)(2,1)S(1)} %multiply_convert_fusion.12, bf16[2,64,64]{2,1,0:T(8,128)(2,1)S(1)} %copy-done.16), kind=kOutput, calls=%fused_computation.clone.1 | convolution fusion | flops 307494912 | bytes 4816896 | tf_op jit(solution)/shard_map/while/body/eval_jaxpr/dot_general | solution.py:175
  152.5 3.4 %bitcast_reduce_fusion.5 = (f32[64,128]{1,0:T(8,128)S(1)}, f32[64,128]{1,0:T(8,128)S(1)}, f32[64,128]{1,0:T(8,128)S(1)}, f32[64,128]{1,0:T(8,128)S(1)}) fusion(f32[4096,512]{1,0:T(8,128)S(1)} %fusion.230, f32[4096]{0:T(1024)S(1)} %mul.1019, bf16[4096,512]{1,0:T(8,128)(2,1)S(1)} %copy-done.1, f32[4096]{0:T(1024)S(1)} %mul.1020, f32[4096]{0:T(1024)S(1)} %mul.1021), kind=kLoop, calls=%fused_computation.15.clone.1 | loop fusion | flops 13598720 | bytes 12763136 | tf_op jit(solution)/shard_map/while/body/eval_jaxpr/reduce_sum | solution.py:187
  156.4 3.1 multiply_reduce_fusion.7
  160.6 3.3 %multiply_convert_fusion.13 = bf16[4096,512]{1,0:T(8,128)(2,1)} fusion(bf16[64,512]{1,0:T(8,128)(2,1)S(1)} %get-tuple-element.591, f32[4096]{0:T(1024)S(1)} %get-tuple-element.521, bf16[4096,64]{0,1:T(8,128)(2,1)S(1)} %multiply_convert_fusion.12, bf16[2,64,64]{2,1,0:T(8,128)(2,1)S(1)} %copy-done.16), kind=kOutput, calls=%fused_computation.clone.1 | convolution fusion | flops 307494912 | bytes 4816896 | tf_op jit(solution)/shard_map/while/body/eval_jaxpr/dot_general | solution.py:175
  166.9 3.4 %bitcast_reduce_fusion.5 = (f32[64,128]{1,0:T(8,128)S(1)}, f32[64,128]{1,0:T(8,128)S(1)}, f32[64,128]{1,0:T(8,128)S(1)}, f32[64,128]{1,0:T(8,128)S(1)}) fusion(f32[4096,512]{1,0:T(8,128)S(1)} %fusion.230, f32[4096]{0:T(1024)S(1)} %mul.1019, bf16[4096,512]{1,0:T(8,128)(2,1)S(1)} %copy-done.1, f32[4096]{0:T(1024)S(1)} %mul.1020, f32[4096]{0:T(1024)S(1)} %mul.1021), kind=kLoop, calls=%fused_computation.15.clone.1 | loop fusion | flops 13598720 | bytes 12763136 | tf_op jit(solution)/shard_map/while/body/eval_jaxpr/reduce_sum | solution.py:187
  170.7 3.1 multiply_reduce_fusion.7
  175.0 3.3 %multiply_convert_fusion.13 = bf16[4096,512]{1,0:T(8,128)(2,1)} fusion(bf16[64,512]{1,0:T(8,128)(2,1)S(1)} %get-tuple-element.591, f32[4096]{0:T(1024)S(1)} %get-tuple-element.521, bf16[4096,64]{0,1:T(8,128)(2,1)S(1)} %multiply_convert_fusion.12, bf16[2,64,64]{2,1,0:T(8,128)(2,1)S(1)} %copy-done.16), kind=kOutput, calls=%fused_computation.clone.1 | convolution fusion | flops 307494912 | bytes 4816896 | tf_op jit(solution)/shard_map/while/body/eval_jaxpr/dot_general | solution.py:175
  181.2 3.4 %bitcast_reduce_fusion.5 = (f32[64,128]{1,0:T(8,128)S(1)}, f32[64,128]{1,0:T(8,128)S(1)}, f32[64,128]{1,0:T(8,128)S(1)}, f32[64,128]{1,0:T(8,128)S(1)}) fusion(f32[4096,512]{1,0:T(8,128)S(1)} %fusion.230, f32[4096]{0:T(1024)S(1)} %mul.1019, bf16[4096,512]{1,0:T(8,128)(2,1)S(1)} %copy-done.1, f32[4096]{0:T(1024)S(1)} %mul.1020, f32[4096]{0:T(1024)S(1)} %mul.1021), kind=kLoop, calls=%fused_computation.15.clone.1 | loop fusion | flops 13598720 | bytes 12763136 | tf_op jit(solution)/shard_map/while/body/eval_jaxpr/reduce_sum | solution.py:187
  185.0 3.1 multiply_reduce_fusion.7
  189.3 3.3 %multiply_convert_fusion.13 = bf16[4096,512]{1,0:T(8,128)(2,1)} fusion(bf16[64,512]{1,0:T(8,128)(2,1)S(1)} %get-tuple-element.591, f32[4096]{0:T(1024)S(1)} %get-tuple-element.521, bf16[4096,64]{0,1:T(8,128)(2,1)S(1)} %multiply_convert_fusion.12, bf16[2,64,64]{2,1,0:T(8,128)(2,1)S(1)} %copy-done.16), kind=kOutput, calls=%fused_computation.clone.1 | convolution fusion | flops 307494912 | bytes 4816896 | tf_op jit(solution)/shard_map/while/body/eval_jaxpr/dot_general | solution.py:175
  195.5 3.4 %bitcast_reduce_fusion.5 = (f32[64,128]{1,0:T(8,128)S(1)}, f32[64,128]{1,0:T(8,128)S(1)}, f32[64,128]{1,0:T(8,128)S(1)}, f32[64,128]{1,0:T(8,128)S(1)}) fusion(f32[4096,512]{1,0:T(8,128)S(1)} %fusion.230, f32[4096]{0:T(1024)S(1)} %mul.1019, bf16[4096,512]{1,0:T(8,128)(2,1)S(1)} %copy-done.1, f32[4096]{0:T(1024)S(1)} %mul.1020, f32[4096]{0:T(1024)S(1)} %mul.1021), kind=kLoop, calls=%fused_computation.15.clone.1 | loop fusion | flops 13598720 | bytes 12763136 | tf_op jit(solution)/shard_map/while/body/eval_jaxpr/reduce_sum | solution.py:187
  200.4 69.1 %all-reduce.3.cloned.1.call-done = (f32[4096,8]{0,1:T(8,128)}, f32[4096,8]{0,1:T(8,128)}) async-done(((f32[4096,8]{0,1:T(8,128)}, f32[4096,8]{0,1:T(8,128)}), (f32[4096,8]{0,1:T(8,128)}, f32[4096,8]{0,1:T(8,128)})) %all-reduce.3.cloned.1.call-update) | async-done | bytes 262160 | tf_op jit(solution)/shard_map/psum | solution.py:377
  270.7 39.2 %while.38 = (s32[]{:T(128)}, f32[256,32]{0,1:T(8,128)S(1)}, f32[3,256]{1,0:T(4,128)S(1)}, f32[3,4096]{1,0:T(4,128)S(1)}, f32[4096,32]{0,1:T(8,128)S(1)}, /*index...) while((s32[]{:T(128)}, f32[256,32]{0,1:T(8,128)S(1)}, ...), condition=%wide.region_14.15_spmd.clone, body=%wide.region_13.14_spmd.clone.sunk | while | flops 101998600 | bytes 299225 | solution.py:123
  311.6 5.0 %all-to-all-start = ((f32[16,2,6,128]{3,1,2,0:T(2,128)}), f32[16,2,6,128]{3,1,2,0:T(2,128)S(1)}, u32[]{:S(2)}, u32[]{:S(2)}) async-start(f32[16,2,6,128]{3,1,2,0:T(2,128)} %broadcast_in_dim.28), calls=%async_computation | async-start | bytes 196608 | tf_op jit(solution)/shard_map/all_to_all | solution.py:60
  316.8 5.6 %all-to-all-done = f32[16,2,6,128]{3,1,2,0:T(2,128)S(1)} async-done(((f32[16,2,6,128]{3,1,2,0:T(2,128)}), f32[16,2,6,128]{3,1,2,0:T(2,128)S(1)}, u32[]{:S(2)}, u32[]{:S(2)}) %all-to-all-start) | async-done | bytes 98336 | tf_op jit(solution)/shard_map/all_to_all | solution.py:60
  (356 shorter events, 129.6 us)
Async XLA Ops:
  7.2 5.4 %copy-start.14 = (s32[2]{0:T(128)S(1)}, s32[2]{0:T(128)}, u32[]{:S(2)}) copy-start(s32[2]{0:T(128)} %param.32) | copy-start | bytes 28
  7.2 5.2 %copy-start.11 = (s32[256]{0:T(256)S(1)}, s32[256]{0:T(256)}, u32[]{:S(2)}) copy-start(s32[256]{0:T(256)} %param.35) | copy-start | bytes 3076
  7.2 45.9 %all-gather.3.cloned.1.call-start = ((), (), s32[]{:S(2)}) async-start(), calls=%async_computation.1 | async-start | bytes 4526080 | tf_op jit(solution)/shard_map/all_gather | solution.py:24
  12.0 257.4 %all-reduce.3.cloned.1.call-start = ((), (), s32[]{:S(2)}) async-start(), calls=%async_computation.2 | async-start | bytes 524288 | tf_op jit(solution)/shard_map/psum | solution.py:377
  62.4 8.9 %copy-start.17 = (bf16[128,8]{0,1:T(8,128)(2,1)S(1)}, bf16[128,8]{0,1:T(8,128)(2,1)}, u32[]{:S(2)}) copy-start(bf16[128,8]{0,1:T(8,128)(2,1)} %param.44) | copy-start | bytes 6148
  63.3 76.8 %collective-permute-start.4 = (bf16[1,1,32,512]{3,2,1,0:T(8,128)(2,1)S(1)}, bf16[1,1,32,512]{3,2,1,0:T(8,128)(2,1)S(1)}, u32[]{:S(2)}, u32[]{:S(2)}) collective-permute-start(bf16[1,1,32,512]{3,2,1,0:T(8,128)(2,1)S(1)} %fusion.87), channel_id=1, source_target_pairs={{0,16},{16,32},{32,48},{48,64},{64,80},{80,96},{96,112},{112,0},{1... | collective-permute-start | bytes 98312 | tf_op jit(solution)/shard_map/ppermute | solution.py:40
  64.6 75.5 %collective-permute-start.5 = (bf16[1,1,32,512]{3,2,1,0:T(8,128)(2,1)S(1)}, bf16[1,1,32,512]{3,2,1,0:T(8,128)(2,1)S(1)}, u32[]{:S(2)}, u32[]{:S(2)}) collective-permute-start(bf16[1,1,32,512]{3,2,1,0:T(8,128)(2,1)S(1)} %fusion.87), channel_id=1, source_target_pairs={{16,0},{32,16},{48,32},{64,48},{80,64},{96,80},{112,96},{0,112},{1... | collective-permute-start | bytes 98312 | tf_op jit(solution)/shard_map/ppermute | solution.py:41
  68.4 71.7 %collective-permute-start.6 = (bf16[1,1,32,512]{3,2,1,0:T(8,128)(2,1)S(1)}, bf16[1,1,32,512]{3,2,1,0:T(8,128)(2,1)S(1)}, u32[]{:S(2)}, u32[]{:S(2)}) collective-permute-start(bf16[1,1,32,512]{3,2,1,0:T(8,128)(2,1)S(1)} %fusion.87), channel_id=1, source_target_pairs={{0,1},{1,2},{2,3},{3,4},{4,5},{5,6},{6,7},{7,8},{8,9},{9,10},{10,1... | collective-permute-start | bytes 98312 | tf_op jit(solution)/shard_map/ppermute | solution.py:40
  70.4 59.6 %collective-permute-start.2 = (bf16[1,1,3,32]{3,2,1,0:T(4,128)(2,1)S(1)}, bf16[1,1,3,32]{3,2,1,0:T(4,128)(2,1)S(1)}, u32[]{:S(2)}, u32[]{:S(2)}) collective-permute-start(bf16[1,1,3,32]{3,2,1,0:T(4,128)(2,1)S(1)} %fusion.90), channel_id=1, source_target_pairs={{0,1},{1,2},{2,3},{3,4},{4,5},{5,6},{6,7},{7,8},{8,9},{9,10},{10,1... | collective-permute-start | bytes 584 | tf_op jit(solution)/shard_map/ppermute | solution.py:40
  70.4 59.7 %collective-permute-start.3 = (bf16[1,1,3,32]{3,2,1,0:T(4,128)(2,1)S(1)}, bf16[1,1,3,32]{3,2,1,0:T(4,128)(2,1)S(1)}, u32[]{:S(2)}, u32[]{:S(2)}) collective-permute-start(bf16[1,1,3,32]{3,2,1,0:T(4,128)(2,1)S(1)} %fusion.90), channel_id=1, source_target_pairs={{1,0},{2,1},{3,2},{4,3},{5,4},{6,5},{7,6},{8,7},{9,8},{10,9},{11,1... | collective-permute-start | bytes 584 | tf_op jit(solution)/shard_map/ppermute | solution.py:41
  71.4 56.8 %copy-start.3 = (bf16[2,128,128]{2,1,0:T(8,128)(2,1)S(1)}, bf16[2,128,128]{2,1,0:T(8,128)(2,1)}, u32[]{:S(2)}) copy-start(bf16[2,128,128]{2,1,0:T(8,128)(2,1)} %param.43) | copy-start | bytes 196612
  71.4 57.9 %copy-start.7 = (f32[6,640]{1,0:T(8,128)S(1)}, f32[6,640]{1,0:T(8,128)}, u32[]{:S(2)}) copy-start(f32[6,640]{1,0:T(8,128)} %param.41) | copy-start | bytes 46084
  128.3 12.7 %copy-start.4 = (bf16[2,128,128]{2,1,0:T(8,128)(2,1)S(1)}, bf16[2,128,128]{2,1,0:T(8,128)(2,1)}, u32[]{:S(2)}) copy-start(bf16[2,128,128]{2,1,0:T(8,128)(2,1)} %param.40) | copy-start | bytes 196612
  130.0 11.7 %copy-start.15 = (bf16[64,512]{1,0:T(8,128)(2,1)S(1)}, bf16[64,512]{1,0:T(8,128)(2,1)}, u32[]{:S(2)}) copy-start(bf16[64,512]{1,0:T(8,128)(2,1)} %param.39) | copy-start | bytes 196612
  130.0 6.1 %collective-permute-start = (bf16[1,1,3,32]{3,2,1,0:T(4,128)(2,1)S(1)}, bf16[1,1,3,32]{3,2,1,0:T(4,128)(2,1)S(1)}, u32[]{:S(2)}, u32[]{:S(2)}) collective-permute-start(bf16[1,1,3,32]{3,2,1,0:T(4,128)(2,1)S(1)} %fusion.90), channel_id=1, source_target_pairs={{0,16},{16,32},{32,48},{48,64},{64,80},{80,96},{96,112},{112,0},{1... | collective-permute-start | bytes 584 | tf_op jit(solution)/shard_map/ppermute | solution.py:40
  130.1 9.7 %collective-permute-start.1 = (bf16[1,1,3,32]{3,2,1,0:T(4,128)(2,1)S(1)}, bf16[1,1,3,32]{3,2,1,0:T(4,128)(2,1)S(1)}, u32[]{:S(2)}, u32[]{:S(2)}) collective-permute-start(bf16[1,1,3,32]{3,2,1,0:T(4,128)(2,1)S(1)} %fusion.90), channel_id=1, source_target_pairs={{16,0},{32,16},{48,32},{64,48},{80,64},{96,80},{112,96},{0,112},{1... | collective-permute-start | bytes 584 | tf_op jit(solution)/shard_map/ppermute | solution.py:41
  136.1 4.6 %collective-permute-start.7 = (bf16[1,1,32,512]{3,2,1,0:T(8,128)(2,1)S(1)}, bf16[1,1,32,512]{3,2,1,0:T(8,128)(2,1)S(1)}, u32[]{:S(2)}, u32[]{:S(2)}) collective-permute-start(bf16[1,1,32,512]{3,2,1,0:T(8,128)(2,1)S(1)} %fusion.87), channel_id=1, source_target_pairs={{1,0},{2,1},{3,2},{4,3},{5,4},{6,5},{7,6},{8,7},{9,8},{10,9},{11,1... | collective-permute-start | bytes 98312 | tf_op jit(solution)/shard_map/ppermute | solution.py:41
  141.7 57.5 %copy-start.5 = (bf16[2,128,128]{2,1,0:T(8,128)(2,1)S(1)}, bf16[2,128,128]{2,1,0:T(8,128)(2,1)}, u32[]{:S(2)}) copy-start(bf16[2,128,128]{2,1,0:T(8,128)(2,1)} %param.42) | copy-start | bytes 196612
  270.6 39.3 %copy-start.9 = (f32[8,128]{1,0:T(8,128)S(1)}, f32[8,128]{1,0:T(8,128)}, u32[]{:S(2)}) copy-start(f32[8,128]{1,0:T(8,128)} %param.45) | copy-start | bytes 12292
  270.6 39.8 %copy-start.10 = (bf16[128,16]{0,1:T(8,128)(2,1)S(1)}, bf16[128,16]{0,1:T(8,128)(2,1)}, u32[]{:S(2)}) copy-start(bf16[128,16]{0,1:T(8,128)(2,1)} %param.46) | copy-start | bytes 12292
  270.6 39.9 %copy-start.19 = (f32[16]{0:T(128)S(1)}, f32[16]{0:T(128)}, u32[]{:S(2)}) copy-start(f32[16]{0:T(128)} %param.47) | copy-start | bytes 196
  270.7 40.1 %copy-start.22 = (s32[2]{0:T(128)S(1)}, s32[2]{0:T(128)}, u32[]{:S(2)}) copy-start(s32[2]{0:T(128)} %add_bitcast_fusion.4) | copy-start | bytes 28
  270.7 46.0 %copy-start.21 = (pred[2]{0:T(512)(128)(4,1)S(1)}, pred[2]{0:T(512)(128)(4,1)}, u32[]{:S(2)}) copy-start(pred[2]{0:T(512)(128)(4,1)} %copy-done.20) | copy-start | bytes 10
  311.6 10.9 %all-to-all-start = ((f32[16,2,6,128]{3,1,2,0:T(2,128)}), f32[16,2,6,128]{3,1,2,0:T(2,128)S(1)}, u32[]{:S(2)}, u32[]{:S(2)}) async-start(f32[16,2,6,128]{3,1,2,0:T(2,128)} %broadcast_in_dim.28), calls=%async_computation | async-start | bytes 196608 | tf_op jit(solution)/shard_map/all_to_all | solution.py:60
  (20 other events, 61.9 us)
Sparse Core Ops, SparseCore 0:
  12.1 40.9 all-gather.2
  129.5 139.9 all-reduce.2
where the time goes:
time: 332 us; the launch traced here: 331 us
  matrix products  129 us (39%)
  waiting for transfers between devices  117 us (35%)
  local copies, waits for them, and re-layouts  21.9 us (7%)
  starting transfers between devices  21.2 us (6%)
  other arithmetic  21.1 us (6%)
  between operations  14.8 us (4%)
  loops' own time  6.18 us (2%)
    psum x1, waiting for transfers between devices, on_device(): total_real, total_imag = lax.psum((part_real, part_imag), ('gx', 'yz'))  69.1 us
    all_gather x1, waiting for transfers between devices, side_by_side(): out, at, outs = (lax.all_gather(both, axis, axis=dim, tiled=True), 0, [])  40.2 us
    dot_general x8, matrix products, one_block(): jnp.einsum('ak,aq->kq', jnp.sin(phases), charges, precision=highest)  23.1 us
    dot_general x8, matrix products, one_block(): jnp.einsum('ak,aq->kq', jnp.cos(phases), charges, precision=highest)  22.9 us
    dot_general x8, matrix products, accumulate(): return running + jnp.dot(jnp.sin(phases), sin_right, precision=highest)  19.2 us
    dot_general x8, matrix products, accumulate(): running = running + jnp.dot(jnp.cos(phases), cos_right, precision=highest)  19.1 us
    reduce_sum x4, other arithmetic, neighbour_sum(): jnp.sum(values.reshape(atom_count, slot_count, channels), axis=1)  13.6 us
    dot_general x4, matrix products, edge_products(): jnp.dot(hidden, radial_out, preferred_element_type=jnp.float32)  13.4 us
  transfers between devices with their start and end apart: 11, of which 5 were waited for; matrix products, arithmetic and copies ran while one was open for 34% of the time, Pallas kernels for 0%

commit v1 on v0

v1 whole, which is shorter than its diff:
```python
import math

import jax
import jax.numpy as jnp
from jax import lax
from jax.experimental import pallas as pl
from jax.experimental.pallas import tpu as pltpu
from jax.sharding import PartitionSpec as P

f32, bf16, i32 = jnp.float32, jnp.bfloat16, jnp.int32
highest = lax.Precision.HIGHEST
two_pi = 2.0 * math.pi
cutoff_radius = 3.5
ewald_width = 0.1
ewald_scale = 0.01

NX, NY, NZ = 16, 32, 2
SLABS = 2 * NZ + 2
SLOT_GROUP = 4


def dot(a, b, ca, cb, precision=None):
    return lax.dot_general(
        a, b, (((ca,), (cb,)), ((), ())), precision=precision, preferred_element_type=f32
    )


def silu(v):
    half = 0.5 * v
    return half + half * jnp.tanh(half)


def iota(shape, dim):
    return lax.broadcasted_iota(i32, shape, dim)


def turns(t):
    angle = two_pi * (t - jnp.floor(t + 0.5))
    return jnp.cos(angle), jnp.sin(angle)


def params(vmem=32):
    return pltpu.CompilerParams(vmem_limit_bytes=vmem << 20)


def cost(flops, transcendentals, moved):
    return pl.CostEstimate(flops=flops, transcendentals=transcendentals, bytes_accessed=moved)


SMEM = pl.BlockSpec(memory_space=pltpu.SMEM)


def up_kernel(feat, up, charge_weight, out, charges):
    charges[...] = dot(charge_weight[...], feat[:, 0:128], 1, 1)
    for b in range(2):
        for c in range(4):
            rows = feat[b * 128 : (b + 1) * 128, c * 128 : (c + 1) * 128]
            mapped = dot(up[min(c, 1)], rows, 0, 1).astype(bf16)
            out[b, c * 128 : (c + 1) * 128, :] = mapped


def moment_kernel(
    dest, slot, place, charges_in, pos, species, halo, out, basis, waves, stage
):
    gx = place[0].astype(f32)
    charges = charges_in[...]
    lane = iota((1, 256), 1)
    second = lane >= 128
    xyz = pos[...].astype(f32)
    along_x = xyz[0:1] + gx
    along_y = xyz[1:2] + jnp.where(second, dest[1], dest[0]).astype(f32)
    along_z = xyz[2:3]
    cos_x, sin_x = turns((iota((NX, 256), 0) + 1).astype(f32) * along_x * (1.0 / 8.0))
    cos_y, sin_y = turns((iota((NY, 256), 0) + 1).astype(f32) * along_y * (1.0 / 16.0))
    cos_z, sin_z = turns(iota((8, 256), 0).astype(f32) * along_z)
    pairs = [
        (cos_z[abs(z) : abs(z) + 1], sin_z[abs(z) : abs(z) + 1] * (1.0 if z >= 0 else -1.0))
        for z in range(-NZ, NZ + 1)
    ]
    for i, (c, s) in enumerate(pairs):
        at = i * 128
        basis[at : at + 32, 0:256] = cos_y * c
        basis[at + 32 : at + 64, 0:256] = sin_y * c
        basis[at + 64 : at + 96, 0:256] = cos_y * s
        basis[at + 96 : at + 128, 0:256] = sin_y * s
        basis[at : at + 32, 256:512] = -(cos_y * s)
        basis[at + 32 : at + 64, 256:512] = -(sin_y * s)
        basis[at + 64 : at + 96, 256:512] = cos_y * c
        basis[at + 96 : at + 128, 256:512] = sin_y * c
    at = 128 * (SLABS - 1)
    basis[at : at + 128, :] = jnp.zeros((128, 512), f32)
    for i, (c, s) in enumerate(pairs):
        basis[at + i : at + i + 1, 0:256] = c
        basis[at + i : at + i + 1, 256:512] = -s
        basis[at + 64 + i : at + 65 + i, 0:256] = s
        basis[at + 64 + i : at + 65 + i, 256:512] = c
    waves[0:8] = charges
    waves[8:24] = cos_x
    waves[24:40] = sin_x
    left_cos = (cos_x[:, None, :] * charges[None]).reshape(128, 256)
    left_sin = (sin_x[:, None, :] * charges[None]).reshape(128, 256)
    moments = dot(left_cos, basis[:, 0:256], 1, 1, highest) + dot(
        left_sin, basis[:, 256:512], 1, 1, highest
    )
    for i in range(SLABS):
        stage[:, i, :] = moments[:, i * 128 : (i + 1) * 128]
    kinds = species[...].astype(f32)
    for b in range(2):
        cut = slice(b * 128, (b + 1) * 128)
        for m in range(3):
            stage[:, 6 + 3 * b + m, :] = jnp.broadcast_to(xyz[m : m + 1, cut], (128, 128))
        stage[:, 12 + b, :] = jnp.broadcast_to(kinds[:, cut], (128, 128))
    listed = jnp.concatenate([halo[...], jnp.zeros((1, 96), i32)], axis=1)
    at = iota((1, 128), 1)
    for b in range(2):
        listed = jnp.where(at == 32 + b, dest[b], listed)
        listed = jnp.where(at == 34 + b, slot[b], listed)
    stage[:, 14, :] = jnp.broadcast_to(listed.astype(f32), (128, 128))
    stage[:, 15, :] = jnp.zeros((128, 128), f32)
    out[...] = stage[...].astype(bf16)


def weight_kernel(place, sent, wave_index, out):
    total = jnp.sum(sent[...].astype(f32), axis=0)[0:8]
    own_x = (place[0] * 16 + place[1]) // 8 + 1
    kx, ky, kz = wave_index[0:1, :], wave_index[1:2, :], wave_index[2:3, :]
    count = kx.shape[1]
    ours = kx == own_x
    rank = iota((8, count), 0)
    z_rows = jnp.where(ours & (kz == rank - NZ), 1.0, 0.0).astype(bf16)
    flat_rows = jnp.where(ours & (ky == 0) & (rank == SLABS - 1), 1.0, 0.0).astype(bf16)
    z_any = jnp.where(kz == rank - NZ, 1.0, 0.0).astype(bf16)
    y_match = jnp.where(jnp.abs(ky) == iota((NY, count), 0) + 1, 1.0, 0.0)
    y_sign = jnp.where(ky < 0, -y_match, y_match)
    even = dot(z_rows, y_match.astype(bf16), 1, 1)
    odd = dot(z_rows, y_sign.astype(bf16), 1, 1)
    flat = dot(flat_rows, z_any, 1, 1)
    gap = jnp.zeros((8, 56), f32)
    even = jnp.concatenate([even] * 4, axis=1)
    odd = jnp.concatenate([odd] * 4, axis=1)
    flat = jnp.concatenate([flat, gap] * 2, axis=1)
    row, lane = iota((8, 128), 0), iota((8, 128), 1)
    in_flat = row == SLABS - 1
    x_wave = own_x.astype(f32) * (two_pi / 8.0)
    y_wave = jnp.where(in_flat, 0, lane % 32 + 1).astype(f32) * (two_pi / 16.0)
    z_wave = (jnp.where(in_flat, lane % 64, row) - NZ).astype(f32) * two_pi
    squared = x_wave * x_wave + y_wave * y_wave + z_wave * z_wave
    prefactor = 8.0 * math.pi * ewald_scale / 128.0
    weight = prefactor * jnp.exp(-0.5 * ewald_width * ewald_width * squared) / squared
    direct = weight * jnp.where(in_flat, flat, even)
    crossed = weight * jnp.where(in_flat, 0.0, odd)
    total = jnp.where(row < SLABS, total, 0.0)
    far = pltpu.roll(total, 64, 1)
    group = lane // 32
    swapped = jnp.where(group % 2 == 0, pltpu.roll(far, 96, 1), pltpu.roll(far, 32, 1))
    swapped = jnp.where((group == 0) | (group == 3), -swapped, swapped)
    coefficient = total * direct + swapped * crossed
    out[...] = jnp.broadcast_to(coefficient[None], out.shape)


def field_kernel(
    coeffs,
    basis,
    waves,
    feat,
    skip_weight,
    field_weight,
    read_weight,
    force_weight,
    out,
    stacked,
):
    lane = iota((128, 128), 1)
    group_even = (lane // 32) % 2 == 0
    low_half = lane < 64
    y_wave = (lane % 32 + 1).astype(f32) * (two_pi / 16.0)
    for i in range(SLABS):
        cut = slice(i * 128, (i + 1) * 128)
        c = coeffs[:, i, :]
        stacked[0:128, cut] = c
        half = pltpu.roll(c, 64, 1)
        if i < SLABS - 1:
            moved = jnp.where(group_even, pltpu.roll(c, 96, 1), -pltpu.roll(c, 32, 1))
            stacked[128:256, cut] = y_wave * moved
            z_wave = two_pi * (i - NZ)
        else:
            stacked[128:256, cut] = jnp.zeros((128, 128), f32)
            z_wave = (lane % 64 - NZ).astype(f32) * two_pi
        stacked[256:384, cut] = z_wave * jnp.where(low_half, half, -half)
    grid = dot(stacked[...], basis[...], 1, 0, highest)
    charges = waves[0:8]
    cos_x = jnp.broadcast_to(waves[8:24][:, None, :], (NX, 8, 256)).reshape(128, 256)
    sin_x = jnp.broadcast_to(waves[24:40][:, None, :], (NX, 8, 256)).reshape(128, 256)
    x_wave = (iota((128, 256), 0) // 8 + 1).astype(f32) * (two_pi / 8.0)

    def channels(v):
        return jnp.sum(v.reshape(NX, 8, 256), axis=0)

    def even_part(at):
        return channels(cos_x * grid[at : at + 128, 0:256] + sin_x * grid[at : at + 128, 256:512])

    potential = even_part(0)
    field = [
        channels(x_wave * (sin_x * grid[0:128, 0:256] - cos_x * grid[0:128, 256:512])),
        -even_part(128),
        -even_part(256),
    ]
    scalars = dot(field_weight[...], potential, 0, 0, highest) + dot(
        skip_weight[0], feat[:, 0:128], 0, 1
    )
    out[0:16] = dot(read_weight[...].astype(f32), scalars, 1, 0, highest)
    for m in range(3):
        vector = dot(skip_weight[1], feat[:, (m + 1) * 128 : (m + 2) * 128], 0, 1)
        out[16 + m : 17 + m] = dot(force_weight[...], vector, 1, 0, highest) + jnp.sum(
            charges * field[m], axis=0, keepdims=True
        )
    out[19:20] = 0.5 * jnp.sum(charges * potential, axis=0, keepdims=True)
    out[20:24] = jnp.zeros((4, 256), f32)


def radial_kernel(
    place,
    sent,
    neighbours,
    live,
    radial_in,
    radial_mid,
    hidden_out,
    offset_out,
    kinds_out,
    home_out,
    stage,
    dist_stage,
    scale_stage,
):
    stage[...] = sent[...].astype(f32)
    gx, yz = place[0], place[1]
    targets = [
        (gx, yz),
        ((gx + 7) % 8, yz),
        ((gx + 1) % 8, yz),
        (gx, (yz + 15) % 16),
        (gx, (yz + 1) % 16),
    ]
    plan = jnp.transpose(stage[:, 14, :])
    row = iota((16, 128), 0)
    device = iota((16, 128), 1)
    want_x, want_y = jnp.full((16, 128), -1, i32), jnp.full((16, 128), -1, i32)
    for t, (tx, ty) in enumerate(targets):
        want_x = jnp.where(row // 2 == t, tx, want_x)
        want_y = jnp.where(row // 2 == t, ty, want_y)
    here = (device // 16 == want_x).astype(f32)
    want_y, want_slot = want_y.astype(f32), (row % 2).astype(f32)
    picks = []
    for b in range(2):
        match = (plan[32 + b : 33 + b] == want_y) & (plan[34 + b : 35 + b] == want_slot)
        picks.append(jnp.where(match, here, 0.0))

    def from_home(first, step):
        return dot(picks[0], stage[:, first, :], 1, 0, highest) + dot(
            picks[1], stage[:, first + step, :], 1, 0, highest
        )

    xyz = [from_home(6 + m, 3) for m in range(3)]
    kinds = from_home(12, 1)
    kinds_out[...] = jnp.concatenate([kinds[0:1], kinds[1:2]], axis=1)
    both = picks[0] + picks[1]
    for s in range(2):
        column = 2.0 * both * (device % 16).astype(f32) + picks[1]
        home_out[s] = jnp.sum(jnp.where(row == s, column, 0.0)).astype(i32)
    lane = iota((1, 128), 1)
    atom = iota((128, 128), 0)
    ghosts = jnp.zeros((8, 128), f32)
    for t, (tx, ty) in enumerate(targets[1:]):
        listed = stage[tx * 16 + ty, 14:15, :].astype(i32)
        if t:
            listed = pltpu.roll(listed, 32 * t, 1)
        listed = jnp.where(lane // 32 == t, listed, -1)
        for s in range(2):
            at = 2 * (t + 1) + s
            rows = jnp.concatenate(
                [x[at : at + 1] for x in xyz] + [jnp.zeros((5, 128), f32)], axis=0
            )
            chosen = jnp.where(atom + 128 * s == listed, 1.0, 0.0)
            ghosts = ghosts + dot(rows, chosen, 1, 0, highest)
    part = lane // 32
    shifts = [
        jnp.where(part == 0, -1.0, jnp.where(part == 1, 1.0, 0.0)),
        jnp.where(part == 2, -1.0, jnp.where(part == 3, 1.0, 0.0)),
        jnp.zeros((1, 128), f32),
    ]
    tables = [
        [
            jnp.broadcast_to(v, (8, 128))
            for v in (xyz[m][0:1], xyz[m][1:2], ghosts[m : m + 1] + shifts[m])
        ]
        for m in range(3)
    ]
    for n in range(0, 64, 8):
        for half in range(2):
            cut = slice(half * 128, (half + 1) * 128)
            index = neighbours[n : n + 8, cut]
            within, block = index & 127, index >> 7
            squared = jnp.zeros((8, 128), f32)
            for m in range(3):
                found = [
                    jnp.take_along_axis(table, within, axis=1, mode="promise_in_bounds")
                    for table in tables[m]
                ]
                picked = jnp.where(block == 0, found[0], jnp.where(block == 1, found[1], found[2]))
                offset = picked - tables[m][half]
                offset_out[m, n : n + 8, cut] = offset
                squared = squared + offset * offset
            dist = jnp.sqrt(squared)
            dist_stage[n : n + 8, cut] = dist
            u = dist * (1.0 / cutoff_radius)
            u6 = (u * u) * (u * u) * (u * u)
            envelope = 1.0 + u6 * (-28.0 + u * (48.0 - 21.0 * u))
            alive = iota((8, 128), 0) + n < live[:, cut]
            scale_stage[n : n + 8, cut] = jnp.where(alive, 0.125 * envelope, 0.0)
    first = jnp.transpose(radial_in[...].astype(f32)).astype(bf16)
    mid = [jnp.transpose(radial_mid[i].astype(f32)).astype(bf16) for i in range(2)]
    centre = iota((8, 256), 0).astype(f32) * (cutoff_radius / 7.0)

    def body(group, carry):
        start = group * SLOT_GROUP
        rows = []
        for j in range(SLOT_GROUP):
            away = dist_stage[pl.ds(start + j, 1), :] - centre
            rows.append(jnp.exp(-4.0 * (away * away)))
        hidden = silu(dot(first, jnp.concatenate(rows, axis=1).astype(bf16), 1, 0)).astype(bf16)
        hidden = silu(dot(mid[0], hidden, 1, 0)).astype(bf16)
        hidden = silu(dot(mid[1], hidden, 1, 0))
        for j in range(SLOT_GROUP):
            scaled = hidden[:, j * 256 : (j + 1) * 256] * scale_stage[pl.ds(start + j, 1), :]
            hidden_out[start + j] = scaled.astype(bf16)
        return carry

    lax.fori_loop(0, 64 // SLOT_GROUP, body, 0)


def halo_kernel(home, first, second, halo, out):
    atom = iota((128, 32), 0)
    chosen = [jnp.where(atom + 128 * s == halo[...], 1.0, 0.0).astype(bf16) for s in range(2)]
    out[...] = (dot(chosen[0], first[0], 0, 1) + dot(chosen[1], second[0], 0, 1)).astype(bf16)


def message_kernel(
    home,
    first,
    second,
    ghost0,
    ghost1,
    ghost2,
    ghost3,
    neighbours,
    offsets,
    hidden,
    kinds,
    radial_out,
    prod_weight,
    out_weight,
    read_weight,
    force_weight,
    out,
    table,
    total,
):
    table[:, 0:128] = first[0]
    table[:, 128:256] = second[0]
    for t, ghost in enumerate((ghost0, ghost1, ghost2, ghost3)):
        table[:, 256 + 32 * t : 288 + 32 * t] = jnp.transpose(ghost[...].astype(f32)).astype(bf16)
    spread = jnp.transpose(radial_out[...].astype(f32)).astype(bf16)
    total[...] = jnp.zeros((512, 256), f32)
    place = iota((384, 256), 0)

    def body(n, carry):
        chosen = jnp.where(place == neighbours[pl.ds(n, 1), :], 1.0, 0.0).astype(bf16)
        radial = dot(spread, hidden[n], 1, 0)
        up = dot(table[...], chosen, 1, 0)
        u0, u1 = up[0:128], [up[128 * m : 128 * (m + 1)] for m in (1, 2, 3)]
        r = [offsets[m, pl.ds(n, 1), :] for m in range(3)]
        along = u1[0] * r[0] + u1[1] * r[1] + u1[2] * r[2]
        total[0:128] += radial[0:128] * u0 + radial[128:256] * along
        scalar = radial[256:384] * u0
        for m in range(3):
            total[128 * (m + 1) : 128 * (m + 2)] += scalar * r[m] + radial[384:512] * u1[m]
        return carry

    lax.fori_loop(0, 64, body, 0, unroll=2)
    kind = jnp.where(iota((6, 256), 0).astype(f32) == kinds[...], 1.0, 0.0)
    paths = dot(prod_weight[...], kind, 0, 0, highest)
    p = [paths[128 * i : 128 * (i + 1)] for i in range(5)]
    a0, a1 = total[0:128], [total[128 * m : 128 * (m + 1)] for m in (1, 2, 3)]
    square = a1[0] * a1[0] + a1[1] * a1[1] + a1[2] * a1[2]
    b0 = (p[0] * a0 + p[1] * a0 * a0 + p[2] * square).astype(bf16)
    rows = [dot(read_weight[...].astype(f32), dot(out_weight[0], b0, 0, 0), 1, 0, highest)]
    for m in range(3):
        b1 = (p[3] * a1[m] + p[4] * a0 * a1[m]).astype(bf16)
        rows.append(dot(force_weight[...], dot(out_weight[1], b1, 0, 0), 1, 0, highest))
    rows.append(jnp.zeros((5, 256), f32))
    result = jnp.concatenate(rows, axis=0)
    out[...] = jnp.zeros(out.shape, f32)
    for s in range(2):
        out[home[s] // 2] = result[:, s * 128 : (s + 1) * 128]


def final_kernel(dest, sent, own, read_vector, forces, energies):
    for b in range(2):
        cut = slice(b * 128, (b + 1) * 128)
        both = own[:, cut] + sent[dest[b]]
        forces[:, cut] = both[16:19]
        energies[:, cut] = (
            dot(read_vector[...], silu(both[0:16]), 1, 0, highest) + both[19:20]
        )


def whole(shape, dtype=f32):
    return jax.ShapeDtypeStruct(shape, dtype)


def blocks_of(shape):
    return pl.BlockSpec(shape, lambda i, home: (0,) * len(shape))


def on_device(
    positions,
    species,
    features,
    move_dest,
    move_slot,
    halo_list,
    neighbours,
    neighbour_count,
    wave_index,
    radial_in,
    radial_mid,
    radial_out,
    up_weight,
    prod_weight,
    out_weight,
    skip_weight,
    charge_weight,
    field_weight,
    read_weight,
    read_vector,
    force_weight,
):
    place = jnp.stack([lax.axis_index("gx"), lax.axis_index("yz")]).astype(i32)
    force_row = force_weight.reshape(1, 128)
    vmem = pl.BlockSpec(memory_space=pltpu.VMEM)

    read_rows = read_weight.T
    send_up, charges = pl.pallas_call(
        up_kernel,
        out_shape=(whole((2, 512, 128), bf16), whole((8, 256))),
        compiler_params=params(56),
        cost_estimate=cost(1 << 25, 0, 1 << 20),
        name="up",
    )(features, up_weight, charge_weight.T)
    moved_up = lax.all_gather(send_up, "yz", axis=0, tiled=True)

    moments, basis, waves = pl.pallas_call(
        moment_kernel,
        out_shape=(
            whole((128, 16, 128), bf16),
            whole((128 * SLABS, 512)),
            whole((40, 256)),
        ),
        in_specs=[SMEM] * 3 + [vmem] * 4,
        scratch_shapes=[pltpu.VMEM((128, 16, 128), f32)],
        compiler_params=params(56),
        cost_estimate=cost(1 << 30, 1 << 15, 3 << 20),
        name="moment",
    )(
        move_dest,
        move_slot,
        place,
        charges,
        positions,
        species.reshape(1, 256),
        halo_list.reshape(1, 32),
    )
    sent = lax.all_to_all(moments, ("gx", "yz"), 0, 0, tiled=True)
    coeffs = pl.pallas_call(
        weight_kernel,
        out_shape=whole((128, 8, 128)),
        in_specs=[SMEM, vmem, vmem],
        compiler_params=params(12),
        cost_estimate=cost(1 << 27, 1 << 11, 1 << 20),
        name="weight",
    )(place, sent, wave_index)
    coeffs = lax.all_to_all(coeffs, ("gx", "yz"), 0, 0, tiled=True)

    hidden, offsets, kinds, home = pl.pallas_call(
        radial_kernel,
        out_shape=(
            whole((64, 64, 256), bf16),
            whole((3, 64, 256)),
            whole((1, 256)),
            whole((2,), i32),
        ),
        in_specs=[SMEM] + [vmem] * 5,
        out_specs=(vmem, vmem, vmem, SMEM),
        scratch_shapes=[
            pltpu.VMEM((128, 16, 128), f32),
            pltpu.VMEM((64, 256), f32),
            pltpu.VMEM((64, 256), f32),
        ],
        compiler_params=params(16),
        cost_estimate=cost(1 << 32, 1 << 22, 4 << 20),
        name="radial",
    )(place, sent, neighbours.T, neighbour_count.reshape(1, 256), radial_in, radial_mid)

    nearby = [
        pl.BlockSpec((1, 512, 128), lambda i, home: (home[0], 0, 0)),
        pl.BlockSpec((1, 512, 128), lambda i, home: (home[1], 0, 0)),
    ]
    send_halo = pl.pallas_call(
        halo_kernel,
        out_shape=whole((32, 512), bf16),
        grid_spec=pltpu.PrefetchScalarGridSpec(
            num_scalar_prefetch=1,
            grid=(1,),
            in_specs=nearby + [blocks_of((1, 32))],
            out_specs=blocks_of((32, 512)),
        ),
        compiler_params=params(4),
        cost_estimate=cost(1 << 24, 0, 1 << 18),
        name="halo",
    )(home, moved_up, moved_up, halo_list.reshape(1, 32))
    ghosts = []
    for axis in ("gx", "yz"):
        count = lax.axis_size(axis)
        up = [(i, (i + 1) % count) for i in range(count)]
        ghosts.append(lax.ppermute(send_halo, axis, up))
        ghosts.append(lax.ppermute(send_halo, axis, [(b, a) for a, b in up]))

    part = pl.pallas_call(
        field_kernel,
        out_shape=whole((24, 256)),
        scratch_shapes=[pltpu.VMEM((384, 128 * SLABS), f32)],
        compiler_params=params(16),
        cost_estimate=cost(1 << 31, 0, 3 << 20),
        name="field",
    )(coeffs, basis, waves, features, skip_weight, field_weight, read_rows, force_row)

    returned = pl.pallas_call(
        message_kernel,
        out_shape=whole((16, 24, 128)),
        grid_spec=pltpu.PrefetchScalarGridSpec(
            num_scalar_prefetch=1,
            grid=(1,),
            in_specs=nearby
            + [blocks_of((32, 512))] * 4
            + [
                blocks_of((64, 256)),
                blocks_of((3, 64, 256)),
                blocks_of((64, 64, 256)),
                blocks_of((1, 256)),
                blocks_of((64, 512)),
                blocks_of((6, 640)),
                blocks_of((2, 128, 128)),
                blocks_of((16, 128)),
                blocks_of((1, 128)),
            ],
            out_specs=blocks_of((16, 24, 128)),
            scratch_shapes=[pltpu.VMEM((512, 384), bf16), pltpu.VMEM((512, 256), f32)],
        ),
        compiler_params=params(16),
        cost_estimate=cost(12 << 30, 0, 4 << 20),
        name="message",
    )(
        home,
        moved_up,
        moved_up,
        *ghosts,
        neighbours.T,
        offsets,
        hidden,
        kinds,
        radial_out,
        prod_weight,
        out_weight,
        read_rows,
        force_row,
    )
    returned = lax.all_to_all(returned, "yz", 0, 0, tiled=True)
    forces, energies = pl.pallas_call(
        final_kernel,
        out_shape=(whole((3, 256)), whole((1, 256))),
        in_specs=[SMEM, vmem, vmem, vmem],
        compiler_params=params(4),
        cost_estimate=cost(1 << 14, 1 << 12, 1 << 16),
        name="final",
    )(move_dest, returned, part, read_vector.reshape(1, 16))
    return forces, energies.reshape(256)


def solution(mesh):
    whole_spec = P(("gx", "yz"))
    in_specs = (
        (P(None, ("gx", "yz")), whole_spec, P(("gx", "yz"), None))
        + (whole_spec,) * 3
        + (P(("gx", "yz"), None), whole_spec)
        + (P(),) * 13
    )
    out_specs = (P(None, ("gx", "yz")), whole_spec)
    return jax.shard_map(
        on_device, mesh=mesh, in_specs=in_specs, out_specs=out_specs, check_vma=False
    )
```

time: 332 us -> 127 us (0.38)
  matrix products: 129 us -> 0 us
  waiting for transfers between devices: 117 us -> 5.53 us
  Pallas kernels: 0 us -> 48.9 us
  blocking collectives: 0 us -> 27.4 us
  other arithmetic: 21.1 us -> 0.58 us
  local copies, waits for them, and re-layouts: 21.9 us -> 7.45 us
  loops' own time: 6.18 us -> 0 us
    dot_general x73 -> x0, matrix products: 129 us -> none  [the longest x8 23.1 us: one_block(): jnp.einsum('ak,aq->kq', jnp.sin(phases), charges, precision=highest)]
    psum x1 -> x0, waiting for transfers between devices: 69.1 us -> none  [on_device(): total_real, total_imag = lax.psum((part_real, part_imag), ('gx', 'yz'))]
    pallas_call x0 -> x8, Pallas kernels: none -> 48.9 us  [the longest x1 24.9 us: on_device(): pl.pallas_call(message_kernel, out_shape=whole((16, 24, 128)), grid_spec=...]
    all_gather x1, waiting for transfers between devices: 40.2 us -> 2.11 us  [on_device(): moved_up = lax.all_gather(send_up, 'yz', axis=0, tiled=True)]
    all_to_all x0 -> x1, blocking collectives: none -> 27.4 us  [on_device(): sent = lax.all_to_all(moments, ('gx', 'yz'), 0, 0, tiled=True)]
    reduce_sum x6 -> x0, other arithmetic: 13.7 us -> none  [the longest x4 13.6 us: neighbour_sum(): jnp.sum(values.reshape(atom_count, slot_count, channels), axis=1)]
    all_to_all x1 -> x2, starting transfers between devices: 5.04 us -> 14.9 us  [the longest x1 9.19 us: on_device(): coeffs = lax.all_to_all(coeffs, ('gx', 'yz'), 0, 0, tiled=True)]
    ppermute x8 -> x4, starting transfers between devices: 16.1 us -> 7.06 us  [the longest x2 5.59 us: on_device(): ghosts.append(lax.ppermute(send_halo, axis, [(b, a) for a, b in up]))]
  transfers between devices with their start and end apart: 11 -> 7, of which waited for: 5 -> 2; matrix products, arithmetic and copies ran while one was open for 34% -> 0% of each run, Pallas kernels for 0% -> 36%
where the time goes in v1:
time: 127 us; the launch traced here: 126 us
  Pallas kernels  48.9 us (39%)
  blocking collectives  27.4 us (22%)
  starting transfers between devices  22 us (17%)
  between operations  14.3 us (11%)
  local copies, waits for them, and re-layouts  7.45 us (6%)
  waiting for transfers between devices  5.53 us (4%)
    all_to_all x1, blocking collectives, on_device(): sent = lax.all_to_all(moments, ('gx', 'yz'), 0, 0, tiled=True)  27.4 us
    pallas_call x1, Pallas kernels, on_device(): pl.pallas_call(message_kernel, out_shape=whole((16, 24, 128)), grid_spec=...  24.9 us
    pallas_call x1, Pallas kernels, on_device(): pl.pallas_call(radial_kernel, out_shape=(whole((64, 64, 256), bf16), whol...  10.9 us
    all_to_all x1, starting transfers between devices, on_device(): coeffs = lax.all_to_all(coeffs, ('gx', 'yz'), 0, 0, tiled=True)  9.19 us
    unnamed x46, local copies, waits for them, and re-layouts  7.45 us
    all_to_all x1, starting transfers between devices, on_device(): returned = lax.all_to_all(returned, 'yz', 0, 0, tiled=True)  5.73 us
    ppermute x2, starting transfers between devices, on_device(): ghosts.append(lax.ppermute(send_halo, axis, [(b, a) for a, b in up]))  5.59 us
    pallas_call x1, Pallas kernels, on_device(): pl.pallas_call(moment_kernel, out_shape=(whole((128, 16, 128), bf16), who...  4.1 us
  transfers between devices with their start and end apart: 7, of which 2 were waited for; matrix products, arithmetic and copies ran while one was open for 0% of the time, Pallas kernels for 36%

profile of v1, /device:TPU:1, one launch (start us, length us, event | category | flops | bytes accessed | tf_op | source)
XLA Modules:
  0.0 126.2 jit_solution(11382488137673439372)
XLA Ops:
  7.2 0.0 all-gather.2.cloned.1.call-start
  7.2 2.0 %up.2 = (bf16[2,512,128]{2,1,0:T(8,128)(2,1)}, f32[8,256]{1,0:T(8,128)}) custom-call(bf16[256,512]{1,0:T(8,128)(2,1)} %feat.3, bf16[2,128,128]{2,1,0:T(8,128)(2,1)} %up.3, bf16[8,128]{1,0:T(8,128)(2,1)} %bitcast.21), custom_call_target="tpu_custom_call" | custom-call | flops 33554432 | bytes 1048576 | tf_op jit(solution)/shard_map/up/pallas_call | solution.py:454
  9.3 0.0 all-gather.2.cloned.1.call-update
  9.3 0.6 pad_add_fusion.place
  9.9 4.1 %moment.1 = (bf16[128,16,128]{2,1,0:T(8,128)(2,1)}, f32[768,512]{1,0:T(8,128)}, f32[40,256]{1,0:T(8,128)}) custom-call(s32[2]{0:T(128)} %dest.3, s32[2]{0:T(128)} %slot.1, s32[2]{0:T(128)} %pad_add_fusion.place, f32[8,256]{1,0:T(8,128)} %get-tuple-element.13.charges_in, bf16[3,256]{1,0:T(4,128)(2,1)} %pos.1, s32[1,256]{1,0:T(1,128)} %bitcast.22, ...), custom_call_target="tpu_custom_call" | custom-call | flops 1073741824 | bytes 3145728 | tf_op jit(solution)/shard_map/moment/pallas_call | solution.py:463
  14.0 27.4 %all_to_all.15.sent = bf16[128,16,128]{2,1,0:T(8,128)(2,1)S(1)} all-to-all(bf16[128,16,128]{2,1,0:T(8,128)(2,1)} %get-tuple-element.14), channel_id=1, replica_groups=mesh['gx'=8,'yz'=16] {'gx','yz'}, dimensions={0} | all-to-all | bytes 1048576 | tf_op jit(solution)/shard_map/all_to_all | solution.py:484
  41.4 10.9 %radial.1 = (bf16[64,64,256]{2,1,0:T(8,128)(2,1)S(1)}, f32[3,64,256]{2,1,0:T(8,128)S(1)}, f32[1,256]{1,0:T(1,128)S(1)}, s32[2]{0:T(128)S(1)}) custom-call(s32[2]{0:T(128)S(1)} %copy-done.7, bf16[128,16,128]{2,1,0:T(8,128)(2,1)S(1)} %all_to_all.15.sent, s32[64,256]{1,0:T(8,128)S(1)} %bitcast.14, s32[1,256]{1,0:T(1,128)S(1)} %bitcast.18, ...), custom_call_target="tpu_custom_call" | custom-call | flops 4294967296 | bytes 4194304 | tf_op jit(solution)/shard_map/radial/pallas_call | solution.py:495
  52.3 1.4 %copy-done.20 = bf16[64,64,256]{2,1,0:T(8,128)(2,1)} copy-done((bf16[64,64,256]{2,1,0:T(8,128)(2,1)}, bf16[64,64,256]{2,1,0:T(8,128)(2,1)S(1)}, u32[]{:S(2)}) %copy-start.20) | copy-done | bytes 2097176
  53.7 2.1 %all-gather.2.cloned.1.call-done.first.second = bf16[32,512,128]{2,1,0:T(8,128)(2,1)} async-done(((bf16[2,512,128]{2,1,0:T(8,128)(2,1)}), bf16[32,512,128]{2,1,0:T(8,128)(2,1)}) %all-gather.2.cloned.1.call-update) | async-done | bytes 4194320 | tf_op jit(solution)/shard_map/all_gather | solution.py:461
  55.8 2.2 %copy-done = bf16[32,512,128]{2,1,0:T(8,128)(2,1)S(1)} copy-done((bf16[32,512,128]{2,1,0:T(8,128)(2,1)S(1)}, bf16[32,512,128]{2,1,0:T(8,128)(2,1)}, u32[]{:S(2)}) %copy-start) | copy-done | bytes 4194328
  58.0 0.7 halo.1
  58.7 0.0 copy-start.10
  58.8 0.3 collective-permute-start.3
  59.1 1.5 %collective-permute-start.2 = (bf16[32,512]{1,0:T(8,128)(2,1)S(1)}, bf16[32,512]{1,0:T(8,128)(2,1)S(1)}, u32[]{:S(2)}, u32[]{:S(2)}) collective-permute-start(bf16[32,512]{1,0:T(8,128)(2,1)S(1)} %halo.1), channel_id=1, source_target_pairs={{0,1},{1,2},{2,3},{3,4},{4,5},{5,6},{6,7},{7,8},{8,9},{9,10},{10,1... | collective-permute-start | bytes 98312 | tf_op jit(solution)/shard_map/ppermute | solution.py:536
  60.6 5.2 %collective-permute-start.1 = (bf16[32,512]{1,0:T(8,128)(2,1)S(1)}, bf16[32,512]{1,0:T(8,128)(2,1)S(1)}, u32[]{:S(2)}, u32[]{:S(2)}) collective-permute-start(bf16[32,512]{1,0:T(8,128)(2,1)S(1)} %halo.1), channel_id=1, source_target_pairs={{16,0},{32,16},{48,32},{64,48},{80,64},{96,80},{112,96},{0,112},{1... | collective-permute-start | bytes 98312 | tf_op jit(solution)/shard_map/ppermute | solution.py:537
  65.9 1.9 %weight.1 = f32[128,8,128]{2,1,0:T(8,128)} custom-call(s32[2]{0:T(128)S(1)} %copy-done.7, bf16[128,16,128]{2,1,0:T(8,128)(2,1)S(1)} %all_to_all.15.sent, s32[3,4096]{1,0:T(4,128)S(1)} %copy-done.3), custom_call_target="tpu_custom_call" | custom-call | flops 134217728 | bytes 1048576 | tf_op jit(solution)/shard_map/weight/pallas_call | solution.py:485
  67.7 9.2 %all-to-all-start.2 = ((f32[128,8,128]{2,1,0:T(8,128)}), f32[128,8,128]{2,1,0:T(8,128)S(1)}, u32[]{:S(2)}, u32[]{:S(2)}) async-start(f32[128,8,128]{2,1,0:T(8,128)} %weight.1), calls=%async_computation.2 | async-start | bytes 1048576 | tf_op jit(solution)/shard_map/all_to_all | solution.py:493
  77.0 2.2 %copy-done.1 = bf16[32,512,128]{2,1,0:T(8,128)(2,1)S(1)} copy-done((bf16[32,512,128]{2,1,0:T(8,128)(2,1)S(1)}, bf16[32,512,128]{2,1,0:T(8,128)(2,1)}, u32[]{:S(2)}) %copy-start.1) | copy-done | bytes 4194328
  79.2 1.6 %copy-done.21 = bf16[64,64,256]{2,1,0:T(8,128)(2,1)S(1)} copy-done((bf16[64,64,256]{2,1,0:T(8,128)(2,1)S(1)}, bf16[64,64,256]{2,1,0:T(8,128)(2,1)}, u32[]{:S(2)}) %copy-start.21) | copy-done | bytes 2097176
  80.8 24.9 %message.1 = f32[16,24,128]{2,1,0:T(8,128)} custom-call(s32[2]{0:T(128)S(1)} %get-tuple-element.15.home, bf16[32,512,128]{2,1,0:T(8,128)(2,1)S(1)} %copy-done.1, bf16[32,512,128]{2,1,0:T(8,128)(2,1)S(1)} %copy-done.1, bf16[32,512]{1,0:T(8,128)(2,1)S(1)} %collective-permute-done.ghost0, bf16[32,512]{1,0:T(8,128)(2,1)S(1)} %collective-permute-done.1.ghost1, ...), custom_call_target="tpu_custom_call" | custom-call | flops 12884901888 | bytes 4194304 | tf_op jit(solution)/shard_map/message/pallas_call | solution.py:548
  105.7 5.7 %all-to-all-start.1 = ((f32[16,24,128]{2,1,0:T(8,128)}), f32[16,24,128]{2,1,0:T(8,128)S(1)}, u32[]{:S(2)}, u32[]{:S(2)}) async-start(f32[16,24,128]{2,1,0:T(8,128)} %message.1), calls=%async_computation.1 | async-start | bytes 393216 | tf_op jit(solution)/shard_map/all_to_all | solution.py:588
  111.5 3.2 %field.1.own = f32[24,256]{1,0:T(8,128)S(1)} custom-call(f32[128,8,128]{2,1,0:T(8,128)S(1)} %all-to-all-done.2.coeffs, f32[768,512]{1,0:T(8,128)S(1)} %copy-done.19, f32[40,256]{1,0:T(8,128)S(1)} %copy-done.22, bf16[256,512]{1,0:T(8,128)(2,1)S(1)} %copy-done.2, bf16[2,128,128]{2,1,0:T(8,128)(2,1)S(1)} %copy-done.11, f32[8,128]{1,0:T(8,128)S(1)} %copy-done.15, ...), custom_call_target="tpu_custom_call" | custom-call | flops 2147483648 | bytes 3145728 | tf_op jit(solution)/shard_map/field/pallas_call | solution.py:539
  114.7 3.4 %all-to-all-done.1.sent = f32[16,24,128]{2,1,0:T(8,128)S(1)} async-done(((f32[16,24,128]{2,1,0:T(8,128)}), f32[16,24,128]{2,1,0:T(8,128)S(1)}, u32[]{:S(2)}, u32[]{:S(2)}) %all-to-all-start.1) | async-done | bytes 196640 | tf_op jit(solution)/shard_map/all_to_all | solution.py:588
  118.1 1.3 %final.1 = (f32[3,256]{1,0:T(4,128)}, f32[1,256]{1,0:T(1,128)}) custom-call(s32[2]{0:T(128)S(1)} %copy-done.5, f32[16,24,128]{2,1,0:T(8,128)S(1)} %all-to-all-done.1.sent, f32[24,256]{1,0:T(8,128)S(1)} %field.1.own, f32[1,16]{1,0:T(1,128)S(1)} %bitcast.13), custom_call_target="tpu_custom_call" | custom-call | flops 16384 | bytes 65536 | tf_op jit(solution)/shard_map/final/pallas_call | solution.py:589
  (47 shorter events, 0.1 us)
Async XLA Ops:
  7.2 48.6 %all-gather.2.cloned.1.call-start = ((), (), s32[]{:S(2)}) async-start(), calls=%async_computation.3 | async-start | bytes 4456448 | tf_op jit(solution)/shard_map/all_gather | solution.py:461
  9.9 31.5 %copy-start.7 = (s32[2]{0:T(128)S(1)}, s32[2]{0:T(128)}, u32[]{:S(2)}) copy-start(s32[2]{0:T(128)} %pad_add_fusion.place) | copy-start | bytes 28
  9.9 31.5 %copy-start.8 = (s32[256,64]{0,1:T(8,128)S(1)}, s32[256,64]{0,1:T(8,128)}, u32[]{:S(2)}) copy-start(s32[256,64]{0,1:T(8,128)} %param.27) | copy-start | bytes 196612
  9.9 31.5 %copy-start.12 = (bf16[2,64,64]{2,1,0:T(8,128)(2,1)S(1)}, bf16[2,64,64]{2,1,0:T(8,128)(2,1)}, u32[]{:S(2)}) copy-start(bf16[2,64,64]{2,1,0:T(8,128)(2,1)} %radial_mid.1) | copy-start | bytes 49156
  9.9 31.6 %copy-start.16 = (bf16[8,64]{1,0:T(8,128)(2,1)S(1)}, bf16[8,64]{1,0:T(8,128)(2,1)}, u32[]{:S(2)}) copy-start(bf16[8,64]{1,0:T(8,128)(2,1)} %radial_in.1) | copy-start | bytes 3076
  9.9 31.6 %copy-start.17 = (s32[256]{0:T(256)S(1)}, s32[256]{0:T(256)}, u32[]{:S(2)}) copy-start(s32[256]{0:T(256)} %param.28) | copy-start | bytes 3076
  41.4 14.4 %copy-start.4 = (s32[32]{0:T(128)S(1)}, s32[32]{0:T(128)}, u32[]{:S(2)}) copy-start(s32[32]{0:T(128)} %param.26) | copy-start | bytes 388
  58.0 7.9 %copy-start.3 = (s32[3,4096]{1,0:T(4,128)S(1)}, s32[3,4096]{1,0:T(4,128)}, u32[]{:S(2)}) copy-start(s32[3,4096]{1,0:T(4,128)} %wave_index.1) | copy-start | bytes 147460
  58.7 18.2 %copy-start.9 = (bf16[64,512]{1,0:T(8,128)(2,1)S(1)}, bf16[64,512]{1,0:T(8,128)(2,1)}, u32[]{:S(2)}) copy-start(bf16[64,512]{1,0:T(8,128)(2,1)} %radial_out.1) | copy-start | bytes 196612
  58.7 18.2 %copy-start.10 = (bf16[2,128,128]{2,1,0:T(8,128)(2,1)S(1)}, bf16[2,128,128]{2,1,0:T(8,128)(2,1)}, u32[]{:S(2)}) copy-start(bf16[2,128,128]{2,1,0:T(8,128)(2,1)} %out_weight.1) | copy-start | bytes 196612
  58.8 18.2 %copy-start.13 = (f32[6,640]{1,0:T(8,128)S(1)}, f32[6,640]{1,0:T(8,128)}, u32[]{:S(2)}) copy-start(f32[6,640]{1,0:T(8,128)} %prod_weight.1) | copy-start | bytes 46084
  58.8 18.2 %copy-start.14 = (bf16[128,16]{0,1:T(8,128)(2,1)S(1)}, bf16[128,16]{0,1:T(8,128)(2,1)}, u32[]{:S(2)}) copy-start(bf16[128,16]{0,1:T(8,128)(2,1)} %param.39) | copy-start | bytes 12292
  58.8 18.2 %copy-start.18 = (f32[128]{0:T(128)S(1)}, f32[128]{0:T(128)}, u32[]{:S(2)}) copy-start(f32[128]{0:T(128)} %param.41) | copy-start | bytes 1540
  58.8 18.1 %collective-permute-start.3 = (bf16[32,512]{1,0:T(8,128)(2,1)S(1)}, bf16[32,512]{1,0:T(8,128)(2,1)S(1)}, u32[]{:S(2)}, u32[]{:S(2)}) collective-permute-start(bf16[32,512]{1,0:T(8,128)(2,1)S(1)} %halo.1), channel_id=1, source_target_pairs={{1,0},{2,1},{3,2},{4,3},{5,4},{6,5},{7,6},{8,7},{9,8},{10,9},{11,1... | collective-permute-start | bytes 98312 | tf_op jit(solution)/shard_map/ppermute | solution.py:537
  59.1 17.8 %collective-permute-start.2 = (bf16[32,512]{1,0:T(8,128)(2,1)S(1)}, bf16[32,512]{1,0:T(8,128)(2,1)S(1)}, u32[]{:S(2)}, u32[]{:S(2)}) collective-permute-start(bf16[32,512]{1,0:T(8,128)(2,1)S(1)} %halo.1), channel_id=1, source_target_pairs={{0,1},{1,2},{2,3},{3,4},{4,5},{5,6},{6,7},{7,8},{8,9},{9,10},{10,1... | collective-permute-start | bytes 98312 | tf_op jit(solution)/shard_map/ppermute | solution.py:536
  60.6 16.3 %collective-permute-start.1 = (bf16[32,512]{1,0:T(8,128)(2,1)S(1)}, bf16[32,512]{1,0:T(8,128)(2,1)S(1)}, u32[]{:S(2)}, u32[]{:S(2)}) collective-permute-start(bf16[32,512]{1,0:T(8,128)(2,1)S(1)} %halo.1), channel_id=1, source_target_pairs={{16,0},{32,16},{48,32},{64,48},{80,64},{96,80},{112,96},{0,112},{1... | collective-permute-start | bytes 98312 | tf_op jit(solution)/shard_map/ppermute | solution.py:537
  65.9 11.1 %collective-permute-start = (bf16[32,512]{1,0:T(8,128)(2,1)S(1)}, bf16[32,512]{1,0:T(8,128)(2,1)S(1)}, u32[]{:S(2)}, u32[]{:S(2)}) collective-permute-start(bf16[32,512]{1,0:T(8,128)(2,1)S(1)} %halo.1), channel_id=1, source_target_pairs={{0,16},{16,32},{32,48},{48,64},{64,80},{80,96},{96,112},{112,0},{1... | collective-permute-start | bytes 98312 | tf_op jit(solution)/shard_map/ppermute | solution.py:536
  67.7 38.0 %all-to-all-start.2 = ((f32[128,8,128]{2,1,0:T(8,128)}), f32[128,8,128]{2,1,0:T(8,128)S(1)}, u32[]{:S(2)}, u32[]{:S(2)}) async-start(f32[128,8,128]{2,1,0:T(8,128)} %weight.1), calls=%async_computation.2 | async-start | bytes 1048576 | tf_op jit(solution)/shard_map/all_to_all | solution.py:493
  80.8 30.6 %copy-start.2 = (bf16[256,512]{1,0:T(8,128)(2,1)S(1)}, bf16[256,512]{1,0:T(8,128)(2,1)}, u32[]{:S(2)}) copy-start(bf16[256,512]{1,0:T(8,128)(2,1)} %feat.3) | copy-start | bytes 786436
  80.8 30.6 %copy-start.11 = (bf16[2,128,128]{2,1,0:T(8,128)(2,1)S(1)}, bf16[2,128,128]{2,1,0:T(8,128)(2,1)}, u32[]{:S(2)}) copy-start(bf16[2,128,128]{2,1,0:T(8,128)(2,1)} %skip_weight.1) | copy-start | bytes 196612
  80.8 30.6 %copy-start.15 = (f32[8,128]{1,0:T(8,128)S(1)}, f32[8,128]{1,0:T(8,128)}, u32[]{:S(2)}) copy-start(f32[8,128]{1,0:T(8,128)} %field_weight.1) | copy-start | bytes 12292
  80.8 30.6 %copy-start.19 = (f32[768,512]{1,0:T(8,128)S(1)}, f32[768,512]{1,0:T(8,128)}, u32[]{:S(2)}) copy-start(f32[768,512]{1,0:T(8,128)} %get-tuple-element.20.basis) | copy-start | bytes 4718596
  80.8 30.6 %copy-start.22 = (f32[40,256]{1,0:T(8,128)S(1)}, f32[40,256]{1,0:T(8,128)}, u32[]{:S(2)}) copy-start(f32[40,256]{1,0:T(8,128)} %get-tuple-element.21.waves) | copy-start | bytes 122884
  105.7 12.4 %all-to-all-start.1 = ((f32[16,24,128]{2,1,0:T(8,128)}), f32[16,24,128]{2,1,0:T(8,128)S(1)}, u32[]{:S(2)}, u32[]{:S(2)}) async-start(f32[16,24,128]{2,1,0:T(8,128)} %message.1), calls=%async_computation.1 | async-start | bytes 393216 | tf_op jit(solution)/shard_map/all_to_all | solution.py:588
  (6 other events, 20.6 us)
Sparse Core Ops, SparseCore 0:
  9.7 46.0 all-gather.1

commit v2 on v1

--- a/solution.py
+++ b/solution.py
@@ -16,7 +16,11 @@
 
 NX, NY, NZ = 16, 32, 2
 SLABS = 2 * NZ + 2
-SLOT_GROUP = 4
+RADIAL_GROUP, SLOT_GROUP = 16, 8
+
+
+def row_of(chunk, component):
+    return 128 * chunk + 32 * component
 
 
 def dot(a, b, ca, cb, precision=None):
@@ -25,6 +29,15 @@
     )
 
 
+def halves(v):
+    high = v.astype(bf16)
+    return high, (v - high.astype(f32)).astype(bf16)
+
+
+def dot_halves(a, b, ca, cb):
+    return dot(a[0], b[0], ca, cb) + (dot(a[0], b[1], ca, cb) + dot(a[1], b[0], ca, cb))
+
+
 def silu(v):
     half = 0.5 * v
     return half + half * jnp.tanh(half)
@@ -39,8 +52,8 @@
     return jnp.cos(angle), jnp.sin(angle)
 
 
-def params(vmem=32):
-    return pltpu.CompilerParams(vmem_limit_bytes=vmem << 20)
+def params(mebibytes=58):
+    return pltpu.CompilerParams(vmem_limit_bytes=mebibytes << 20)
 
 
 def cost(flops, transcendentals, moved):
@@ -56,11 +69,12 @@
         for c in range(4):
             rows = feat[b * 128 : (b + 1) * 128, c * 128 : (c + 1) * 128]
             mapped = dot(up[min(c, 1)], rows, 0, 1).astype(bf16)
-            out[b, c * 128 : (c + 1) * 128, :] = mapped
+            for q in range(4):
+                out[b, row_of(q, c) : row_of(q, c) + 32, :] = mapped[32 * q : 32 * (q + 1)]
 
 
 def moment_kernel(
-    dest, slot, place, charges_in, pos, species, halo, out, basis, waves, stage
+    dest, slot, place, charges_in, pos, species, halo, out, basis_high, basis_low, waves, basis, stage
 ):
     gx = place[0].astype(f32)
     charges = charges_in[...]
@@ -99,9 +113,9 @@
     waves[24:40] = sin_x
     left_cos = (cos_x[:, None, :] * charges[None]).reshape(128, 256)
     left_sin = (sin_x[:, None, :] * charges[None]).reshape(128, 256)
-    moments = dot(left_cos, basis[:, 0:256], 1, 1, highest) + dot(
-        left_sin, basis[:, 256:512], 1, 1, highest
-    )
+    basis_high[...], basis_low[...] = halves(basis[...])
+    left = halves(jnp.concatenate([left_cos, left_sin], axis=1))
+    moments = dot_halves(left, (basis_high[...], basis_low[...]), 1, 1)
     for i in range(SLABS):
         stage[:, i, :] = moments[:, i * 128 : (i + 1) * 128]
     kinds = species[...].astype(f32)
@@ -120,8 +134,7 @@
     out[...] = stage[...].astype(bf16)
 
 
-def weight_kernel(place, sent, wave_index, out):
-    total = jnp.sum(sent[...].astype(f32), axis=0)[0:8]
+def count_kernel(place, wave_index, out):
     own_x = (place[0] * 16 + place[1]) // 8 + 1
     kx, ky, kz = wave_index[0:1, :], wave_index[1:2, :], wave_index[2:3, :]
     count = kx.shape[1]
@@ -147,20 +160,89 @@
     squared = x_wave * x_wave + y_wave * y_wave + z_wave * z_wave
     prefactor = 8.0 * math.pi * ewald_scale / 128.0
     weight = prefactor * jnp.exp(-0.5 * ewald_width * ewald_width * squared) / squared
-    direct = weight * jnp.where(in_flat, flat, even)
-    crossed = weight * jnp.where(in_flat, 0.0, odd)
+    out[0:8] = weight * jnp.where(in_flat, flat, even)
+    out[8:16] = weight * jnp.where(in_flat, 0.0, odd)
+
+
+def weight_kernel(
+    place, sent, weights, out, table_out, kinds_out, lists_out, home_out, stage
+):
+    stage[...] = sent[...].astype(f32)
+    total = jnp.sum(stage[:, 0:8, :], axis=0)
+    row, lane = iota((8, 128), 0), iota((8, 128), 1)
     total = jnp.where(row < SLABS, total, 0.0)
     far = pltpu.roll(total, 64, 1)
     group = lane // 32
     swapped = jnp.where(group % 2 == 0, pltpu.roll(far, 96, 1), pltpu.roll(far, 32, 1))
     swapped = jnp.where((group == 0) | (group == 3), -swapped, swapped)
-    coefficient = total * direct + swapped * crossed
+    coefficient = total * weights[0:8] + swapped * weights[8:16]
     out[...] = jnp.broadcast_to(coefficient[None], out.shape)
+    gx, yz = place[0], place[1]
+    targets = [
+        (gx, yz),
+        ((gx + 7) % 8, yz),
+        ((gx + 1) % 8, yz),
+        (gx, (yz + 15) % 16),
+        (gx, (yz + 1) % 16),
+    ]
+    plan = jnp.transpose(stage[:, 14, :])
+    row = iota((16, 128), 0)
+    device = iota((16, 128), 1)
+    want_x, want_y = jnp.full((16, 128), -1, i32), jnp.full((16, 128), -1, i32)
+    for t, (tx, ty) in enumerate(targets):
+        want_x = jnp.where(row // 2 == t, tx, want_x)
+        want_y = jnp.where(row // 2 == t, ty, want_y)
+    here = (device // 16 == want_x).astype(f32)
+    want_y, want_slot = want_y.astype(f32), (row % 2).astype(f32)
+    picks = []
+    for b in range(2):
+        match = (plan[32 + b : 33 + b] == want_y) & (plan[34 + b : 35 + b] == want_slot)
+        picks.append(jnp.where(match, here, 0.0))
+    exact = [pick.astype(bf16) for pick in picks]
+
+    def from_home(first, step):
+        return sum(
+            dot(exact[b], stage[:, first + b * step, :].astype(bf16), 1, 0) for b in range(2)
+        )
+
+    xyz = [from_home(6 + m, 3) for m in range(3)]
+    kinds = from_home(12, 1)
+    kinds_out[...] = jnp.concatenate([kinds[0:1], kinds[1:2]], axis=1)
+    both = picks[0] + picks[1]
+    column = 2.0 * both * (device % 16).astype(f32) + picks[1]
+    for i, r in enumerate((0, 1, 6, 7, 8, 9)):
+        home_out[i] = jnp.sum(jnp.where(row == r, column, 0.0)).astype(i32)
+    lane = iota((1, 128), 1)
+    atom = iota((128, 128), 0)
+    ghosts = jnp.zeros((8, 128), f32)
+    for t, (tx, ty) in enumerate(targets[1:]):
+        listed = stage[tx * 16 + ty, 14:15, :].astype(i32)
+        if t:
+            listed = pltpu.roll(listed, 32 * t, 1)
+        listed = jnp.where(lane // 32 == t, listed, -1)
+        lists_out[t : t + 1] = listed
+        for s in range(2):
+            at = 2 * (t + 1) + s
+            rows = jnp.concatenate(
+                [x[at : at + 1] for x in xyz] + [jnp.zeros((5, 128), f32)], axis=0
+            )
+            chosen = jnp.where(atom + 128 * s == listed, 1.0, 0.0).astype(bf16)
+            ghosts = ghosts + dot(rows.astype(bf16), chosen, 1, 0)
+    part = lane // 32
+    shifts = [
+        jnp.where(part == 0, -1.0, jnp.where(part == 1, 1.0, 0.0)),
+        jnp.where(part == 2, -1.0, jnp.where(part == 3, 1.0, 0.0)),
+        jnp.zeros((1, 128), f32),
+    ]
+    zero = jnp.zeros((1, 128), f32)
+    rows = [v for m in range(3) for v in (xyz[m][0:1], xyz[m][1:2], ghosts[m : m + 1] + shifts[m])]
+    table_out[...] = jnp.concatenate(rows + [zero] * 7, axis=0)
 
 
 def field_kernel(
     coeffs,
-    basis,
+    basis_high,
+    basis_low,
     waves,
     feat,
     skip_weight,
@@ -187,7 +269,7 @@
             stacked[128:256, cut] = jnp.zeros((128, 128), f32)
             z_wave = (lane % 64 - NZ).astype(f32) * two_pi
         stacked[256:384, cut] = z_wave * jnp.where(low_half, half, -half)
-    grid = dot(stacked[...], basis[...], 1, 0, highest)
+    grid = dot_halves(halves(stacked[...]), (basis_high[...], basis_low[...]), 1, 0)
     charges = waves[0:8]
     cos_x = jnp.broadcast_to(waves[8:24][:, None, :], (NX, 8, 256)).reshape(128, 256)
     sin_x = jnp.broadcast_to(waves[24:40][:, None, :], (NX, 8, 256)).reshape(128, 256)
@@ -219,81 +301,18 @@
 
 
 def radial_kernel(
-    place,
-    sent,
+    table,
     neighbours,
     live,
     radial_in,
     radial_mid,
     hidden_out,
     offset_out,
-    kinds_out,
-    home_out,
-    stage,
     dist_stage,
     scale_stage,
 ):
-    stage[...] = sent[...].astype(f32)
-    gx, yz = place[0], place[1]
-    targets = [
-        (gx, yz),
-        ((gx + 7) % 8, yz),
-        ((gx + 1) % 8, yz),
-        (gx, (yz + 15) % 16),
-        (gx, (yz + 1) % 16),
-    ]
-    plan = jnp.transpose(stage[:, 14, :])
-    row = iota((16, 128), 0)
-    device = iota((16, 128), 1)
-    want_x, want_y = jnp.full((16, 128), -1, i32), jnp.full((16, 128), -1, i32)
-    for t, (tx, ty) in enumerate(targets):
-        want_x = jnp.where(row // 2 == t, tx, want_x)
-        want_y = jnp.where(row // 2 == t, ty, want_y)
-    here = (device // 16 == want_x).astype(f32)
-    want_y, want_slot = want_y.astype(f32), (row % 2).astype(f32)
-    picks = []
-    for b in range(2):
-        match = (plan[32 + b : 33 + b] == want_y) & (plan[34 + b : 35 + b] == want_slot)
-        picks.append(jnp.where(match, here, 0.0))
-
-    def from_home(first, step):
-        return dot(picks[0], stage[:, first, :], 1, 0, highest) + dot(
-            picks[1], stage[:, first + step, :], 1, 0, highest
-        )
-
-    xyz = [from_home(6 + m, 3) for m in range(3)]
-    kinds = from_home(12, 1)
-    kinds_out[...] = jnp.concatenate([kinds[0:1], kinds[1:2]], axis=1)
-    both = picks[0] + picks[1]
-    for s in range(2):
-        column = 2.0 * both * (device % 16).astype(f32) + picks[1]
-        home_out[s] = jnp.sum(jnp.where(row == s, column, 0.0)).astype(i32)
-    lane = iota((1, 128), 1)
-    atom = iota((128, 128), 0)
-    ghosts = jnp.zeros((8, 128), f32)
-    for t, (tx, ty) in enumerate(targets[1:]):
-        listed = stage[tx * 16 + ty, 14:15, :].astype(i32)
-        if t:
-            listed = pltpu.roll(listed, 32 * t, 1)
-        listed = jnp.where(lane // 32 == t, listed, -1)
-        for s in range(2):
-            at = 2 * (t + 1) + s
-            rows = jnp.concatenate(
-                [x[at : at + 1] for x in xyz] + [jnp.zeros((5, 128), f32)], axis=0
-            )
-            chosen = jnp.where(atom + 128 * s == listed, 1.0, 0.0)
-            ghosts = ghosts + dot(rows, chosen, 1, 0, highest)
-    part = lane // 32
-    shifts = [
-        jnp.where(part == 0, -1.0, jnp.where(part == 1, 1.0, 0.0)),
-        jnp.where(part == 2, -1.0, jnp.where(part == 3, 1.0, 0.0)),
-        jnp.zeros((1, 128), f32),
-    ]
     tables = [
-        [
-            jnp.broadcast_to(v, (8, 128))
-            for v in (xyz[m][0:1], xyz[m][1:2], ghosts[m : m + 1] + shifts[m])
-        ]
+        [jnp.broadcast_to(table[3 * m + i : 3 * m + i + 1], (8, 128)) for i in range(3)]
         for m in range(3)
     ]
     for n in range(0, 64, 8):
@@ -323,20 +342,48 @@
     centre = iota((8, 256), 0).astype(f32) * (cutoff_radius / 7.0)
 
     def body(group, carry):
-        start = group * SLOT_GROUP
+        start = group * RADIAL_GROUP
         rows = []
-        for j in range(SLOT_GROUP):
+        for j in range(RADIAL_GROUP):
             away = dist_stage[pl.ds(start + j, 1), :] - centre
             rows.append(jnp.exp(-4.0 * (away * away)))
         hidden = silu(dot(first, jnp.concatenate(rows, axis=1).astype(bf16), 1, 0)).astype(bf16)
         hidden = silu(dot(mid[0], hidden, 1, 0)).astype(bf16)
         hidden = silu(dot(mid[1], hidden, 1, 0))
-        for j in range(SLOT_GROUP):
+        for j in range(RADIAL_GROUP):
             scaled = hidden[:, j * 256 : (j + 1) * 256] * scale_stage[pl.ds(start + j, 1), :]
             hidden_out[start + j] = scaled.astype(bf16)
         return carry
 
+    lax.fori_loop(0, 64 // RADIAL_GROUP, body, 0)
+
+
+def spread_kernel(hidden, radial_out, out, spread):
+    mapped = jnp.transpose(radial_out[...].astype(f32)).astype(bf16)
+    for q in range(4):
+        for c in range(4):
+            at = 128 * c + 32 * q
+            spread[row_of(q, c) : row_of(q, c) + 32] = mapped[at : at + 32]
+
+    def body(group, carry):
+        for j in range(SLOT_GROUP):
+            n = group * SLOT_GROUP + j
+            out[n] = dot(spread[...], hidden[n], 1, 0).astype(bf16)
+        return carry
+
     lax.fori_loop(0, 64 // SLOT_GROUP, body, 0)
+
+
+def near_kernel(home, own0, own1, low0, low1, high0, high1, lists, table):
+    table[:, 0:128] = own0[0]
+    table[:, 128:256] = own1[0]
+    atom = iota((128, 128), 0)
+    ghosts = jnp.zeros((512, 128), f32)
+    for t, pair in ((2, (low0, low1)), (3, (high0, high1))):
+        for s, block in enumerate(pair):
+            chosen = jnp.where(atom + 128 * s == lists[t : t + 1], 1.0, 0.0).astype(bf16)
+            ghosts = ghosts + dot(block[0], chosen, 1, 0)
+    table[:, 256:384] = ghosts.astype(bf16)
 
 
 def halo_kernel(home, first, second, halo, out):
@@ -347,17 +394,13 @@
 
 def message_kernel(
     home,
-    first,
-    second,
-    ghost0,
-    ghost1,
-    ghost2,
-    ghost3,
+    near,
+    left,
+    right,
     neighbours,
     offsets,
-    hidden,
+    radials,
     kinds,
-    radial_out,
     prod_weight,
     out_weight,
     read_weight,
@@ -366,32 +409,59 @@
     table,
     total,
 ):
-    table[:, 0:128] = first[0]
-    table[:, 128:256] = second[0]
-    for t, ghost in enumerate((ghost0, ghost1, ghost2, ghost3)):
-        table[:, 256 + 32 * t : 288 + 32 * t] = jnp.transpose(ghost[...].astype(f32)).astype(bf16)
-    spread = jnp.transpose(radial_out[...].astype(f32)).astype(bf16)
+    table[...] = near[...]
+    table[:, 256:288] = jnp.transpose(left[...].astype(f32)).astype(bf16)
+    table[:, 288:320] = jnp.transpose(right[...].astype(f32)).astype(bf16)
     total[...] = jnp.zeros((512, 256), f32)
-    place = iota((384, 256), 0)
-
-    def body(n, carry):
-        chosen = jnp.where(place == neighbours[pl.ds(n, 1), :], 1.0, 0.0).astype(bf16)
-        radial = dot(spread, hidden[n], 1, 0)
-        up = dot(table[...], chosen, 1, 0)
-        u0, u1 = up[0:128], [up[128 * m : 128 * (m + 1)] for m in (1, 2, 3)]
-        r = [offsets[m, pl.ds(n, 1), :] for m in range(3)]
-        along = u1[0] * r[0] + u1[1] * r[1] + u1[2] * r[2]
-        total[0:128] += radial[0:128] * u0 + radial[128:256] * along
-        scalar = radial[256:384] * u0
-        for m in range(3):
-            total[128 * (m + 1) : 128 * (m + 2)] += scalar * r[m] + radial[384:512] * u1[m]
+    own_place = iota((256, 256), 0).astype(f32).astype(bf16)
+    ghost_place = iota((128, 256), 0).astype(f32).astype(bf16)
+
+    def choice(n):
+        row = neighbours[pl.ds(n, 1), :]
+        own = jnp.where(row < 256, row, -1).astype(f32).astype(bf16)
+        ghost = (row - 256).astype(f32).astype(bf16)
+        one, none = jnp.ones((), bf16), jnp.zeros((), bf16)
+        return jnp.concatenate(
+            [jnp.where(own_place == own, one, none), jnp.where(ghost_place == ghost, one, none)],
+            axis=0,
+        )
+
+    def body(group, carry):
+        slots = [group * SLOT_GROUP + j for j in range(SLOT_GROUP)]
+        chosen = [choice(n) for n in slots]
+        away = [[offsets[m, pl.ds(n, 1), :] for m in range(3)] for n in slots]
+        for q in range(4):
+            rows = slice(128 * q, 128 * (q + 1))
+            cuts = [slice(row_of(q, c), row_of(q, c) + 32) for c in range(4)]
+            sums = [total[cut] for cut in cuts]
+            for j, r in enumerate(away):
+                up = dot(table[rows], chosen[j], 1, 0)
+                radial = radials[slots[j], rows].astype(f32)
+                u = [up[32 * c : 32 * (c + 1)] for c in range(4)]
+                path = [radial[32 * c : 32 * (c + 1)] for c in range(4)]
+                along = u[1] * r[0] + u[2] * r[1] + u[3] * r[2]
+                sums[0] = sums[0] + path[0] * u[0] + path[1] * along
+                scalar = path[2] * u[0]
+                for m in range(3):
+                    sums[m + 1] = sums[m + 1] + scalar * r[m] + path[3] * u[m + 1]
+            for cut, value in zip(cuts, sums):
+                total[cut] = value
         return carry
 
-    lax.fori_loop(0, 64, body, 0, unroll=2)
+    lax.fori_loop(0, 64 // SLOT_GROUP, body, 0)
+    finish_messages(total, home, kinds, prod_weight, out_weight, read_weight, force_weight, out)
+
+
+def finish_messages(
+    total, home, kinds, prod_weight, out_weight, read_weight, force_weight, out
+):
     kind = jnp.where(iota((6, 256), 0).astype(f32) == kinds[...], 1.0, 0.0)
     paths = dot(prod_weight[...], kind, 0, 0, highest)
     p = [paths[128 * i : 128 * (i + 1)] for i in range(5)]
-    a0, a1 = total[0:128], [total[128 * m : 128 * (m + 1)] for m in (1, 2, 3)]
+    a0, *a1 = [
+        jnp.concatenate([total[row_of(q, c) : row_of(q, c) + 32] for q in range(4)], axis=0)
+        for c in range(4)
+    ]
     square = a1[0] * a1[0] + a1[1] * a1[1] + a1[2] * a1[2]
     b0 = (p[0] * a0 + p[1] * a0 * a0 + p[2] * square).astype(bf16)
     rows = [dot(read_weight[...].astype(f32), dot(out_weight[0], b0, 0, 0), 1, 0, highest)]
@@ -454,22 +524,26 @@
     send_up, charges = pl.pallas_call(
         up_kernel,
         out_shape=(whole((2, 512, 128), bf16), whole((8, 256))),
-        compiler_params=params(56),
+        compiler_params=params(),
         cost_estimate=cost(1 << 25, 0, 1 << 20),
         name="up",
     )(features, up_weight, charge_weight.T)
     moved_up = lax.all_gather(send_up, "yz", axis=0, tiled=True)
 
-    moments, basis, waves = pl.pallas_call(
+    moments, basis_high, basis_low, waves = pl.pallas_call(
         moment_kernel,
         out_shape=(
             whole((128, 16, 128), bf16),
-            whole((128 * SLABS, 512)),
+            whole((128 * SLABS, 512), bf16),
+            whole((128 * SLABS, 512), bf16),
             whole((40, 256)),
         ),
         in_specs=[SMEM] * 3 + [vmem] * 4,
-        scratch_shapes=[pltpu.VMEM((128, 16, 128), f32)],
-        compiler_params=params(56),
+        scratch_shapes=[
+            pltpu.VMEM((128 * SLABS, 512), f32),
+            pltpu.VMEM((128, 16, 128), f32),
+        ],
+        compiler_params=params(),
         cost_estimate=cost(1 << 30, 1 << 15, 3 << 20),
         name="moment",
     )(
@@ -482,39 +556,44 @@
         halo_list.reshape(1, 32),
     )
     sent = lax.all_to_all(moments, ("gx", "yz"), 0, 0, tiled=True)
-    coeffs = pl.pallas_call(
+    weights = pl.pallas_call(
+        count_kernel,
+        out_shape=whole((16, 128)),
+        in_specs=[SMEM, vmem],
+        compiler_params=params(),
+        cost_estimate=cost(1 << 28, 1 << 11, 1 << 18),
+        name="count",
+    )(place, wave_index)
+    coeffs, table, kinds, lists, home = pl.pallas_call(
         weight_kernel,
-        out_shape=whole((128, 8, 128)),
+        out_shape=(
+            whole((128, 8, 128)),
+            whole((16, 128)),
+            whole((1, 256)),
+            whole((4, 128), i32),
+            whole((6,), i32),
+        ),
         in_specs=[SMEM, vmem, vmem],
-        compiler_params=params(12),
+        out_specs=(vmem, vmem, vmem, vmem, SMEM),
+        scratch_shapes=[pltpu.VMEM((128, 16, 128), f32)],
+        compiler_params=params(),
         cost_estimate=cost(1 << 27, 1 << 11, 1 << 20),
         name="weight",
-    )(place, sent, wave_index)
+    )(place, sent, weights)
     coeffs = lax.all_to_all(coeffs, ("gx", "yz"), 0, 0, tiled=True)
 
-    hidden, offsets, kinds, home = pl.pallas_call(
+    hidden, offsets = pl.pallas_call(
         radial_kernel,
-        out_shape=(
-            whole((64, 64, 256), bf16),
-            whole((3, 64, 256)),
-            whole((1, 256)),
-            whole((2,), i32),
-        ),
-        in_specs=[SMEM] + [vmem] * 5,
-        out_specs=(vmem, vmem, vmem, SMEM),
-        scratch_shapes=[
-            pltpu.VMEM((128, 16, 128), f32),
-            pltpu.VMEM((64, 256), f32),
-            pltpu.VMEM((64, 256), f32),
-        ],
-        compiler_params=params(16),
+        out_shape=(whole((64, 64, 256), bf16), whole((3, 64, 256))),
+        scratch_shapes=[pltpu.VMEM((64, 256), f32), pltpu.VMEM((64, 256), f32)],
+        compiler_params=params(),
         cost_estimate=cost(1 << 32, 1 << 22, 4 << 20),
         name="radial",
-    )(place, sent, neighbours.T, neighbour_count.reshape(1, 256), radial_in, radial_mid)
-
+    )(table, neighbours.T, neighbour_count.reshape(1, 256), radial_in, radial_mid)
+
+    moved_up, hidden = lax.optimization_barrier((moved_up, hidden))
     nearby = [
-        pl.BlockSpec((1, 512, 128), lambda i, home: (home[0], 0, 0)),
-        pl.BlockSpec((1, 512, 128), lambda i, home: (home[1], 0, 0)),
+        pl.BlockSpec((1, 512, 128), lambda i, home, at=at: (home[at], 0, 0)) for at in range(6)
     ]
     send_halo = pl.pallas_call(
         halo_kernel,
@@ -522,64 +601,68 @@
         grid_spec=pltpu.PrefetchScalarGridSpec(
             num_scalar_prefetch=1,
             grid=(1,),
-            in_specs=nearby + [blocks_of((1, 32))],
+            in_specs=nearby[0:2] + [blocks_of((1, 32))],
             out_specs=blocks_of((32, 512)),
         ),
-        compiler_params=params(4),
+        compiler_params=params(),
         cost_estimate=cost(1 << 24, 0, 1 << 18),
         name="halo",
     )(home, moved_up, moved_up, halo_list.reshape(1, 32))
-    ghosts = []
-    for axis in ("gx", "yz"):
-        count = lax.axis_size(axis)
-        up = [(i, (i + 1) % count) for i in range(count)]
-        ghosts.append(lax.ppermute(send_halo, axis, up))
-        ghosts.append(lax.ppermute(send_halo, axis, [(b, a) for a, b in up]))
+    send_halo, late_hidden, late_up = lax.optimization_barrier((send_halo, hidden, moved_up))
+    near = pl.pallas_call(
+        near_kernel,
+        out_shape=whole((512, 384), bf16),
+        grid_spec=pltpu.PrefetchScalarGridSpec(
+            num_scalar_prefetch=1,
+            grid=(1,),
+            in_specs=nearby + [blocks_of((4, 128))],
+            out_specs=blocks_of((512, 384)),
+        ),
+        compiler_params=params(12),
+        cost_estimate=cost(1 << 28, 0, 1 << 20),
+        name="near",
+    )(home, *[late_up] * 6, lists)
+    radials = pl.pallas_call(
+        spread_kernel,
+        out_shape=whole((64, 512, 256), bf16),
+        in_specs=[vmem, vmem],
+        out_specs=vmem,
+        scratch_shapes=[pltpu.VMEM((512, 64), bf16)],
+        compiler_params=params(12),
+        cost_estimate=cost(6 << 30, 0, 18 << 20),
+        name="spread",
+    )(late_hidden, radial_out)
+    up = [(i, (i + 1) % 8) for i in range(8)]
+    left = lax.ppermute(send_halo, "gx", up)
+    right = lax.ppermute(send_halo, "gx", [(b, a) for a, b in up])
 
     part = pl.pallas_call(
         field_kernel,
         out_shape=whole((24, 256)),
         scratch_shapes=[pltpu.VMEM((384, 128 * SLABS), f32)],
-        compiler_params=params(16),
+        compiler_params=params(),
         cost_estimate=cost(1 << 31, 0, 3 << 20),
         name="field",
-    )(coeffs, basis, waves, features, skip_weight, field_weight, read_rows, force_row)
+    )(coeffs, basis_high, basis_low, waves, features, skip_weight, field_weight, read_rows, force_row)
 
     returned = pl.pallas_call(
         message_kernel,
         out_shape=whole((16, 24, 128)),
-        grid_spec=pltpu.PrefetchScalarGridSpec(
-            num_scalar_prefetch=1,
-            grid=(1,),
-            in_specs=nearby
-            + [blocks_of((32, 512))] * 4
-            + [
-                blocks_of((64, 256)),
-                blocks_of((3, 64, 256)),
-                blocks_of((64, 64, 256)),
-                blocks_of((1, 256)),
-                blocks_of((64, 512)),
-                blocks_of((6, 640)),
-                blocks_of((2, 128, 128)),
-                blocks_of((16, 128)),
-                blocks_of((1, 128)),
-            ],
-            out_specs=blocks_of((16, 24, 128)),
-            scratch_shapes=[pltpu.VMEM((512, 384), bf16), pltpu.VMEM((512, 256), f32)],
-        ),
-        compiler_params=params(16),
+        in_specs=[SMEM] + [vmem] * 11,
+        out_specs=vmem,
+        scratch_shapes=[pltpu.VMEM((512, 384), bf16), pltpu.VMEM((512, 256), f32)],
+        compiler_params=params(12),
         cost_estimate=cost(12 << 30, 0, 4 << 20),
         name="message",
     )(
         home,
-        moved_up,
-        moved_up,
-        *ghosts,
+        near,
+        left,
+        right,
         neighbours.T,
         offsets,
-        hidden,
+        radials,
         kinds,
-        radial_out,
         prod_weight,
         out_weight,
         read_rows,
@@ -590,7 +673,7 @@
         final_kernel,
         out_shape=(whole((3, 256)), whole((1, 256))),
         in_specs=[SMEM, vmem, vmem, vmem],
-        compiler_params=params(4),
+        compiler_params=params(),
         cost_estimate=cost(1 << 14, 1 << 12, 1 << 16),
         name="final",
     )(move_dest, returned, part, read_vector.reshape(1, 16))

time: 127 us -> 112 us (0.88)
  blocking collectives: 27.4 us -> 0 us
  waiting for transfers between devices: 5.53 us -> 17.5 us
  starting transfers between devices: 22 us -> 30 us
  local copies, waits for them, and re-layouts: 7.45 us -> 1.6 us
  Pallas kernels: 48.9 us -> 47.1 us
    all_to_all x1 -> x0, blocking collectives: 27.4 us -> none  [on_device(): sent = lax.all_to_all(moments, ('gx', 'yz'), 0, 0, tiled=True)]
    all_to_all x0 -> x1, waiting for transfers between devices: none -> 14 us  [on_device(): sent = lax.all_to_all(moments, ('gx', 'yz'), 0, 0, tiled=True)]
    all_to_all x0 -> x1, starting transfers between devices: none -> 11.5 us  [on_device(): sent = lax.all_to_all(moments, ('gx', 'yz'), 0, 0, tiled=True)]
    unnamed x46 -> x30, local copies, waits for them, and re-layouts: 7.45 us -> 1.6 us
    pallas_call x1, Pallas kernels: 10.9 us -> 6.22 us  [on_device(): pl.pallas_call(radial_kernel, out_shape=(whole((64, 64, 256), bf16), whol...]
    all_to_all x1, starting transfers between devices: 9.19 us -> 5.41 us  [on_device(): coeffs = lax.all_to_all(coeffs, ('gx', 'yz'), 0, 0, tiled=True)]
    pallas_call x1, Pallas kernels: 0.72 us -> 2.6 us  [on_device(): pl.pallas_call(halo_kernel, out_shape=whole((32, 512), bf16), grid_spec=p...]
    ppermute x4 -> x2, starting transfers between devices: 7.06 us -> 8 us  [the longest x1 8 us: on_device(): right = lax.ppermute(send_halo, 'gx', [(b, a) for a, b in up])]
  transfers between devices with their start and end apart: 7 -> 6, of which waited for: 2 -> 3; matrix products, arithmetic and copies ran while one was open for 0% -> 1% of each run, Pallas kernels for 36% -> 39%
where the time goes in v2:
time: 112 us; the launch traced here: 111 us
  Pallas kernels  47.1 us (42%)
  starting transfers between devices  30 us (27%)
  waiting for transfers between devices  17.5 us (16%)
  between operations  14.2 us (13%)
  local copies, waits for them, and re-layouts  1.6 us (1%)
    pallas_call x1, Pallas kernels, on_device(): pl.pallas_call(message_kernel, out_shape=whole((16, 24, 128)), in_specs=[...  15.6 us
    all_to_all x1, waiting for transfers between devices, on_device(): sent = lax.all_to_all(moments, ('gx', 'yz'), 0, 0, tiled=True)  14 us
    all_to_all x1, starting transfers between devices, on_device(): sent = lax.all_to_all(moments, ('gx', 'yz'), 0, 0, tiled=True)  11.5 us
    ppermute x1, starting transfers between devices, on_device(): right = lax.ppermute(send_halo, 'gx', [(b, a) for a, b in up])  8 us
    pallas_call x1, Pallas kernels, on_device(): pl.pallas_call(radial_kernel, out_shape=(whole((64, 64, 256), bf16), whol...  6.22 us
    pallas_call x1, Pallas kernels, on_device(): pl.pallas_call(spread_kernel, out_shape=whole((64, 512, 256), bf16), in_s...  5.56 us
    all_to_all x1, starting transfers between devices, on_device(): coeffs = lax.all_to_all(coeffs, ('gx', 'yz'), 0, 0, tiled=True)  5.41 us
    all_to_all x1, starting transfers between devices, on_device(): returned = lax.all_to_all(returned, 'yz', 0, 0, tiled=True)  5.04 us
  transfers between devices with their start and end apart: 6, of which 3 were waited for; matrix products, arithmetic and copies ran while one was open for 1% of the time, Pallas kernels for 39%

profile of v2, /device:TPU:1, one launch (start us, length us, event | category | flops | bytes accessed | tf_op | source)
XLA Modules:
  0.0 111.1 jit_solution(14917890453062861019)
XLA Ops:
  7.2 0.0 all-gather.2.cloned.1.call-start
  7.2 2.0 %up.2 = (bf16[2,512,128]{2,1,0:T(8,128)(2,1)}, f32[8,256]{1,0:T(8,128)}) custom-call(bf16[256,512]{1,0:T(8,128)(2,1)} %feat.3, bf16[2,128,128]{2,1,0:T(8,128)(2,1)} %up.3, bf16[8,128]{1,0:T(8,128)(2,1)} %bitcast.17), custom_call_target="tpu_custom_call" | custom-call | flops 33554432 | bytes 1048576 | tf_op jit(solution)/shard_map/up/pallas_call | solution.py:524
  9.2 0.0 all-gather.2.cloned.1.call-update
  9.3 0.6 pad_add_fusion.place
  9.9 3.4 %moment.1 = (bf16[128,16,128]{2,1,0:T(8,128)(2,1)}, bf16[768,512]{1,0:T(8,128)(2,1)}, bf16[768,512]{1,0:T(8,128)(2,1)}, f32[40,256]{1,0:T(8,128)}) custom-call(s32[2]{0:T(128)} %dest.3, s32[2]{0:T(128)} %slot.1, s32[2]{0:T(128)} %pad_add_fusion.place, f32[8,256]{1,0:T(8,128)} %get-tuple-element.22.charges_in, bf16[3,256]{1,0:T(4,128)(2,1)} %pos.1, ...), custom_call_target="tpu_custom_call" | custom-call | flops 1073741824 | bytes 3145728 | tf_op jit(solution)/shard_map/moment/pallas_call | solution.py:533
  13.3 11.5 %all-to-all-start = ((bf16[128,16,128]{2,1,0:T(8,128)(2,1)}), bf16[128,16,128]{2,1,0:T(8,128)(2,1)S(1)}, u32[]{:S(2)}, u32[]{:S(2)}) async-start(bf16[128,16,128]{2,1,0:T(8,128)(2,1)} %get-tuple-element.23), calls=%async_computation | async-start | bytes 1048576 | tf_op jit(solution)/shard_map/all_to_all | solution.py:558
  24.8 1.9 %count.1.weights = f32[16,128]{1,0:T(8,128)} custom-call(s32[2]{0:T(128)} %pad_add_fusion.place, s32[3,4096]{1,0:T(4,128)} %wave_index.1), custom_call_target="tpu_custom_call" | custom-call | flops 268435456 | bytes 262144 | tf_op jit(solution)/shard_map/count/pallas_call | solution.py:559
  26.7 14.0 %all-to-all-done.sent = bf16[128,16,128]{2,1,0:T(8,128)(2,1)S(1)} async-done(((bf16[128,16,128]{2,1,0:T(8,128)(2,1)}), bf16[128,16,128]{2,1,0:T(8,128)(2,1)S(1)}, u32[]{:S(2)}, u32[]{:S(2)}) %all-to-all-start) | async-done | bytes 524320 | tf_op jit(solution)/shard_map/all_to_all | solution.py:558
  40.7 0.8 copy-done.12
  41.5 2.8 %weight.1 = (f32[128,8,128]{2,1,0:T(8,128)}, f32[16,128]{1,0:T(8,128)}, f32[1,256]{1,0:T(1,128)}, s32[4,128]{1,0:T(4,128)}, s32[6]{0:T(128)}) custom-call(s32[2]{0:T(128)} %pad_add_fusion.place, bf16[128,16,128]{2,1,0:T(8,128)(2,1)} %copy-done.12, f32[16,128]{1,0:T(8,128)} %count.1.weights), custom_call_target="tpu_custom_call" | custom-call | flops 134217728 | bytes 1048576 | tf_op jit(solution)/shard_map/weight/pallas_call | solution.py:567
  44.4 5.4 %all-to-all-start.2 = ((f32[128,8,128]{2,1,0:T(8,128)}), f32[128,8,128]{2,1,0:T(8,128)S(1)}, u32[]{:S(2)}, u32[]{:S(2)}) async-start(f32[128,8,128]{2,1,0:T(8,128)} %get-tuple-element.36), calls=%async_computation.2 | async-start | bytes 1048576 | tf_op jit(solution)/shard_map/all_to_all | solution.py:583
  49.8 6.2 %radial.1 = (bf16[64,64,256]{2,1,0:T(8,128)(2,1)}, f32[3,64,256]{2,1,0:T(8,128)}) custom-call(f32[16,128]{1,0:T(8,128)} %get-tuple-element.26.table, s32[64,256]{1,0:T(8,128)} %bitcast.11, s32[1,256]{1,0:T(1,128)} %bitcast.22, bf16[8,64]{1,0:T(8,128)(2,1)} %radial_in.1, bf16[2,64,64]{2,1,0:T(8,128)(2,1)} %radial_mid.1), custom_call_target="tpu_custom_call" | custom-call | flops 4294967296 | bytes 4194304 | tf_op jit(solution)/shard_map/radial/pallas_call | solution.py:585
  56.0 1.3 %all-gather.2.cloned.1.call-done.first.second.own0.own1.low0.low1.high0.high1 = bf16[32,512,128]{2,1,0:T(8,128)(2,1)} async-done(((bf16[2,512,128]{2,1,0:T(8,128)(2,1)}), bf16[32,512,128]{2,1,0:T(8,128)(2,1)}) %all-gather.2.cloned.1.call-update) | async-done | bytes 4194320 | tf_op jit(solution)/shard_map/all_gather | solution.py:531
  57.3 2.6 %halo.1 = bf16[32,512]{1,0:T(8,128)(2,1)} custom-call(s32[6]{0:T(128)} %get-tuple-element.24.home, bf16[32,512,128]{2,1,0:T(8,128)(2,1)} %all-gather.2.cloned.1.call-done.first.second.own0.own1.low0.low1.high0.high1, bf16[32,512,128]{2,1,0:T(8,128)(2,1)} %all-gather.2.cloned.1.call-done.first.second.own0.own1.low0.low1.high0.high1, s32[1,32]{1,0:T(1,128)} %bitcast.19), custom_call_target="tpu_custom_call" | custom-call | flops 16777216 | bytes 262144 | tf_op jit(solution)/shard_map/halo/pallas_call | solution.py:598
  59.9 8.0 %collective-permute-start.1 = (bf16[32,512]{1,0:T(8,128)(2,1)}, bf16[32,512]{1,0:T(8,128)(2,1)S(1)}, u32[]{:S(2)}, u32[]{:S(2)}) collective-permute-start(bf16[32,512]{1,0:T(8,128)(2,1)} %halo.1), channel_id=1, source_target_pairs={{16,0},{32,16},{48,32},{64,48},{80,64},{96,80},{112,96},{0,112},{1... | collective-permute-start | bytes 98312 | tf_op jit(solution)/shard_map/ppermute | solution.py:637
  67.9 5.6 %spread.1.radials = bf16[64,512,256]{2,1,0:T(8,128)(2,1)S(1)} custom-call(bf16[64,64,256]{2,1,0:T(8,128)(2,1)S(1)} %copy-done.10, bf16[64,512]{1,0:T(8,128)(2,1)S(1)} %copy-done.3), custom_call_target="tpu_custom_call" | custom-call | flops 6442450944 | bytes 18874368 | tf_op jit(solution)/shard_map/spread/pallas_call | solution.py:625
  73.6 0.9 near.1
  74.5 0.0 copy-done.11
  74.6 15.6 %message.1 = f32[16,24,128]{2,1,0:T(8,128)} custom-call(s32[6]{0:T(128)S(1)} %copy-done.2, bf16[512,384]{1,0:T(8,128)(2,1)S(1)} %near.1, bf16[32,512]{1,0:T(8,128)(2,1)S(1)} %collective-permute-done.left, bf16[32,512]{1,0:T(8,128)(2,1)S(1)} %collective-permute-done.1.right, s32[64,256]{1,0:T(8,128)S(1)} %bitcast.12, f32[3,64,256]{2,1,0:T(8,128)S(1)} %copy-done.11, ...), custom_call_target="tpu_custom_call" | custom-call | flops 12884901888 | bytes 4194304 | tf_op jit(solution)/shard_map/message/pallas_call | solution.py:648
  90.1 5.0 %all-to-all-start.1 = ((f32[16,24,128]{2,1,0:T(8,128)}), f32[16,24,128]{2,1,0:T(8,128)S(1)}, u32[]{:S(2)}, u32[]{:S(2)}) async-start(f32[16,24,128]{2,1,0:T(8,128)} %message.1), calls=%async_computation.1 | async-start | bytes 393216 | tf_op jit(solution)/shard_map/all_to_all | solution.py:671
  95.2 4.5 %field.1.own = f32[24,256]{1,0:T(8,128)} custom-call(f32[128,8,128]{2,1,0:T(8,128)} %copy-done.14, bf16[768,512]{1,0:T(8,128)(2,1)} %get-tuple-element.37.basis_high, bf16[768,512]{1,0:T(8,128)(2,1)} %get-tuple-element.38.basis_low, f32[40,256]{1,0:T(8,128)} %get-tuple-element.39.waves, bf16[256,512]{1,0:T(8,128)(2,1)} %feat.3, ...), custom_call_target="tpu_custom_call" | custom-call | flops 2147483648 | bytes 3145728 | tf_op jit(solution)/shard_map/field/pallas_call | solution.py:639
  99.6 2.2 %all-to-all-done.1.sent = f32[16,24,128]{2,1,0:T(8,128)S(1)} async-done(((f32[16,24,128]{2,1,0:T(8,128)}), f32[16,24,128]{2,1,0:T(8,128)S(1)}, u32[]{:S(2)}, u32[]{:S(2)}) %all-to-all-start.1) | async-done | bytes 196640 | tf_op jit(solution)/shard_map/all_to_all | solution.py:671
  101.9 0.7 copy-done.13
  102.5 1.7 %final.1 = (f32[3,256]{1,0:T(4,128)}, f32[1,256]{1,0:T(1,128)}) custom-call(s32[2]{0:T(128)} %dest.3, f32[16,24,128]{2,1,0:T(8,128)} %copy-done.13, f32[24,256]{1,0:T(8,128)} %field.1.own, f32[1,16]{1,0:T(1,128)} %bitcast.20), custom_call_target="tpu_custom_call" | custom-call | flops 16384 | bytes 65536 | tf_op jit(solution)/shard_map/final/pallas_call | solution.py:672
  (31 shorter events, 0.1 us)
Async XLA Ops:
  7.2 50.1 %all-gather.2.cloned.1.call-start = ((), (), s32[]{:S(2)}) async-start(), calls=%async_computation.3 | async-start | bytes 4456448 | tf_op jit(solution)/shard_map/all_gather | solution.py:531
  13.3 27.4 %all-to-all-start = ((bf16[128,16,128]{2,1,0:T(8,128)(2,1)}), bf16[128,16,128]{2,1,0:T(8,128)(2,1)S(1)}, u32[]{:S(2)}, u32[]{:S(2)}) async-start(bf16[128,16,128]{2,1,0:T(8,128)(2,1)} %get-tuple-element.23), calls=%async_computation | async-start | bytes 1048576 | tf_op jit(solution)/shard_map/all_to_all | solution.py:558
  40.7 0.8 copy-start.12
  44.4 45.8 %all-to-all-start.2 = ((f32[128,8,128]{2,1,0:T(8,128)}), f32[128,8,128]{2,1,0:T(8,128)S(1)}, u32[]{:S(2)}, u32[]{:S(2)}) async-start(f32[128,8,128]{2,1,0:T(8,128)} %get-tuple-element.36), calls=%async_computation.2 | async-start | bytes 1048576 | tf_op jit(solution)/shard_map/all_to_all | solution.py:583
  57.3 10.6 %copy-start.3 = (bf16[64,512]{1,0:T(8,128)(2,1)S(1)}, bf16[64,512]{1,0:T(8,128)(2,1)}, u32[]{:S(2)}) copy-start(bf16[64,512]{1,0:T(8,128)(2,1)} %radial_out.1) | copy-start | bytes 196612
  57.3 10.6 %copy-start.10 = (bf16[64,64,256]{2,1,0:T(8,128)(2,1)S(1)}, bf16[64,64,256]{2,1,0:T(8,128)(2,1)}, u32[]{:S(2)}) copy-start(bf16[64,64,256]{2,1,0:T(8,128)(2,1)} %get-tuple-element.34.hidden) | copy-start | bytes 6291460
  59.9 13.6 %copy-start = (bf16[32,512,128]{2,1,0:T(8,128)(2,1)S(1)}, bf16[32,512,128]{2,1,0:T(8,128)(2,1)}, u32[]{:S(2)}) copy-start(bf16[32,512,128]{2,1,0:T(8,128)(2,1)} %all-gather.2.cloned.1.call-done.first.second.own0.own1.low0.low1.high0.high1) | copy-start | bytes 12582916
  59.9 13.6 %copy-start.1 = (s32[4,128]{1,0:T(4,128)S(1)}, s32[4,128]{1,0:T(4,128)}, u32[]{:S(2)}) copy-start(s32[4,128]{1,0:T(4,128)} %get-tuple-element.31.lists) | copy-start | bytes 6148
  59.9 13.6 %copy-start.2 = (s32[6]{0:T(128)S(1)}, s32[6]{0:T(128)}, u32[]{:S(2)}) copy-start(s32[6]{0:T(128)} %get-tuple-element.24.home) | copy-start | bytes 76
  59.9 14.6 %collective-permute-start.1 = (bf16[32,512]{1,0:T(8,128)(2,1)}, bf16[32,512]{1,0:T(8,128)(2,1)S(1)}, u32[]{:S(2)}, u32[]{:S(2)}) collective-permute-start(bf16[32,512]{1,0:T(8,128)(2,1)} %halo.1), channel_id=1, source_target_pairs={{16,0},{32,16},{48,32},{64,48},{80,64},{96,80},{112,96},{0,112},{1... | collective-permute-start | bytes 98312 | tf_op jit(solution)/shard_map/ppermute | solution.py:637
  67.9 6.6 %collective-permute-start = (bf16[32,512]{1,0:T(8,128)(2,1)}, bf16[32,512]{1,0:T(8,128)(2,1)S(1)}, u32[]{:S(2)}, u32[]{:S(2)}) collective-permute-start(bf16[32,512]{1,0:T(8,128)(2,1)} %halo.1), channel_id=1, source_target_pairs={{0,16},{16,32},{32,48},{48,64},{64,80},{80,96},{96,112},{112,0},{1... | collective-permute-start | bytes 98312 | tf_op jit(solution)/shard_map/ppermute | solution.py:636
  73.5 1.0 copy-start.4
  73.5 1.0 copy-start.5
  73.5 1.0 copy-start.6
  73.5 1.0 copy-start.7
  73.5 1.0 copy-start.8
  73.6 1.0 copy-start.9
  73.6 1.0 copy-start.11
  90.1 5.0 %copy-start.14 = (f32[128,8,128]{2,1,0:T(8,128)}, f32[128,8,128]{2,1,0:T(8,128)S(1)}, u32[]{:S(2)}) copy-start(f32[128,8,128]{2,1,0:T(8,128)S(1)} %all-to-all-done.2.coeffs) | copy-start | bytes 1572868
  90.1 11.7 %all-to-all-start.1 = ((f32[16,24,128]{2,1,0:T(8,128)}), f32[16,24,128]{2,1,0:T(8,128)S(1)}, u32[]{:S(2)}, u32[]{:S(2)}) async-start(f32[16,24,128]{2,1,0:T(8,128)} %message.1), calls=%async_computation.1 | async-start | bytes 393216 | tf_op jit(solution)/shard_map/all_to_all | solution.py:671
  101.9 0.7 copy-start.13
Sparse Core Ops, SparseCore 0:
  9.7 47.5 all-gather.1

commit v3 on v2

--- a/solution.py
+++ b/solution.py
@@ -16,7 +16,7 @@
 
 NX, NY, NZ = 16, 32, 2
 SLABS = 2 * NZ + 2
-RADIAL_GROUP, SLOT_GROUP = 16, 8
+RADIAL_GROUP, SLOT_GROUP = 16, 16
 
 
 def row_of(chunk, component):
@@ -74,9 +74,9 @@
 
 
 def moment_kernel(
-    dest, slot, place, charges_in, pos, species, halo, out, basis_high, basis_low, waves, basis, stage
+    dest, slot, charges_in, pos, species, halo, out, basis_high, basis_low, waves, basis, stage
 ):
-    gx = place[0].astype(f32)
+    gx = lax.axis_index("gx").astype(f32)
     charges = charges_in[...]
     lane = iota((1, 256), 1)
     second = lane >= 128
@@ -134,8 +134,8 @@
     out[...] = stage[...].astype(bf16)
 
 
-def count_kernel(place, wave_index, out):
-    own_x = (place[0] * 16 + place[1]) // 8 + 1
+def count_kernel(wave_index, out):
+    own_x = (lax.axis_index("gx") * 16 + lax.axis_index("yz")) // 8 + 1
     kx, ky, kz = wave_index[0:1, :], wave_index[1:2, :], wave_index[2:3, :]
     count = kx.shape[1]
     ours = kx == own_x
@@ -165,7 +165,7 @@
 
 
 def weight_kernel(
-    place, sent, weights, out, table_out, kinds_out, lists_out, home_out, stage
+    sent, weights, out, table_out, kinds_out, lists_out, home_out, stage
 ):
     stage[...] = sent[...].astype(f32)
     total = jnp.sum(stage[:, 0:8, :], axis=0)
@@ -177,7 +177,7 @@
     swapped = jnp.where((group == 0) | (group == 3), -swapped, swapped)
     coefficient = total * weights[0:8] + swapped * weights[8:16]
     out[...] = jnp.broadcast_to(coefficient[None], out.shape)
-    gx, yz = place[0], place[1]
+    gx, yz = lax.axis_index("gx"), lax.axis_index("yz")
     targets = [
         (gx, yz),
         ((gx + 7) % 8, yz),
@@ -456,7 +456,10 @@
     total, home, kinds, prod_weight, out_weight, read_weight, force_weight, out
 ):
     kind = jnp.where(iota((6, 256), 0).astype(f32) == kinds[...], 1.0, 0.0)
-    paths = dot(prod_weight[...], kind, 0, 0, highest)
+    high, mid = halves(prod_weight[...])
+    low = (prod_weight[...] - high.astype(f32) - mid.astype(f32)).astype(bf16)
+    kind = kind.astype(bf16)
+    paths = dot(high, kind, 0, 0) + (dot(mid, kind, 0, 0) + dot(low, kind, 0, 0))
     p = [paths[128 * i : 128 * (i + 1)] for i in range(5)]
     a0, *a1 = [
         jnp.concatenate([total[row_of(q, c) : row_of(q, c) + 32] for q in range(4)], axis=0)
@@ -516,7 +519,6 @@
     read_vector,
     force_weight,
 ):
-    place = jnp.stack([lax.axis_index("gx"), lax.axis_index("yz")]).astype(i32)
     force_row = force_weight.reshape(1, 128)
     vmem = pl.BlockSpec(memory_space=pltpu.VMEM)
 
@@ -538,18 +540,17 @@
             whole((128 * SLABS, 512), bf16),
             whole((40, 256)),
         ),
-        in_specs=[SMEM] * 3 + [vmem] * 4,
+        in_specs=[SMEM] * 2 + [vmem] * 4,
         scratch_shapes=[
             pltpu.VMEM((128 * SLABS, 512), f32),
             pltpu.VMEM((128, 16, 128), f32),
         ],
-        compiler_params=params(),
+        compiler_params=params(20),
         cost_estimate=cost(1 << 30, 1 << 15, 3 << 20),
         name="moment",
     )(
         move_dest,
         move_slot,
-        place,
         charges,
         positions,
         species.reshape(1, 256),
@@ -559,11 +560,10 @@
     weights = pl.pallas_call(
         count_kernel,
         out_shape=whole((16, 128)),
-        in_specs=[SMEM, vmem],
-        compiler_params=params(),
+        compiler_params=params(12),
         cost_estimate=cost(1 << 28, 1 << 11, 1 << 18),
         name="count",
-    )(place, wave_index)
+    )(wave_index)
     coeffs, table, kinds, lists, home = pl.pallas_call(
         weight_kernel,
         out_shape=(
@@ -573,20 +573,20 @@
             whole((4, 128), i32),
             whole((6,), i32),
         ),
-        in_specs=[SMEM, vmem, vmem],
+        in_specs=[vmem, vmem],
         out_specs=(vmem, vmem, vmem, vmem, SMEM),
         scratch_shapes=[pltpu.VMEM((128, 16, 128), f32)],
-        compiler_params=params(),
+        compiler_params=params(12),
         cost_estimate=cost(1 << 27, 1 << 11, 1 << 20),
         name="weight",
-    )(place, sent, weights)
+    )(sent, weights)
     coeffs = lax.all_to_all(coeffs, ("gx", "yz"), 0, 0, tiled=True)
 
     hidden, offsets = pl.pallas_call(
         radial_kernel,
         out_shape=(whole((64, 64, 256), bf16), whole((3, 64, 256))),
         scratch_shapes=[pltpu.VMEM((64, 256), f32), pltpu.VMEM((64, 256), f32)],
-        compiler_params=params(),
+        compiler_params=params(20),
         cost_estimate=cost(1 << 32, 1 << 22, 4 << 20),
         name="radial",
     )(table, neighbours.T, neighbour_count.reshape(1, 256), radial_in, radial_mid)
@@ -604,7 +604,7 @@
             in_specs=nearby[0:2] + [blocks_of((1, 32))],
             out_specs=blocks_of((32, 512)),
         ),
-        compiler_params=params(),
+        compiler_params=params(61),
         cost_estimate=cost(1 << 24, 0, 1 << 18),
         name="halo",
     )(home, moved_up, moved_up, halo_list.reshape(1, 32))
@@ -640,7 +640,7 @@
         field_kernel,
         out_shape=whole((24, 256)),
         scratch_shapes=[pltpu.VMEM((384, 128 * SLABS), f32)],
-        compiler_params=params(),
+        compiler_params=params(20),
         cost_estimate=cost(1 << 31, 0, 3 << 20),
         name="field",
     )(coeffs, basis_high, basis_low, waves, features, skip_weight, field_weight, read_rows, force_row)
@@ -673,7 +673,7 @@
         final_kernel,
         out_shape=(whole((3, 256)), whole((1, 256))),
         in_specs=[SMEM, vmem, vmem, vmem],
-        compiler_params=params(),
+        compiler_params=params(12),
         cost_estimate=cost(1 << 14, 1 << 12, 1 << 16),
         name="final",
     )(move_dest, returned, part, read_vector.reshape(1, 16))

time: 112 us -> 109 us (0.973)
  Pallas kernels: 47.1 us -> 38.4 us
  local copies, waits for them, and re-layouts: 1.6 us -> 6.41 us
  waiting for transfers between devices: 17.5 us -> 20.6 us
    unnamed x30 -> x56, local copies, waits for them, and re-layouts: 1.6 us -> 6.41 us
    ppermute x1, starting transfers between devices: 8 us -> 5.69 us  [on_device(): right = lax.ppermute(send_halo, 'gx', [(b, a) for a, b in up])]
    pallas_call x1, Pallas kernels: 6.22 us -> 3.96 us  [on_device(): pl.pallas_call(radial_kernel, out_shape=(whole((64, 64, 256), bf16), whol...]
    pallas_call x1, Pallas kernels: 4.46 us -> 2.21 us  [on_device(): pl.pallas_call(field_kernel, out_shape=whole((24, 256)), scratch_shapes=[...]
    all_to_all x1, waiting for transfers between devices: 2.21 us -> 4.43 us  [on_device(): returned = lax.all_to_all(returned, 'yz', 0, 0, tiled=True)]
    all_to_all x1, waiting for transfers between devices: 14 us -> 15.5 us  [on_device(): sent = lax.all_to_all(moments, ('gx', 'yz'), 0, 0, tiled=True)]
    pallas_call x1, Pallas kernels: 1.88 us -> 0.43 us  [on_device(): pl.pallas_call(count_kernel, out_shape=whole((16, 128)), compiler_params=...]
    all_to_all x1, starting transfers between devices: 5.04 us -> 6.37 us  [on_device(): returned = lax.all_to_all(returned, 'yz', 0, 0, tiled=True)]
  transfers between devices with their start and end apart: 6 -> 6, of which waited for: 3 -> 3; matrix products, arithmetic and copies ran while one was open for 1% -> 0% of each run, Pallas kernels for 39% -> 32%
where the time goes in v3:
time: 109 us
  Pallas kernels  38.4 us (35%)
  starting transfers between devices  29 us (27%)
  waiting for transfers between devices  20.6 us (19%)
  between operations  14.3 us (13%)
  local copies, waits for them, and re-layouts  6.41 us (6%)
    all_to_all x1, waiting for transfers between devices, on_device(): sent = lax.all_to_all(moments, ('gx', 'yz'), 0, 0, tiled=True)  15.5 us
    pallas_call x1, Pallas kernels, on_device(): pl.pallas_call(message_kernel, out_shape=whole((16, 24, 128)), in_specs=[...  15.1 us
    all_to_all x1, starting transfers between devices, on_device(): sent = lax.all_to_all(moments, ('gx', 'yz'), 0, 0, tiled=True)  11.5 us
    unnamed x56, local copies, waits for them, and re-layouts  6.41 us
    all_to_all x1, starting transfers between devices, on_device(): returned = lax.all_to_all(returned, 'yz', 0, 0, tiled=True)  6.37 us
    ppermute x1, starting transfers between devices, on_device(): right = lax.ppermute(send_halo, 'gx', [(b, a) for a, b in up])  5.69 us
    all_to_all x1, starting transfers between devices, on_device(): coeffs = lax.all_to_all(coeffs, ('gx', 'yz'), 0, 0, tiled=True)  5.39 us
    pallas_call x1, Pallas kernels, on_device(): pl.pallas_call(spread_kernel, out_shape=whole((64, 512, 256), bf16), in_s...  5.02 us
  transfers between devices with their start and end apart: 6, of which 3 were waited for; matrix products, arithmetic and copies ran while one was open for 0% of the time, Pallas kernels for 32%

profile of v3, /device:TPU:1, one launch (start us, length us, event | category | flops | bytes accessed | tf_op | source)
XLA Modules:
  0.0 108.7 jit_solution(1721331834476639051)
XLA Ops:
  7.3 2.0 %up.2 = (bf16[2,512,128]{2,1,0:T(8,128)(2,1)}, f32[8,256]{1,0:T(8,128)}) custom-call(bf16[256,512]{1,0:T(8,128)(2,1)} %feat.3, bf16[2,128,128]{2,1,0:T(8,128)(2,1)} %up.3, bf16[8,128]{1,0:T(8,128)(2,1)} %bitcast.20), custom_call_target="tpu_custom_call" | custom-call | flops 33554432 | bytes 1048576 | tf_op jit(solution)/shard_map/up/pallas_call | solution.py:526
  9.3 0.6 copy-done.4
  10.0 0.7 copy-done.5
  10.7 0.7 copy-done.15
  11.3 0.7 copy-done.18
  12.0 0.7 copy-done.20
  12.7 0.7 copy-done.22
  13.4 3.1 %moment.1 = (bf16[128,16,128]{2,1,0:T(8,128)(2,1)}, bf16[768,512]{1,0:T(8,128)(2,1)S(1)}, bf16[768,512]{1,0:T(8,128)(2,1)S(1)}, f32[40,256]{1,0:T(8,128)S(1)}) custom-call(s32[2]{0:T(128)S(1)} %copy-done.5, s32[2]{0:T(128)S(1)} %copy-done.22, f32[8,256]{1,0:T(8,128)S(1)} %copy-done.15, bf16[3,256]{1,0:T(4,128)(2,1)S(1)} %copy-done.18, ...), custom_call_target="tpu_custom_call" | custom-call | flops 1073741824 | bytes 3145728 | tf_op jit(solution)/shard_map/moment/pallas_call | solution.py:535
  16.5 0.9 copy-done.24
  17.4 0.9 copy-done.26
  18.3 11.5 %all-to-all-start = ((bf16[128,16,128]{2,1,0:T(8,128)(2,1)}), bf16[128,16,128]{2,1,0:T(8,128)(2,1)S(1)}, u32[]{:S(2)}, u32[]{:S(2)}) async-start(bf16[128,16,128]{2,1,0:T(8,128)(2,1)} %get-tuple-element.23), calls=%async_computation | async-start | bytes 1048576 | tf_op jit(solution)/shard_map/all_to_all | solution.py:559
  30.3 15.5 %all-to-all-done.sent = bf16[128,16,128]{2,1,0:T(8,128)(2,1)S(1)} async-done(((bf16[128,16,128]{2,1,0:T(8,128)(2,1)}), bf16[128,16,128]{2,1,0:T(8,128)(2,1)S(1)}, u32[]{:S(2)}, u32[]{:S(2)}) %all-to-all-start) | async-done | bytes 524320 | tf_op jit(solution)/shard_map/all_to_all | solution.py:559
  45.7 1.7 %weight.1 = (f32[128,8,128]{2,1,0:T(8,128)}, f32[16,128]{1,0:T(8,128)S(1)}, f32[1,256]{1,0:T(1,128)S(1)}, s32[4,128]{1,0:T(4,128)S(1)}, s32[6]{0:T(128)S(1)}) custom-call(bf16[128,16,128]{2,1,0:T(8,128)(2,1)S(1)} %all-to-all-done.sent, f32[16,128]{1,0:T(8,128)S(1)} %count.1.weights), custom_call_target="tpu_custom_call" | custom-call | flops 134217728 | bytes 1048576 | tf_op jit(solution)/shard_map/weight/pallas_call | solution.py:567
  48.0 5.4 %all-to-all-start.2 = ((f32[128,8,128]{2,1,0:T(8,128)}), f32[128,8,128]{2,1,0:T(8,128)S(1)}, u32[]{:S(2)}, u32[]{:S(2)}) async-start(f32[128,8,128]{2,1,0:T(8,128)} %get-tuple-element.36), calls=%async_computation.2 | async-start | bytes 1048576 | tf_op jit(solution)/shard_map/all_to_all | solution.py:583
  53.4 4.0 %radial.1 = (bf16[64,64,256]{2,1,0:T(8,128)(2,1)S(1)}, f32[3,64,256]{2,1,0:T(8,128)S(1)}) custom-call(f32[16,128]{1,0:T(8,128)S(1)} %get-tuple-element.26.table, s32[64,256]{1,0:T(8,128)S(1)} %bitcast.12, s32[1,256]{1,0:T(1,128)S(1)} %bitcast.17, bf16[8,64]{1,0:T(8,128)(2,1)S(1)} %copy-done.19, bf16[2,64,64]{2,1,0:T(8,128)(2,1)S(1)} %copy-done.13), custom_call_target="tpu_custom_call" | custom-call | flops 4294967296 | bytes 4194304 | tf_op jit(solution)/shard_map/radial/pallas_call | solution.py:585
  57.5 2.6 %halo.1 = bf16[32,512]{1,0:T(8,128)(2,1)} custom-call(s32[6]{0:T(128)} %copy-done.2, bf16[32,512,128]{2,1,0:T(8,128)(2,1)} %all-gather.2.cloned.1.call-done.first.second.own0.own1.low0.low1.high0.high1, bf16[32,512,128]{2,1,0:T(8,128)(2,1)} %all-gather.2.cloned.1.call-done.first.second.own0.own1.low0.low1.high0.high1, s32[1,32]{1,0:T(1,128)} %bitcast.9), custom_call_target="tpu_custom_call" | custom-call | flops 16777216 | bytes 262144 | tf_op jit(solution)/shard_map/halo/pallas_call | solution.py:598
  60.0 5.7 %collective-permute-start.1 = (bf16[32,512]{1,0:T(8,128)(2,1)}, bf16[32,512]{1,0:T(8,128)(2,1)S(1)}, u32[]{:S(2)}, u32[]{:S(2)}) collective-permute-start(bf16[32,512]{1,0:T(8,128)(2,1)} %halo.1), channel_id=1, source_target_pairs={{16,0},{32,16},{48,32},{64,48},{80,64},{96,80},{112,96},{0,112},{1... | collective-permute-start | bytes 98312 | tf_op jit(solution)/shard_map/ppermute | solution.py:637
  65.7 5.0 %spread.1.radials = bf16[64,512,256]{2,1,0:T(8,128)(2,1)S(1)} custom-call(bf16[64,64,256]{2,1,0:T(8,128)(2,1)S(1)} %get-tuple-element.34.hidden, bf16[64,512]{1,0:T(8,128)(2,1)S(1)} %copy-done.9), custom_call_target="tpu_custom_call" | custom-call | flops 6442450944 | bytes 18874368 | tf_op jit(solution)/shard_map/spread/pallas_call | solution.py:625
  70.8 0.9 near.1
  72.4 15.1 %message.1 = f32[16,24,128]{2,1,0:T(8,128)} custom-call(s32[6]{0:T(128)S(1)} %copy-done.3, bf16[512,384]{1,0:T(8,128)(2,1)S(1)} %near.1, bf16[32,512]{1,0:T(8,128)(2,1)S(1)} %collective-permute-done.left, bf16[32,512]{1,0:T(8,128)(2,1)S(1)} %collective-permute-done.1.right, s32[64,256]{1,0:T(8,128)S(1)} %bitcast.13, ...), custom_call_target="tpu_custom_call" | custom-call | flops 12884901888 | bytes 4194304 | tf_op jit(solution)/shard_map/message/pallas_call | solution.py:648
  87.5 6.4 %all-to-all-start.1 = ((f32[16,24,128]{2,1,0:T(8,128)}), f32[16,24,128]{2,1,0:T(8,128)S(1)}, u32[]{:S(2)}, u32[]{:S(2)}) async-start(f32[16,24,128]{2,1,0:T(8,128)} %message.1), calls=%async_computation.1 | async-start | bytes 393216 | tf_op jit(solution)/shard_map/all_to_all | solution.py:671
  93.9 2.2 %field.1.own = f32[24,256]{1,0:T(8,128)S(1)} custom-call(f32[128,8,128]{2,1,0:T(8,128)S(1)} %all-to-all-done.2.coeffs, bf16[768,512]{1,0:T(8,128)(2,1)S(1)} %copy-done.25, bf16[768,512]{1,0:T(8,128)(2,1)S(1)} %copy-done.27, f32[40,256]{1,0:T(8,128)S(1)} %get-tuple-element.39.waves, bf16[256,512]{1,0:T(8,128)(2,1)S(1)} %copy-done.1, ...), custom_call_target="tpu_custom_call" | custom-call | flops 2147483648 | bytes 3145728 | tf_op jit(solution)/shard_map/field/pallas_call | solution.py:639
  96.1 4.4 %all-to-all-done.1.sent = f32[16,24,128]{2,1,0:T(8,128)S(1)} async-done(((f32[16,24,128]{2,1,0:T(8,128)}), f32[16,24,128]{2,1,0:T(8,128)S(1)}, u32[]{:S(2)}, u32[]{:S(2)}) %all-to-all-start.1) | async-done | bytes 196640 | tf_op jit(solution)/shard_map/all_to_all | solution.py:671
  100.5 1.3 %final.1 = (f32[3,256]{1,0:T(4,128)}, f32[1,256]{1,0:T(1,128)}) custom-call(s32[2]{0:T(128)S(1)} %copy-done.6, f32[16,24,128]{2,1,0:T(8,128)S(1)} %all-to-all-done.1.sent, f32[24,256]{1,0:T(8,128)S(1)} %field.1.own, f32[1,16]{1,0:T(1,128)S(1)} %bitcast.11), custom_call_target="tpu_custom_call" | custom-call | flops 16384 | bytes 65536 | tf_op jit(solution)/shard_map/final/pallas_call | solution.py:672
  (56 shorter events, 1.7 us)
Async XLA Ops:
  7.2 22.6 %copy-start.8 = (s32[3,4096]{1,0:T(4,128)S(1)}, s32[3,4096]{1,0:T(4,128)}, u32[]{:S(2)}) copy-start(s32[3,4096]{1,0:T(4,128)} %wave_index.1) | copy-start | bytes 147460
  7.2 46.2 %copy-start.13 = (bf16[2,64,64]{2,1,0:T(8,128)(2,1)S(1)}, bf16[2,64,64]{2,1,0:T(8,128)(2,1)}, u32[]{:S(2)}) copy-start(bf16[2,64,64]{2,1,0:T(8,128)(2,1)} %radial_mid.1) | copy-start | bytes 49156
  7.2 46.2 %copy-start.19 = (bf16[8,64]{1,0:T(8,128)(2,1)S(1)}, bf16[8,64]{1,0:T(8,128)(2,1)}, u32[]{:S(2)}) copy-start(bf16[8,64]{1,0:T(8,128)(2,1)} %radial_in.1) | copy-start | bytes 3076
  7.2 46.2 %copy-start.21 = (s32[256]{0:T(256)S(1)}, s32[256]{0:T(256)}, u32[]{:S(2)}) copy-start(s32[256]{0:T(256)} %param.28) | copy-start | bytes 3076
  7.2 46.2 %copy-start.10 = (s32[256,64]{0,1:T(8,128)S(1)}, s32[256,64]{0,1:T(8,128)}, u32[]{:S(2)}) copy-start(s32[256,64]{0,1:T(8,128)} %param.27) | copy-start | bytes 196612
  7.2 50.2 %all-gather.2.cloned.1.call-start = ((), (), s32[]{:S(2)}) async-start(), calls=%async_computation.3 | async-start | bytes 4456448 | tf_op jit(solution)/shard_map/all_gather | solution.py:533
  18.3 27.4 %all-to-all-start = ((bf16[128,16,128]{2,1,0:T(8,128)(2,1)}), bf16[128,16,128]{2,1,0:T(8,128)(2,1)S(1)}, u32[]{:S(2)}, u32[]{:S(2)}) async-start(bf16[128,16,128]{2,1,0:T(8,128)(2,1)} %get-tuple-element.23), calls=%async_computation | async-start | bytes 1048576 | tf_op jit(solution)/shard_map/all_to_all | solution.py:559
  48.0 39.5 %all-to-all-start.2 = ((f32[128,8,128]{2,1,0:T(8,128)}), f32[128,8,128]{2,1,0:T(8,128)S(1)}, u32[]{:S(2)}, u32[]{:S(2)}) async-start(f32[128,8,128]{2,1,0:T(8,128)} %get-tuple-element.36), calls=%async_computation.2 | async-start | bytes 1048576 | tf_op jit(solution)/shard_map/all_to_all | solution.py:583
  57.4 8.3 %copy-start.9 = (bf16[64,512]{1,0:T(8,128)(2,1)S(1)}, bf16[64,512]{1,0:T(8,128)(2,1)}, u32[]{:S(2)}) copy-start(bf16[64,512]{1,0:T(8,128)(2,1)} %radial_out.1) | copy-start | bytes 196612
  60.0 10.7 %copy-start = (bf16[32,512,128]{2,1,0:T(8,128)(2,1)S(1)}, bf16[32,512,128]{2,1,0:T(8,128)(2,1)}, u32[]{:S(2)}) copy-start(bf16[32,512,128]{2,1,0:T(8,128)(2,1)} %all-gather.2.cloned.1.call-done.first.second.own0.own1.low0.low1.high0.high1) | copy-start | bytes 12582916
  60.0 10.7 %copy-start.3 = (s32[6]{0:T(128)S(1)}, s32[6]{0:T(128)}, u32[]{:S(2)}) copy-start(s32[6]{0:T(128)} %copy-done.2) | copy-start | bytes 76
  60.0 11.7 %collective-permute-start.1 = (bf16[32,512]{1,0:T(8,128)(2,1)}, bf16[32,512]{1,0:T(8,128)(2,1)S(1)}, u32[]{:S(2)}, u32[]{:S(2)}) collective-permute-start(bf16[32,512]{1,0:T(8,128)(2,1)} %halo.1), channel_id=1, source_target_pairs={{16,0},{32,16},{48,32},{64,48},{80,64},{96,80},{112,96},{0,112},{1... | collective-permute-start | bytes 98312 | tf_op jit(solution)/shard_map/ppermute | solution.py:637
  65.7 6.6 %collective-permute-start = (bf16[32,512]{1,0:T(8,128)(2,1)}, bf16[32,512]{1,0:T(8,128)(2,1)S(1)}, u32[]{:S(2)}, u32[]{:S(2)}) collective-permute-start(bf16[32,512]{1,0:T(8,128)(2,1)} %halo.1), channel_id=1, source_target_pairs={{0,16},{16,32},{32,48},{48,64},{64,80},{80,96},{96,112},{112,0},{1... | collective-permute-start | bytes 98312 | tf_op jit(solution)/shard_map/ppermute | solution.py:636
  70.8 1.5 %copy-start.11 = (bf16[2,128,128]{2,1,0:T(8,128)(2,1)S(1)}, bf16[2,128,128]{2,1,0:T(8,128)(2,1)}, u32[]{:S(2)}) copy-start(bf16[2,128,128]{2,1,0:T(8,128)(2,1)} %out_weight.1) | copy-start | bytes 196612
  70.8 1.5 %copy-start.14 = (f32[6,640]{1,0:T(8,128)S(1)}, f32[6,640]{1,0:T(8,128)}, u32[]{:S(2)}) copy-start(f32[6,640]{1,0:T(8,128)} %prod_weight.1) | copy-start | bytes 46084
  70.8 1.5 %copy-start.16 = (bf16[128,16]{0,1:T(8,128)(2,1)S(1)}, bf16[128,16]{0,1:T(8,128)(2,1)}, u32[]{:S(2)}) copy-start(bf16[128,16]{0,1:T(8,128)(2,1)} %param.39) | copy-start | bytes 12292
  72.3 21.5 %copy-start.1 = (bf16[256,512]{1,0:T(8,128)(2,1)S(1)}, bf16[256,512]{1,0:T(8,128)(2,1)}, u32[]{:S(2)}) copy-start(bf16[256,512]{1,0:T(8,128)(2,1)} %feat.3) | copy-start | bytes 786436
  72.4 21.5 %copy-start.12 = (bf16[2,128,128]{2,1,0:T(8,128)(2,1)S(1)}, bf16[2,128,128]{2,1,0:T(8,128)(2,1)}, u32[]{:S(2)}) copy-start(bf16[2,128,128]{2,1,0:T(8,128)(2,1)} %skip_weight.1) | copy-start | bytes 196612
  72.4 21.5 %copy-start.17 = (f32[8,128]{1,0:T(8,128)S(1)}, f32[8,128]{1,0:T(8,128)}, u32[]{:S(2)}) copy-start(f32[8,128]{1,0:T(8,128)} %field_weight.1) | copy-start | bytes 12292
  72.4 21.5 %copy-start.25 = (bf16[768,512]{1,0:T(8,128)(2,1)S(1)}, bf16[768,512]{1,0:T(8,128)(2,1)}, u32[]{:S(2)}) copy-start(bf16[768,512]{1,0:T(8,128)(2,1)} %copy-done.24) | copy-start | bytes 2359300
  72.4 21.5 %copy-start.27 = (bf16[768,512]{1,0:T(8,128)(2,1)S(1)}, bf16[768,512]{1,0:T(8,128)(2,1)}, u32[]{:S(2)}) copy-start(bf16[768,512]{1,0:T(8,128)(2,1)} %copy-done.26) | copy-start | bytes 2359300
  87.5 13.1 %copy-start.6 = (s32[2]{0:T(128)S(1)}, s32[2]{0:T(128)}, u32[]{:S(2)}) copy-start(s32[2]{0:T(128)} %dest.3) | copy-start | bytes 28
  87.5 13.1 %copy-start.7 = (f32[16]{0:T(128)S(1)}, f32[16]{0:T(128)}, u32[]{:S(2)}) copy-start(f32[16]{0:T(128)} %param.40) | copy-start | bytes 196
  87.5 13.1 %all-to-all-start.1 = ((f32[16,24,128]{2,1,0:T(8,128)}), f32[16,24,128]{2,1,0:T(8,128)S(1)}, u32[]{:S(2)}, u32[]{:S(2)}) async-start(f32[16,24,128]{2,1,0:T(8,128)} %message.1), calls=%async_computation.1 | async-start | bytes 393216 | tf_op jit(solution)/shard_map/all_to_all | solution.py:671
  (10 other events, 7.8 us)
Sparse Core Ops, SparseCore 0:
  9.8 46.2 all-gather.1

commit v4 on v3

--- a/solution.py
+++ b/solution.py
@@ -410,8 +410,10 @@
     total,
 ):
     table[...] = near[...]
-    table[:, 256:288] = jnp.transpose(left[...].astype(f32)).astype(bf16)
-    table[:, 288:320] = jnp.transpose(right[...].astype(f32)).astype(bf16)
+    odd = lax.axis_index("gx") % 2 == 1
+    pair = [jnp.transpose(ghost[...].astype(f32)) for ghost in (left, right)]
+    table[:, 256:288] = jnp.where(odd, pair[1], pair[0]).astype(bf16)
+    table[:, 288:320] = jnp.where(odd, pair[0], pair[1]).astype(bf16)
     total[...] = jnp.zeros((512, 256), f32)
     own_place = iota((256, 256), 0).astype(f32).astype(bf16)
     ghost_place = iota((128, 256), 0).astype(f32).astype(bf16)
@@ -633,8 +635,10 @@
         name="spread",
     )(late_hidden, radial_out)
     up = [(i, (i + 1) % 8) for i in range(8)]
-    left = lax.ppermute(send_halo, "gx", up)
-    right = lax.ppermute(send_halo, "gx", [(b, a) for a, b in up])
+    first = [pair for a, b in up[1::2] for pair in ((a, b), (b, a))]
+    second = [pair for a, b in up[0::2] for pair in ((a, b), (b, a))]
+    left = lax.ppermute(send_halo, "gx", first)
+    right = lax.ppermute(send_halo, "gx", second)
 
     part = pl.pallas_call(
         field_kernel,

time: 109 us -> 108 us (level)
  transfers between devices with their start and end apart: 6 -> 6, of which waited for: 3 -> 2; matrix products, arithmetic and copies ran while one was open for 0% -> 0% of each run, Pallas kernels for 32% -> 33%
where the time goes in v4:
time: 108 us
  Pallas kernels  38.4 us (36%)
  starting transfers between devices  28.4 us (26%)
  waiting for transfers between devices  20 us (19%)
  between operations  14.4 us (13%)
  local copies, waits for them, and re-layouts  6.41 us (6%)
    all_to_all x1, waiting for transfers between devices, on_device(): sent = lax.all_to_all(moments, ('gx', 'yz'), 0, 0, tiled=True)  15.5 us
    pallas_call x1, Pallas kernels, on_device(): pl.pallas_call(message_kernel, out_shape=whole((16, 24, 128)), in_specs=[...  15.1 us
    all_to_all x1, starting transfers between devices, on_device(): sent = lax.all_to_all(moments, ('gx', 'yz'), 0, 0, tiled=True)  11.5 us
    unnamed x56, local copies, waits for them, and re-layouts  6.41 us
    all_to_all x1, starting transfers between devices, on_device(): returned = lax.all_to_all(returned, 'yz', 0, 0, tiled=True)  5.46 us
    all_to_all x1, starting transfers between devices, on_device(): coeffs = lax.all_to_all(coeffs, ('gx', 'yz'), 0, 0, tiled=True)  5.39 us
    pallas_call x1, Pallas kernels, on_device(): pl.pallas_call(spread_kernel, out_shape=whole((64, 512, 256), bf16), in_s...  5.05 us
    ppermute x1, starting transfers between devices, on_device(): left = lax.ppermute(send_halo, 'gx', first)  4.49 us
  transfers between devices with their start and end apart: 6, of which 2 were waited for; matrix products, arithmetic and copies ran while one was open for 0% of the time, Pallas kernels for 33%

profile of v4, /device:TPU:1, one launch (start us, length us, event | category | flops | bytes accessed | tf_op | source)
XLA Modules:
  0.0 107.5 jit_solution(17409657637938100516)
XLA Ops:
  7.3 2.0 %up.2 = (bf16[2,512,128]{2,1,0:T(8,128)(2,1)}, f32[8,256]{1,0:T(8,128)}) custom-call(bf16[256,512]{1,0:T(8,128)(2,1)} %feat.3, bf16[2,128,128]{2,1,0:T(8,128)(2,1)} %up.3, bf16[8,128]{1,0:T(8,128)(2,1)} %bitcast.20), custom_call_target="tpu_custom_call" | custom-call | flops 33554432 | bytes 1048576 | tf_op jit(solution)/shard_map/up/pallas_call | solution.py:528
  10.0 0.7 copy-done.5
  10.7 0.7 copy-done.15
  11.3 0.7 copy-done.18
  12.0 0.7 copy-done.20
  12.7 0.7 copy-done.22
  13.4 3.1 %moment.1 = (bf16[128,16,128]{2,1,0:T(8,128)(2,1)}, bf16[768,512]{1,0:T(8,128)(2,1)S(1)}, bf16[768,512]{1,0:T(8,128)(2,1)S(1)}, f32[40,256]{1,0:T(8,128)S(1)}) custom-call(s32[2]{0:T(128)S(1)} %copy-done.5, s32[2]{0:T(128)S(1)} %copy-done.22, f32[8,256]{1,0:T(8,128)S(1)} %copy-done.15, bf16[3,256]{1,0:T(4,128)(2,1)S(1)} %copy-done.18, ...), custom_call_target="tpu_custom_call" | custom-call | flops 1073741824 | bytes 3145728 | tf_op jit(solution)/shard_map/moment/pallas_call | solution.py:537
  16.5 0.9 copy-done.24
  17.4 0.9 copy-done.26
  18.3 11.5 %all-to-all-start = ((bf16[128,16,128]{2,1,0:T(8,128)(2,1)}), bf16[128,16,128]{2,1,0:T(8,128)(2,1)S(1)}, u32[]{:S(2)}, u32[]{:S(2)}) async-start(bf16[128,16,128]{2,1,0:T(8,128)(2,1)} %get-tuple-element.23), calls=%async_computation | async-start | bytes 1048576 | tf_op jit(solution)/shard_map/all_to_all | solution.py:561
  30.3 15.5 %all-to-all-done.sent = bf16[128,16,128]{2,1,0:T(8,128)(2,1)S(1)} async-done(((bf16[128,16,128]{2,1,0:T(8,128)(2,1)}), bf16[128,16,128]{2,1,0:T(8,128)(2,1)S(1)}, u32[]{:S(2)}, u32[]{:S(2)}) %all-to-all-start) | async-done | bytes 524320 | tf_op jit(solution)/shard_map/all_to_all | solution.py:561
  45.7 1.7 %weight.1 = (f32[128,8,128]{2,1,0:T(8,128)}, f32[16,128]{1,0:T(8,128)S(1)}, f32[1,256]{1,0:T(1,128)S(1)}, s32[4,128]{1,0:T(4,128)S(1)}, s32[6]{0:T(128)S(1)}) custom-call(bf16[128,16,128]{2,1,0:T(8,128)(2,1)S(1)} %all-to-all-done.sent, f32[16,128]{1,0:T(8,128)S(1)} %count.1.weights), custom_call_target="tpu_custom_call" | custom-call | flops 134217728 | bytes 1048576 | tf_op jit(solution)/shard_map/weight/pallas_call | solution.py:569
  48.0 5.4 %all-to-all-start.2 = ((f32[128,8,128]{2,1,0:T(8,128)}), f32[128,8,128]{2,1,0:T(8,128)S(1)}, u32[]{:S(2)}, u32[]{:S(2)}) async-start(f32[128,8,128]{2,1,0:T(8,128)} %get-tuple-element.36), calls=%async_computation.2 | async-start | bytes 1048576 | tf_op jit(solution)/shard_map/all_to_all | solution.py:585
  53.4 4.0 %radial.1 = (bf16[64,64,256]{2,1,0:T(8,128)(2,1)S(1)}, f32[3,64,256]{2,1,0:T(8,128)S(1)}) custom-call(f32[16,128]{1,0:T(8,128)S(1)} %get-tuple-element.26.table, s32[64,256]{1,0:T(8,128)S(1)} %bitcast.12, s32[1,256]{1,0:T(1,128)S(1)} %bitcast.17, bf16[8,64]{1,0:T(8,128)(2,1)S(1)} %copy-done.19, bf16[2,64,64]{2,1,0:T(8,128)(2,1)S(1)} %copy-done.13), custom_call_target="tpu_custom_call" | custom-call | flops 4294967296 | bytes 4194304 | tf_op jit(solution)/shard_map/radial/pallas_call | solution.py:587
  57.5 2.6 %halo.1 = bf16[32,512]{1,0:T(8,128)(2,1)} custom-call(s32[6]{0:T(128)} %copy-done.2, bf16[32,512,128]{2,1,0:T(8,128)(2,1)} %all-gather.2.cloned.1.call-done.first.second.own0.own1.low0.low1.high0.high1, bf16[32,512,128]{2,1,0:T(8,128)(2,1)} %all-gather.2.cloned.1.call-done.first.second.own0.own1.low0.low1.high0.high1, s32[1,32]{1,0:T(1,128)} %bitcast.9), custom_call_target="tpu_custom_call" | custom-call | flops 16777216 | bytes 262144 | tf_op jit(solution)/shard_map/halo/pallas_call | solution.py:600
  60.0 1.5 %collective-permute-start.1 = (bf16[32,512]{1,0:T(8,128)(2,1)}, bf16[32,512]{1,0:T(8,128)(2,1)S(1)}, u32[]{:S(2)}, u32[]{:S(2)}) collective-permute-start(bf16[32,512]{1,0:T(8,128)(2,1)} %halo.1), channel_id=1, source_target_pairs={{0,16},{16,0},{32,48},{48,32},{64,80},{80,64},{96,112},{112,96},{1... | collective-permute-start | bytes 98312 | tf_op jit(solution)/shard_map/ppermute | solution.py:641
  61.6 4.5 %collective-permute-start = (bf16[32,512]{1,0:T(8,128)(2,1)}, bf16[32,512]{1,0:T(8,128)(2,1)S(1)}, u32[]{:S(2)}, u32[]{:S(2)}) collective-permute-start(bf16[32,512]{1,0:T(8,128)(2,1)} %halo.1), channel_id=1, source_target_pairs={{16,32},{32,16},{48,64},{64,48},{80,96},{96,80},{112,0},{0,112},{1... | collective-permute-start | bytes 98312 | tf_op jit(solution)/shard_map/ppermute | solution.py:640
  66.0 5.0 %spread.1.radials = bf16[64,512,256]{2,1,0:T(8,128)(2,1)S(1)} custom-call(bf16[64,64,256]{2,1,0:T(8,128)(2,1)S(1)} %get-tuple-element.34.hidden, bf16[64,512]{1,0:T(8,128)(2,1)S(1)} %copy-done.9), custom_call_target="tpu_custom_call" | custom-call | flops 6442450944 | bytes 18874368 | tf_op jit(solution)/shard_map/spread/pallas_call | solution.py:627
  71.2 0.9 near.1
  72.2 15.1 %message.1 = f32[16,24,128]{2,1,0:T(8,128)} custom-call(s32[6]{0:T(128)S(1)} %copy-done.3, bf16[512,384]{1,0:T(8,128)(2,1)S(1)} %near.1, bf16[32,512]{1,0:T(8,128)(2,1)S(1)} %collective-permute-done.left, bf16[32,512]{1,0:T(8,128)(2,1)S(1)} %collective-permute-done.1.right, s32[64,256]{1,0:T(8,128)S(1)} %bitcast.13, ...), custom_call_target="tpu_custom_call" | custom-call | flops 12884901888 | bytes 4194304 | tf_op jit(solution)/shard_map/message/pallas_call | solution.py:652
  87.3 5.5 %all-to-all-start.1 = ((f32[16,24,128]{2,1,0:T(8,128)}), f32[16,24,128]{2,1,0:T(8,128)S(1)}, u32[]{:S(2)}, u32[]{:S(2)}) async-start(f32[16,24,128]{2,1,0:T(8,128)} %message.1), calls=%async_computation.1 | async-start | bytes 393216 | tf_op jit(solution)/shard_map/all_to_all | solution.py:675
  92.8 2.2 %field.1.own = f32[24,256]{1,0:T(8,128)S(1)} custom-call(f32[128,8,128]{2,1,0:T(8,128)S(1)} %all-to-all-done.2.coeffs, bf16[768,512]{1,0:T(8,128)(2,1)S(1)} %copy-done.25, bf16[768,512]{1,0:T(8,128)(2,1)S(1)} %copy-done.27, f32[40,256]{1,0:T(8,128)S(1)} %get-tuple-element.39.waves, bf16[256,512]{1,0:T(8,128)(2,1)S(1)} %copy-done.1, ...), custom_call_target="tpu_custom_call" | custom-call | flops 2147483648 | bytes 3145728 | tf_op jit(solution)/shard_map/field/pallas_call | solution.py:643
  95.0 4.4 %all-to-all-done.1.sent = f32[16,24,128]{2,1,0:T(8,128)S(1)} async-done(((f32[16,24,128]{2,1,0:T(8,128)}), f32[16,24,128]{2,1,0:T(8,128)S(1)}, u32[]{:S(2)}, u32[]{:S(2)}) %all-to-all-start.1) | async-done | bytes 196640 | tf_op jit(solution)/shard_map/all_to_all | solution.py:675
  99.4 1.3 %final.1 = (f32[3,256]{1,0:T(4,128)}, f32[1,256]{1,0:T(1,128)}) custom-call(s32[2]{0:T(128)S(1)} %copy-done.6, f32[16,24,128]{2,1,0:T(8,128)S(1)} %all-to-all-done.1.sent, f32[24,256]{1,0:T(8,128)S(1)} %field.1.own, f32[1,16]{1,0:T(1,128)S(1)} %bitcast.11), custom_call_target="tpu_custom_call" | custom-call | flops 16384 | bytes 65536 | tf_op jit(solution)/shard_map/final/pallas_call | solution.py:676
  (56 shorter events, 1.8 us)
Async XLA Ops:
  7.2 22.6 %copy-start.8 = (s32[3,4096]{1,0:T(4,128)S(1)}, s32[3,4096]{1,0:T(4,128)}, u32[]{:S(2)}) copy-start(s32[3,4096]{1,0:T(4,128)} %wave_index.1) | copy-start | bytes 147460
  7.2 46.2 %copy-start.13 = (bf16[2,64,64]{2,1,0:T(8,128)(2,1)S(1)}, bf16[2,64,64]{2,1,0:T(8,128)(2,1)}, u32[]{:S(2)}) copy-start(bf16[2,64,64]{2,1,0:T(8,128)(2,1)} %radial_mid.1) | copy-start | bytes 49156
  7.2 46.2 %copy-start.19 = (bf16[8,64]{1,0:T(8,128)(2,1)S(1)}, bf16[8,64]{1,0:T(8,128)(2,1)}, u32[]{:S(2)}) copy-start(bf16[8,64]{1,0:T(8,128)(2,1)} %radial_in.1) | copy-start | bytes 3076
  7.2 46.2 %copy-start.21 = (s32[256]{0:T(256)S(1)}, s32[256]{0:T(256)}, u32[]{:S(2)}) copy-start(s32[256]{0:T(256)} %param.28) | copy-start | bytes 3076
  7.2 46.2 %copy-start.10 = (s32[256,64]{0,1:T(8,128)S(1)}, s32[256,64]{0,1:T(8,128)}, u32[]{:S(2)}) copy-start(s32[256,64]{0,1:T(8,128)} %param.27) | copy-start | bytes 196612
  7.2 50.2 %all-gather.2.cloned.1.call-start = ((), (), s32[]{:S(2)}) async-start(), calls=%async_computation.3 | async-start | bytes 4456448 | tf_op jit(solution)/shard_map/all_gather | solution.py:535
  18.3 27.4 %all-to-all-start = ((bf16[128,16,128]{2,1,0:T(8,128)(2,1)}), bf16[128,16,128]{2,1,0:T(8,128)(2,1)S(1)}, u32[]{:S(2)}, u32[]{:S(2)}) async-start(bf16[128,16,128]{2,1,0:T(8,128)(2,1)} %get-tuple-element.23), calls=%async_computation | async-start | bytes 1048576 | tf_op jit(solution)/shard_map/all_to_all | solution.py:561
  48.0 39.3 %all-to-all-start.2 = ((f32[128,8,128]{2,1,0:T(8,128)}), f32[128,8,128]{2,1,0:T(8,128)S(1)}, u32[]{:S(2)}, u32[]{:S(2)}) async-start(f32[128,8,128]{2,1,0:T(8,128)} %get-tuple-element.36), calls=%async_computation.2 | async-start | bytes 1048576 | tf_op jit(solution)/shard_map/all_to_all | solution.py:585
  57.4 8.6 %copy-start.9 = (bf16[64,512]{1,0:T(8,128)(2,1)S(1)}, bf16[64,512]{1,0:T(8,128)(2,1)}, u32[]{:S(2)}) copy-start(bf16[64,512]{1,0:T(8,128)(2,1)} %radial_out.1) | copy-start | bytes 196612
  60.0 11.1 %copy-start = (bf16[32,512,128]{2,1,0:T(8,128)(2,1)S(1)}, bf16[32,512,128]{2,1,0:T(8,128)(2,1)}, u32[]{:S(2)}) copy-start(bf16[32,512,128]{2,1,0:T(8,128)(2,1)} %all-gather.2.cloned.1.call-done.first.second.own0.own1.low0.low1.high0.high1) | copy-start | bytes 12582916
  60.0 11.1 %copy-start.3 = (s32[6]{0:T(128)S(1)}, s32[6]{0:T(128)}, u32[]{:S(2)}) copy-start(s32[6]{0:T(128)} %copy-done.2) | copy-start | bytes 76
  60.0 12.0 %collective-permute-start.1 = (bf16[32,512]{1,0:T(8,128)(2,1)}, bf16[32,512]{1,0:T(8,128)(2,1)S(1)}, u32[]{:S(2)}, u32[]{:S(2)}) collective-permute-start(bf16[32,512]{1,0:T(8,128)(2,1)} %halo.1), channel_id=1, source_target_pairs={{0,16},{16,0},{32,48},{48,32},{64,80},{80,64},{96,112},{112,96},{1... | collective-permute-start | bytes 98312 | tf_op jit(solution)/shard_map/ppermute | solution.py:641
  61.6 10.5 %collective-permute-start = (bf16[32,512]{1,0:T(8,128)(2,1)}, bf16[32,512]{1,0:T(8,128)(2,1)S(1)}, u32[]{:S(2)}, u32[]{:S(2)}) collective-permute-start(bf16[32,512]{1,0:T(8,128)(2,1)} %halo.1), channel_id=1, source_target_pairs={{16,32},{32,16},{48,64},{64,48},{80,96},{96,80},{112,0},{0,112},{1... | collective-permute-start | bytes 98312 | tf_op jit(solution)/shard_map/ppermute | solution.py:640
  71.1 0.9 copy-start.11
  71.1 0.9 copy-start.14
  71.1 0.9 copy-start.16
  72.1 20.6 %copy-start.1 = (bf16[256,512]{1,0:T(8,128)(2,1)S(1)}, bf16[256,512]{1,0:T(8,128)(2,1)}, u32[]{:S(2)}) copy-start(bf16[256,512]{1,0:T(8,128)(2,1)} %feat.3) | copy-start | bytes 786436
  72.1 20.6 %copy-start.12 = (bf16[2,128,128]{2,1,0:T(8,128)(2,1)S(1)}, bf16[2,128,128]{2,1,0:T(8,128)(2,1)}, u32[]{:S(2)}) copy-start(bf16[2,128,128]{2,1,0:T(8,128)(2,1)} %skip_weight.1) | copy-start | bytes 196612
  72.1 20.6 %copy-start.17 = (f32[8,128]{1,0:T(8,128)S(1)}, f32[8,128]{1,0:T(8,128)}, u32[]{:S(2)}) copy-start(f32[8,128]{1,0:T(8,128)} %field_weight.1) | copy-start | bytes 12292
  72.1 20.6 %copy-start.25 = (bf16[768,512]{1,0:T(8,128)(2,1)S(1)}, bf16[768,512]{1,0:T(8,128)(2,1)}, u32[]{:S(2)}) copy-start(bf16[768,512]{1,0:T(8,128)(2,1)} %copy-done.24) | copy-start | bytes 2359300
  72.2 20.6 %copy-start.27 = (bf16[768,512]{1,0:T(8,128)(2,1)S(1)}, bf16[768,512]{1,0:T(8,128)(2,1)}, u32[]{:S(2)}) copy-start(bf16[768,512]{1,0:T(8,128)(2,1)} %copy-done.26) | copy-start | bytes 2359300
  87.3 12.2 %copy-start.6 = (s32[2]{0:T(128)S(1)}, s32[2]{0:T(128)}, u32[]{:S(2)}) copy-start(s32[2]{0:T(128)} %dest.3) | copy-start | bytes 28
  87.3 12.2 %copy-start.7 = (f32[16]{0:T(128)S(1)}, f32[16]{0:T(128)}, u32[]{:S(2)}) copy-start(f32[16]{0:T(128)} %param.40) | copy-start | bytes 196
  87.3 12.1 %all-to-all-start.1 = ((f32[16,24,128]{2,1,0:T(8,128)}), f32[16,24,128]{2,1,0:T(8,128)S(1)}, u32[]{:S(2)}, u32[]{:S(2)}) async-start(f32[16,24,128]{2,1,0:T(8,128)} %message.1), calls=%async_computation.1 | async-start | bytes 393216 | tf_op jit(solution)/shard_map/all_to_all | solution.py:675
  (10 other events, 7.3 us)
Sparse Core Ops, SparseCore 0:
  9.8 46.2 all-gather.1

commit v5 on v4

--- a/solution.py
+++ b/solution.py
@@ -410,10 +410,10 @@
     total,
 ):
     table[...] = near[...]
-    odd = lax.axis_index("gx") % 2 == 1
+    even = lax.axis_index("gx") % 2 == 0
     pair = [jnp.transpose(ghost[...].astype(f32)) for ghost in (left, right)]
-    table[:, 256:288] = jnp.where(odd, pair[1], pair[0]).astype(bf16)
-    table[:, 288:320] = jnp.where(odd, pair[0], pair[1]).astype(bf16)
+    table[:, 256:288] = jnp.where(even, pair[1], pair[0]).astype(bf16)
+    table[:, 288:320] = jnp.where(even, pair[0], pair[1]).astype(bf16)
     total[...] = jnp.zeros((512, 256), f32)
     own_place = iota((256, 256), 0).astype(f32).astype(bf16)
     ghost_place = iota((128, 256), 0).astype(f32).astype(bf16)
@@ -637,8 +637,8 @@
     up = [(i, (i + 1) % 8) for i in range(8)]
     first = [pair for a, b in up[1::2] for pair in ((a, b), (b, a))]
     second = [pair for a, b in up[0::2] for pair in ((a, b), (b, a))]
-    left = lax.ppermute(send_halo, "gx", first)
-    right = lax.ppermute(send_halo, "gx", second)
+    left = lax.ppermute(send_halo, "gx", second)
+    right = lax.ppermute(send_halo, "gx", first)
 
     part = pl.pallas_call(
         field_kernel,

time: 108 us -> 107 us (level)
  no operation moved by 1% of the time
where the time goes in v5:
time: 107 us
  Pallas kernels  38.4 us (36%)
  starting transfers between devices  27.8 us (26%)
  waiting for transfers between devices  20 us (19%)
  between operations  14.4 us (13%)
  local copies, waits for them, and re-layouts  6.41 us (6%)
    all_to_all x1, waiting for transfers between devices, on_device(): sent = lax.all_to_all(moments, ('gx', 'yz'), 0, 0, tiled=True)  15.5 us
    pallas_call x1, Pallas kernels, on_device(): pl.pallas_call(message_kernel, out_shape=whole((16, 24, 128)), in_specs=[...  15.1 us
    all_to_all x1, starting transfers between devices, on_device(): sent = lax.all_to_all(moments, ('gx', 'yz'), 0, 0, tiled=True)  11.5 us
    unnamed x56, local copies, waits for them, and re-layouts  6.41 us
    ppermute x1, starting transfers between devices, on_device(): right = lax.ppermute(send_halo, 'gx', first)  5.69 us
    all_to_all x1, starting transfers between devices, on_device(): coeffs = lax.all_to_all(coeffs, ('gx', 'yz'), 0, 0, tiled=True)  5.39 us
    all_to_all x1, starting transfers between devices, on_device(): returned = lax.all_to_all(returned, 'yz', 0, 0, tiled=True)  5.23 us
    pallas_call x1, Pallas kernels, on_device(): pl.pallas_call(spread_kernel, out_shape=whole((64, 512, 256), bf16), in_s...  5.02 us
  transfers between devices with their start and end apart: 6, of which 2 were waited for; matrix products, arithmetic and copies ran while one was open for 0% of the time, Pallas kernels for 33%

profile of v5, /device:TPU:1, one launch (start us, length us, event | category | flops | bytes accessed | tf_op | source)
XLA Modules:
  0.0 107.0 jit_solution(13697145222489426491)
XLA Ops:
  7.3 2.0 %up.2 = (bf16[2,512,128]{2,1,0:T(8,128)(2,1)}, f32[8,256]{1,0:T(8,128)}) custom-call(bf16[256,512]{1,0:T(8,128)(2,1)} %feat.3, bf16[2,128,128]{2,1,0:T(8,128)(2,1)} %up.3, bf16[8,128]{1,0:T(8,128)(2,1)} %bitcast.20), custom_call_target="tpu_custom_call" | custom-call | flops 33554432 | bytes 1048576 | tf_op jit(solution)/shard_map/up/pallas_call | solution.py:528
  9.3 0.6 copy-done.4
  10.0 0.7 copy-done.5
  10.7 0.7 copy-done.15
  11.3 0.7 copy-done.18
  12.0 0.7 copy-done.20
  12.7 0.7 copy-done.22
  13.4 3.1 %moment.1 = (bf16[128,16,128]{2,1,0:T(8,128)(2,1)}, bf16[768,512]{1,0:T(8,128)(2,1)S(1)}, bf16[768,512]{1,0:T(8,128)(2,1)S(1)}, f32[40,256]{1,0:T(8,128)S(1)}) custom-call(s32[2]{0:T(128)S(1)} %copy-done.5, s32[2]{0:T(128)S(1)} %copy-done.22, f32[8,256]{1,0:T(8,128)S(1)} %copy-done.15, bf16[3,256]{1,0:T(4,128)(2,1)S(1)} %copy-done.18, ...), custom_call_target="tpu_custom_call" | custom-call | flops 1073741824 | bytes 3145728 | tf_op jit(solution)/shard_map/moment/pallas_call | solution.py:537
  16.5 0.9 copy-done.24
  17.4 0.9 copy-done.26
  18.3 11.5 %all-to-all-start = ((bf16[128,16,128]{2,1,0:T(8,128)(2,1)}), bf16[128,16,128]{2,1,0:T(8,128)(2,1)S(1)}, u32[]{:S(2)}, u32[]{:S(2)}) async-start(bf16[128,16,128]{2,1,0:T(8,128)(2,1)} %get-tuple-element.23), calls=%async_computation | async-start | bytes 1048576 | tf_op jit(solution)/shard_map/all_to_all | solution.py:561
  30.3 15.5 %all-to-all-done.sent = bf16[128,16,128]{2,1,0:T(8,128)(2,1)S(1)} async-done(((bf16[128,16,128]{2,1,0:T(8,128)(2,1)}), bf16[128,16,128]{2,1,0:T(8,128)(2,1)S(1)}, u32[]{:S(2)}, u32[]{:S(2)}) %all-to-all-start) | async-done | bytes 524320 | tf_op jit(solution)/shard_map/all_to_all | solution.py:561
  45.7 1.7 %weight.1 = (f32[128,8,128]{2,1,0:T(8,128)}, f32[16,128]{1,0:T(8,128)S(1)}, f32[1,256]{1,0:T(1,128)S(1)}, s32[4,128]{1,0:T(4,128)S(1)}, s32[6]{0:T(128)S(1)}) custom-call(bf16[128,16,128]{2,1,0:T(8,128)(2,1)S(1)} %all-to-all-done.sent, f32[16,128]{1,0:T(8,128)S(1)} %count.1.weights), custom_call_target="tpu_custom_call" | custom-call | flops 134217728 | bytes 1048576 | tf_op jit(solution)/shard_map/weight/pallas_call | solution.py:569
  48.0 5.4 %all-to-all-start.2 = ((f32[128,8,128]{2,1,0:T(8,128)}), f32[128,8,128]{2,1,0:T(8,128)S(1)}, u32[]{:S(2)}, u32[]{:S(2)}) async-start(f32[128,8,128]{2,1,0:T(8,128)} %get-tuple-element.36), calls=%async_computation.2 | async-start | bytes 1048576 | tf_op jit(solution)/shard_map/all_to_all | solution.py:585
  53.4 4.0 %radial.1 = (bf16[64,64,256]{2,1,0:T(8,128)(2,1)S(1)}, f32[3,64,256]{2,1,0:T(8,128)S(1)}) custom-call(f32[16,128]{1,0:T(8,128)S(1)} %get-tuple-element.26.table, s32[64,256]{1,0:T(8,128)S(1)} %bitcast.12, s32[1,256]{1,0:T(1,128)S(1)} %bitcast.17, bf16[8,64]{1,0:T(8,128)(2,1)S(1)} %copy-done.19, bf16[2,64,64]{2,1,0:T(8,128)(2,1)S(1)} %copy-done.13), custom_call_target="tpu_custom_call" | custom-call | flops 4294967296 | bytes 4194304 | tf_op jit(solution)/shard_map/radial/pallas_call | solution.py:587
  57.5 2.6 %halo.1 = bf16[32,512]{1,0:T(8,128)(2,1)} custom-call(s32[6]{0:T(128)} %copy-done.2, bf16[32,512,128]{2,1,0:T(8,128)(2,1)} %all-gather.2.cloned.1.call-done.first.second.own0.own1.low0.low1.high0.high1, bf16[32,512,128]{2,1,0:T(8,128)(2,1)} %all-gather.2.cloned.1.call-done.first.second.own0.own1.low0.low1.high0.high1, s32[1,32]{1,0:T(1,128)} %bitcast.9), custom_call_target="tpu_custom_call" | custom-call | flops 16777216 | bytes 262144 | tf_op jit(solution)/shard_map/halo/pallas_call | solution.py:600
  60.0 5.7 %collective-permute-start.1 = (bf16[32,512]{1,0:T(8,128)(2,1)}, bf16[32,512]{1,0:T(8,128)(2,1)S(1)}, u32[]{:S(2)}, u32[]{:S(2)}) collective-permute-start(bf16[32,512]{1,0:T(8,128)(2,1)} %halo.1), channel_id=1, source_target_pairs={{16,32},{32,16},{48,64},{64,48},{80,96},{96,80},{112,0},{0,112},{1... | collective-permute-start | bytes 98312 | tf_op jit(solution)/shard_map/ppermute | solution.py:641
  65.7 5.0 %spread.1.radials = bf16[64,512,256]{2,1,0:T(8,128)(2,1)S(1)} custom-call(bf16[64,64,256]{2,1,0:T(8,128)(2,1)S(1)} %get-tuple-element.34.hidden, bf16[64,512]{1,0:T(8,128)(2,1)S(1)} %copy-done.9), custom_call_target="tpu_custom_call" | custom-call | flops 6442450944 | bytes 18874368 | tf_op jit(solution)/shard_map/spread/pallas_call | solution.py:627
  70.8 0.9 near.1
  71.8 15.1 %message.1 = f32[16,24,128]{2,1,0:T(8,128)} custom-call(s32[6]{0:T(128)S(1)} %copy-done.3, bf16[512,384]{1,0:T(8,128)(2,1)S(1)} %near.1, bf16[32,512]{1,0:T(8,128)(2,1)S(1)} %collective-permute-done.left, bf16[32,512]{1,0:T(8,128)(2,1)S(1)} %collective-permute-done.1.right, s32[64,256]{1,0:T(8,128)S(1)} %bitcast.13, ...), custom_call_target="tpu_custom_call" | custom-call | flops 12884901888 | bytes 4194304 | tf_op jit(solution)/shard_map/message/pallas_call | solution.py:652
  86.9 5.2 %all-to-all-start.1 = ((f32[16,24,128]{2,1,0:T(8,128)}), f32[16,24,128]{2,1,0:T(8,128)S(1)}, u32[]{:S(2)}, u32[]{:S(2)}) async-start(f32[16,24,128]{2,1,0:T(8,128)} %message.1), calls=%async_computation.1 | async-start | bytes 393216 | tf_op jit(solution)/shard_map/all_to_all | solution.py:675
  92.2 2.2 %field.1.own = f32[24,256]{1,0:T(8,128)S(1)} custom-call(f32[128,8,128]{2,1,0:T(8,128)S(1)} %all-to-all-done.2.coeffs, bf16[768,512]{1,0:T(8,128)(2,1)S(1)} %copy-done.25, bf16[768,512]{1,0:T(8,128)(2,1)S(1)} %copy-done.27, f32[40,256]{1,0:T(8,128)S(1)} %get-tuple-element.39.waves, bf16[256,512]{1,0:T(8,128)(2,1)S(1)} %copy-done.1, ...), custom_call_target="tpu_custom_call" | custom-call | flops 2147483648 | bytes 3145728 | tf_op jit(solution)/shard_map/field/pallas_call | solution.py:643
  94.4 4.4 %all-to-all-done.1.sent = f32[16,24,128]{2,1,0:T(8,128)S(1)} async-done(((f32[16,24,128]{2,1,0:T(8,128)}), f32[16,24,128]{2,1,0:T(8,128)S(1)}, u32[]{:S(2)}, u32[]{:S(2)}) %all-to-all-start.1) | async-done | bytes 196640 | tf_op jit(solution)/shard_map/all_to_all | solution.py:675
  98.8 1.3 %final.1 = (f32[3,256]{1,0:T(4,128)}, f32[1,256]{1,0:T(1,128)}) custom-call(s32[2]{0:T(128)S(1)} %copy-done.6, f32[16,24,128]{2,1,0:T(8,128)S(1)} %all-to-all-done.1.sent, f32[24,256]{1,0:T(8,128)S(1)} %field.1.own, f32[1,16]{1,0:T(1,128)S(1)} %bitcast.11), custom_call_target="tpu_custom_call" | custom-call | flops 16384 | bytes 65536 | tf_op jit(solution)/shard_map/final/pallas_call | solution.py:676
  (56 shorter events, 1.1 us)
Async XLA Ops:
  7.2 22.6 %copy-start.8 = (s32[3,4096]{1,0:T(4,128)S(1)}, s32[3,4096]{1,0:T(4,128)}, u32[]{:S(2)}) copy-start(s32[3,4096]{1,0:T(4,128)} %wave_index.1) | copy-start | bytes 147460
  7.2 46.2 %copy-start.13 = (bf16[2,64,64]{2,1,0:T(8,128)(2,1)S(1)}, bf16[2,64,64]{2,1,0:T(8,128)(2,1)}, u32[]{:S(2)}) copy-start(bf16[2,64,64]{2,1,0:T(8,128)(2,1)} %radial_mid.1) | copy-start | bytes 49156
  7.2 46.2 %copy-start.19 = (bf16[8,64]{1,0:T(8,128)(2,1)S(1)}, bf16[8,64]{1,0:T(8,128)(2,1)}, u32[]{:S(2)}) copy-start(bf16[8,64]{1,0:T(8,128)(2,1)} %radial_in.1) | copy-start | bytes 3076
  7.2 46.2 %copy-start.21 = (s32[256]{0:T(256)S(1)}, s32[256]{0:T(256)}, u32[]{:S(2)}) copy-start(s32[256]{0:T(256)} %param.28) | copy-start | bytes 3076
  7.2 46.2 %copy-start.10 = (s32[256,64]{0,1:T(8,128)S(1)}, s32[256,64]{0,1:T(8,128)}, u32[]{:S(2)}) copy-start(s32[256,64]{0,1:T(8,128)} %param.27) | copy-start | bytes 196612
  7.2 50.2 %all-gather.2.cloned.1.call-start = ((), (), s32[]{:S(2)}) async-start(), calls=%async_computation.3 | async-start | bytes 4456448 | tf_op jit(solution)/shard_map/all_gather | solution.py:535
  18.3 27.4 %all-to-all-start = ((bf16[128,16,128]{2,1,0:T(8,128)(2,1)}), bf16[128,16,128]{2,1,0:T(8,128)(2,1)S(1)}, u32[]{:S(2)}, u32[]{:S(2)}) async-start(bf16[128,16,128]{2,1,0:T(8,128)(2,1)} %get-tuple-element.23), calls=%async_computation | async-start | bytes 1048576 | tf_op jit(solution)/shard_map/all_to_all | solution.py:561
  48.0 38.9 %all-to-all-start.2 = ((f32[128,8,128]{2,1,0:T(8,128)}), f32[128,8,128]{2,1,0:T(8,128)S(1)}, u32[]{:S(2)}, u32[]{:S(2)}) async-start(f32[128,8,128]{2,1,0:T(8,128)} %get-tuple-element.36), calls=%async_computation.2 | async-start | bytes 1048576 | tf_op jit(solution)/shard_map/all_to_all | solution.py:585
  57.4 8.3 %copy-start.9 = (bf16[64,512]{1,0:T(8,128)(2,1)S(1)}, bf16[64,512]{1,0:T(8,128)(2,1)}, u32[]{:S(2)}) copy-start(bf16[64,512]{1,0:T(8,128)(2,1)} %radial_out.1) | copy-start | bytes 196612
  60.0 10.7 %copy-start = (bf16[32,512,128]{2,1,0:T(8,128)(2,1)S(1)}, bf16[32,512,128]{2,1,0:T(8,128)(2,1)}, u32[]{:S(2)}) copy-start(bf16[32,512,128]{2,1,0:T(8,128)(2,1)} %all-gather.2.cloned.1.call-done.first.second.own0.own1.low0.low1.high0.high1) | copy-start | bytes 12582916
  60.0 10.7 %copy-start.3 = (s32[6]{0:T(128)S(1)}, s32[6]{0:T(128)}, u32[]{:S(2)}) copy-start(s32[6]{0:T(128)} %copy-done.2) | copy-start | bytes 76
  60.0 11.7 %collective-permute-start.1 = (bf16[32,512]{1,0:T(8,128)(2,1)}, bf16[32,512]{1,0:T(8,128)(2,1)S(1)}, u32[]{:S(2)}, u32[]{:S(2)}) collective-permute-start(bf16[32,512]{1,0:T(8,128)(2,1)} %halo.1), channel_id=1, source_target_pairs={{16,32},{32,16},{48,64},{64,48},{80,96},{96,80},{112,0},{0,112},{1... | collective-permute-start | bytes 98312 | tf_op jit(solution)/shard_map/ppermute | solution.py:641
  65.7 6.0 %collective-permute-start = (bf16[32,512]{1,0:T(8,128)(2,1)}, bf16[32,512]{1,0:T(8,128)(2,1)S(1)}, u32[]{:S(2)}, u32[]{:S(2)}) collective-permute-start(bf16[32,512]{1,0:T(8,128)(2,1)} %halo.1), channel_id=1, source_target_pairs={{0,16},{16,0},{32,48},{48,32},{64,80},{80,64},{96,112},{112,96},{1... | collective-permute-start | bytes 98312 | tf_op jit(solution)/shard_map/ppermute | solution.py:640
  70.8 0.9 copy-start.11
  70.8 0.9 copy-start.14
  70.8 0.9 copy-start.16
  71.8 20.4 %copy-start.1 = (bf16[256,512]{1,0:T(8,128)(2,1)S(1)}, bf16[256,512]{1,0:T(8,128)(2,1)}, u32[]{:S(2)}) copy-start(bf16[256,512]{1,0:T(8,128)(2,1)} %feat.3) | copy-start | bytes 786436
  71.8 20.4 %copy-start.12 = (bf16[2,128,128]{2,1,0:T(8,128)(2,1)S(1)}, bf16[2,128,128]{2,1,0:T(8,128)(2,1)}, u32[]{:S(2)}) copy-start(bf16[2,128,128]{2,1,0:T(8,128)(2,1)} %skip_weight.1) | copy-start | bytes 196612
  71.8 20.4 %copy-start.17 = (f32[8,128]{1,0:T(8,128)S(1)}, f32[8,128]{1,0:T(8,128)}, u32[]{:S(2)}) copy-start(f32[8,128]{1,0:T(8,128)} %field_weight.1) | copy-start | bytes 12292
  71.8 20.4 %copy-start.25 = (bf16[768,512]{1,0:T(8,128)(2,1)S(1)}, bf16[768,512]{1,0:T(8,128)(2,1)}, u32[]{:S(2)}) copy-start(bf16[768,512]{1,0:T(8,128)(2,1)} %copy-done.24) | copy-start | bytes 2359300
  71.8 20.4 %copy-start.27 = (bf16[768,512]{1,0:T(8,128)(2,1)S(1)}, bf16[768,512]{1,0:T(8,128)(2,1)}, u32[]{:S(2)}) copy-start(bf16[768,512]{1,0:T(8,128)(2,1)} %copy-done.26) | copy-start | bytes 2359300
  86.9 11.9 %copy-start.6 = (s32[2]{0:T(128)S(1)}, s32[2]{0:T(128)}, u32[]{:S(2)}) copy-start(s32[2]{0:T(128)} %dest.3) | copy-start | bytes 28
  86.9 11.9 %copy-start.7 = (f32[16]{0:T(128)S(1)}, f32[16]{0:T(128)}, u32[]{:S(2)}) copy-start(f32[16]{0:T(128)} %param.40) | copy-start | bytes 196
  86.9 11.9 %all-to-all-start.1 = ((f32[16,24,128]{2,1,0:T(8,128)}), f32[16,24,128]{2,1,0:T(8,128)S(1)}, u32[]{:S(2)}, u32[]{:S(2)}) async-start(f32[16,24,128]{2,1,0:T(8,128)} %message.1), calls=%async_computation.1 | async-start | bytes 393216 | tf_op jit(solution)/shard_map/all_to_all | solution.py:675
  (10 other events, 7.3 us)
Sparse Core Ops, SparseCore 0:
  9.8 46.2 all-gather.1

commit v6 on v5

--- a/solution.py
+++ b/solution.py
@@ -16,7 +16,7 @@
 
 NX, NY, NZ = 16, 32, 2
 SLABS = 2 * NZ + 2
-RADIAL_GROUP, SLOT_GROUP = 16, 16
+RADIAL_GROUP, SLOT_GROUP = 32, 16
 
 
 def row_of(chunk, component):

time: 107 us -> 108 us (level)
  no operation moved by 1% of the time
where the time goes in v6:
time: 108 us; the launch traced here: 107 us
  Pallas kernels  38.6 us (36%)
  starting transfers between devices  27.8 us (26%)
  waiting for transfers between devices  20 us (19%)
  between operations  14.4 us (13%)
  local copies, waits for them, and re-layouts  6.41 us (6%)
    all_to_all x1, waiting for transfers between devices, on_device(): sent = lax.all_to_all(moments, ('gx', 'yz'), 0, 0, tiled=True)  15.5 us
    pallas_call x1, Pallas kernels, on_device(): pl.pallas_call(message_kernel, out_shape=whole((16, 24, 128)), in_specs=[...  15.1 us
    all_to_all x1, starting transfers between devices, on_device(): sent = lax.all_to_all(moments, ('gx', 'yz'), 0, 0, tiled=True)  11.5 us
    unnamed x56, local copies, waits for them, and re-layouts  6.41 us
    ppermute x1, starting transfers between devices, on_device(): right = lax.ppermute(send_halo, 'gx', first)  5.69 us
    all_to_all x1, starting transfers between devices, on_device(): coeffs = lax.all_to_all(coeffs, ('gx', 'yz'), 0, 0, tiled=True)  5.39 us
    all_to_all x1, starting transfers between devices, on_device(): returned = lax.all_to_all(returned, 'yz', 0, 0, tiled=True)  5.19 us
    pallas_call x1, Pallas kernels, on_device(): pl.pallas_call(spread_kernel, out_shape=whole((64, 512, 256), bf16), in_s...  5.04 us
  transfers between devices with their start and end apart: 6, of which 2 were waited for; matrix products, arithmetic and copies ran while one was open for 0% of the time, Pallas kernels for 33%

profile of v6, /device:TPU:1, one launch (start us, length us, event | category | flops | bytes accessed | tf_op | source)
XLA Modules:
  0.0 107.2 jit_solution(17629478345895832745)
XLA Ops:
  7.3 2.0 %up.2 = (bf16[2,512,128]{2,1,0:T(8,128)(2,1)}, f32[8,256]{1,0:T(8,128)}) custom-call(bf16[256,512]{1,0:T(8,128)(2,1)} %feat.3, bf16[2,128,128]{2,1,0:T(8,128)(2,1)} %up.3, bf16[8,128]{1,0:T(8,128)(2,1)} %bitcast.20), custom_call_target="tpu_custom_call" | custom-call | flops 33554432 | bytes 1048576 | tf_op jit(solution)/shard_map/up/pallas_call | solution.py:528
  9.3 0.6 copy-done.4
  10.0 0.7 copy-done.5
  10.7 0.7 copy-done.15
  11.3 0.7 copy-done.18
  12.0 0.7 copy-done.20
  12.7 0.7 copy-done.22
  13.4 3.1 %moment.1 = (bf16[128,16,128]{2,1,0:T(8,128)(2,1)}, bf16[768,512]{1,0:T(8,128)(2,1)S(1)}, bf16[768,512]{1,0:T(8,128)(2,1)S(1)}, f32[40,256]{1,0:T(8,128)S(1)}) custom-call(s32[2]{0:T(128)S(1)} %copy-done.5, s32[2]{0:T(128)S(1)} %copy-done.22, f32[8,256]{1,0:T(8,128)S(1)} %copy-done.15, bf16[3,256]{1,0:T(4,128)(2,1)S(1)} %copy-done.18, ...), custom_call_target="tpu_custom_call" | custom-call | flops 1073741824 | bytes 3145728 | tf_op jit(solution)/shard_map/moment/pallas_call | solution.py:537
  16.5 0.9 copy-done.24
  17.4 0.9 copy-done.26
  18.3 11.5 %all-to-all-start = ((bf16[128,16,128]{2,1,0:T(8,128)(2,1)}), bf16[128,16,128]{2,1,0:T(8,128)(2,1)S(1)}, u32[]{:S(2)}, u32[]{:S(2)}) async-start(bf16[128,16,128]{2,1,0:T(8,128)(2,1)} %get-tuple-element.23), calls=%async_computation | async-start | bytes 1048576 | tf_op jit(solution)/shard_map/all_to_all | solution.py:561
  30.2 15.5 %all-to-all-done.sent = bf16[128,16,128]{2,1,0:T(8,128)(2,1)S(1)} async-done(((bf16[128,16,128]{2,1,0:T(8,128)(2,1)}), bf16[128,16,128]{2,1,0:T(8,128)(2,1)S(1)}, u32[]{:S(2)}, u32[]{:S(2)}) %all-to-all-start) | async-done | bytes 524320 | tf_op jit(solution)/shard_map/all_to_all | solution.py:561
  45.7 1.7 %weight.1 = (f32[128,8,128]{2,1,0:T(8,128)}, f32[16,128]{1,0:T(8,128)S(1)}, f32[1,256]{1,0:T(1,128)S(1)}, s32[4,128]{1,0:T(4,128)S(1)}, s32[6]{0:T(128)S(1)}) custom-call(bf16[128,16,128]{2,1,0:T(8,128)(2,1)S(1)} %all-to-all-done.sent, f32[16,128]{1,0:T(8,128)S(1)} %count.1.weights), custom_call_target="tpu_custom_call" | custom-call | flops 134217728 | bytes 1048576 | tf_op jit(solution)/shard_map/weight/pallas_call | solution.py:569
  48.0 5.4 %all-to-all-start.2 = ((f32[128,8,128]{2,1,0:T(8,128)}), f32[128,8,128]{2,1,0:T(8,128)S(1)}, u32[]{:S(2)}, u32[]{:S(2)}) async-start(f32[128,8,128]{2,1,0:T(8,128)} %get-tuple-element.36), calls=%async_computation.2 | async-start | bytes 1048576 | tf_op jit(solution)/shard_map/all_to_all | solution.py:585
  53.4 4.2 %radial.1 = (bf16[64,64,256]{2,1,0:T(8,128)(2,1)S(1)}, f32[3,64,256]{2,1,0:T(8,128)S(1)}) custom-call(f32[16,128]{1,0:T(8,128)S(1)} %get-tuple-element.26.table, s32[64,256]{1,0:T(8,128)S(1)} %bitcast.12, s32[1,256]{1,0:T(1,128)S(1)} %bitcast.17, bf16[8,64]{1,0:T(8,128)(2,1)S(1)} %copy-done.19, bf16[2,64,64]{2,1,0:T(8,128)(2,1)S(1)} %copy-done.13), custom_call_target="tpu_custom_call" | custom-call | flops 4294967296 | bytes 4194304 | tf_op jit(solution)/shard_map/radial/pallas_call | solution.py:587
  57.7 2.6 %halo.1 = bf16[32,512]{1,0:T(8,128)(2,1)} custom-call(s32[6]{0:T(128)} %copy-done.2, bf16[32,512,128]{2,1,0:T(8,128)(2,1)} %all-gather.2.cloned.1.call-done.first.second.own0.own1.low0.low1.high0.high1, bf16[32,512,128]{2,1,0:T(8,128)(2,1)} %all-gather.2.cloned.1.call-done.first.second.own0.own1.low0.low1.high0.high1, s32[1,32]{1,0:T(1,128)} %bitcast.9), custom_call_target="tpu_custom_call" | custom-call | flops 16777216 | bytes 262144 | tf_op jit(solution)/shard_map/halo/pallas_call | solution.py:600
  60.3 5.7 %collective-permute-start.1 = (bf16[32,512]{1,0:T(8,128)(2,1)}, bf16[32,512]{1,0:T(8,128)(2,1)S(1)}, u32[]{:S(2)}, u32[]{:S(2)}) collective-permute-start(bf16[32,512]{1,0:T(8,128)(2,1)} %halo.1), channel_id=1, source_target_pairs={{16,32},{32,16},{48,64},{64,48},{80,96},{96,80},{112,0},{0,112},{1... | collective-permute-start | bytes 98312 | tf_op jit(solution)/shard_map/ppermute | solution.py:641
  66.0 5.0 %spread.1.radials = bf16[64,512,256]{2,1,0:T(8,128)(2,1)S(1)} custom-call(bf16[64,64,256]{2,1,0:T(8,128)(2,1)S(1)} %get-tuple-element.34.hidden, bf16[64,512]{1,0:T(8,128)(2,1)S(1)} %copy-done.9), custom_call_target="tpu_custom_call" | custom-call | flops 6442450944 | bytes 18874368 | tf_op jit(solution)/shard_map/spread/pallas_call | solution.py:627
  71.1 0.9 near.1
  72.1 15.1 %message.1 = f32[16,24,128]{2,1,0:T(8,128)} custom-call(s32[6]{0:T(128)S(1)} %copy-done.3, bf16[512,384]{1,0:T(8,128)(2,1)S(1)} %near.1, bf16[32,512]{1,0:T(8,128)(2,1)S(1)} %collective-permute-done.left, bf16[32,512]{1,0:T(8,128)(2,1)S(1)} %collective-permute-done.1.right, s32[64,256]{1,0:T(8,128)S(1)} %bitcast.13, ...), custom_call_target="tpu_custom_call" | custom-call | flops 12884901888 | bytes 4194304 | tf_op jit(solution)/shard_map/message/pallas_call | solution.py:652
  87.2 5.2 %all-to-all-start.1 = ((f32[16,24,128]{2,1,0:T(8,128)}), f32[16,24,128]{2,1,0:T(8,128)S(1)}, u32[]{:S(2)}, u32[]{:S(2)}) async-start(f32[16,24,128]{2,1,0:T(8,128)} %message.1), calls=%async_computation.1 | async-start | bytes 393216 | tf_op jit(solution)/shard_map/all_to_all | solution.py:675
  92.4 2.2 %field.1.own = f32[24,256]{1,0:T(8,128)S(1)} custom-call(f32[128,8,128]{2,1,0:T(8,128)S(1)} %all-to-all-done.2.coeffs, bf16[768,512]{1,0:T(8,128)(2,1)S(1)} %copy-done.25, bf16[768,512]{1,0:T(8,128)(2,1)S(1)} %copy-done.27, f32[40,256]{1,0:T(8,128)S(1)} %get-tuple-element.39.waves, bf16[256,512]{1,0:T(8,128)(2,1)S(1)} %copy-done.1, ...), custom_call_target="tpu_custom_call" | custom-call | flops 2147483648 | bytes 3145728 | tf_op jit(solution)/shard_map/field/pallas_call | solution.py:643
  94.6 4.4 %all-to-all-done.1.sent = f32[16,24,128]{2,1,0:T(8,128)S(1)} async-done(((f32[16,24,128]{2,1,0:T(8,128)}), f32[16,24,128]{2,1,0:T(8,128)S(1)}, u32[]{:S(2)}, u32[]{:S(2)}) %all-to-all-start.1) | async-done | bytes 196640 | tf_op jit(solution)/shard_map/all_to_all | solution.py:675
  99.1 1.3 %final.1 = (f32[3,256]{1,0:T(4,128)}, f32[1,256]{1,0:T(1,128)}) custom-call(s32[2]{0:T(128)S(1)} %copy-done.6, f32[16,24,128]{2,1,0:T(8,128)S(1)} %all-to-all-done.1.sent, f32[24,256]{1,0:T(8,128)S(1)} %field.1.own, f32[1,16]{1,0:T(1,128)S(1)} %bitcast.11), custom_call_target="tpu_custom_call" | custom-call | flops 16384 | bytes 65536 | tf_op jit(solution)/shard_map/final/pallas_call | solution.py:676
  (56 shorter events, 1.1 us)
Async XLA Ops:
  7.2 22.6 %copy-start.8 = (s32[3,4096]{1,0:T(4,128)S(1)}, s32[3,4096]{1,0:T(4,128)}, u32[]{:S(2)}) copy-start(s32[3,4096]{1,0:T(4,128)} %wave_index.1) | copy-start | bytes 147460
  7.2 46.2 %copy-start.13 = (bf16[2,64,64]{2,1,0:T(8,128)(2,1)S(1)}, bf16[2,64,64]{2,1,0:T(8,128)(2,1)}, u32[]{:S(2)}) copy-start(bf16[2,64,64]{2,1,0:T(8,128)(2,1)} %radial_mid.1) | copy-start | bytes 49156
  7.2 46.2 %copy-start.19 = (bf16[8,64]{1,0:T(8,128)(2,1)S(1)}, bf16[8,64]{1,0:T(8,128)(2,1)}, u32[]{:S(2)}) copy-start(bf16[8,64]{1,0:T(8,128)(2,1)} %radial_in.1) | copy-start | bytes 3076
  7.2 46.2 %copy-start.21 = (s32[256]{0:T(256)S(1)}, s32[256]{0:T(256)}, u32[]{:S(2)}) copy-start(s32[256]{0:T(256)} %param.28) | copy-start | bytes 3076
  7.2 46.2 %copy-start.10 = (s32[256,64]{0,1:T(8,128)S(1)}, s32[256,64]{0,1:T(8,128)}, u32[]{:S(2)}) copy-start(s32[256,64]{0,1:T(8,128)} %param.27) | copy-start | bytes 196612
  7.2 50.5 %all-gather.2.cloned.1.call-start = ((), (), s32[]{:S(2)}) async-start(), calls=%async_computation.3 | async-start | bytes 4456448 | tf_op jit(solution)/shard_map/all_gather | solution.py:535
  18.3 27.4 %all-to-all-start = ((bf16[128,16,128]{2,1,0:T(8,128)(2,1)}), bf16[128,16,128]{2,1,0:T(8,128)(2,1)S(1)}, u32[]{:S(2)}, u32[]{:S(2)}) async-start(bf16[128,16,128]{2,1,0:T(8,128)(2,1)} %get-tuple-element.23), calls=%async_computation | async-start | bytes 1048576 | tf_op jit(solution)/shard_map/all_to_all | solution.py:561
  48.0 39.2 %all-to-all-start.2 = ((f32[128,8,128]{2,1,0:T(8,128)}), f32[128,8,128]{2,1,0:T(8,128)S(1)}, u32[]{:S(2)}, u32[]{:S(2)}) async-start(f32[128,8,128]{2,1,0:T(8,128)} %get-tuple-element.36), calls=%async_computation.2 | async-start | bytes 1048576 | tf_op jit(solution)/shard_map/all_to_all | solution.py:585
  57.7 8.3 %copy-start.9 = (bf16[64,512]{1,0:T(8,128)(2,1)S(1)}, bf16[64,512]{1,0:T(8,128)(2,1)}, u32[]{:S(2)}) copy-start(bf16[64,512]{1,0:T(8,128)(2,1)} %radial_out.1) | copy-start | bytes 196612
  60.3 10.8 %copy-start = (bf16[32,512,128]{2,1,0:T(8,128)(2,1)S(1)}, bf16[32,512,128]{2,1,0:T(8,128)(2,1)}, u32[]{:S(2)}) copy-start(bf16[32,512,128]{2,1,0:T(8,128)(2,1)} %all-gather.2.cloned.1.call-done.first.second.own0.own1.low0.low1.high0.high1) | copy-start | bytes 12582916
  60.3 10.8 %copy-start.3 = (s32[6]{0:T(128)S(1)}, s32[6]{0:T(128)}, u32[]{:S(2)}) copy-start(s32[6]{0:T(128)} %copy-done.2) | copy-start | bytes 76
  60.3 11.7 %collective-permute-start.1 = (bf16[32,512]{1,0:T(8,128)(2,1)}, bf16[32,512]{1,0:T(8,128)(2,1)S(1)}, u32[]{:S(2)}, u32[]{:S(2)}) collective-permute-start(bf16[32,512]{1,0:T(8,128)(2,1)} %halo.1), channel_id=1, source_target_pairs={{16,32},{32,16},{48,64},{64,48},{80,96},{96,80},{112,0},{0,112},{1... | collective-permute-start | bytes 98312 | tf_op jit(solution)/shard_map/ppermute | solution.py:641
  66.0 6.0 %collective-permute-start = (bf16[32,512]{1,0:T(8,128)(2,1)}, bf16[32,512]{1,0:T(8,128)(2,1)S(1)}, u32[]{:S(2)}, u32[]{:S(2)}) collective-permute-start(bf16[32,512]{1,0:T(8,128)(2,1)} %halo.1), channel_id=1, source_target_pairs={{0,16},{16,0},{32,48},{48,32},{64,80},{80,64},{96,112},{112,96},{1... | collective-permute-start | bytes 98312 | tf_op jit(solution)/shard_map/ppermute | solution.py:640
  71.0 0.9 copy-start.11
  71.1 0.9 copy-start.14
  71.1 0.9 copy-start.16
  72.0 20.4 %copy-start.1 = (bf16[256,512]{1,0:T(8,128)(2,1)S(1)}, bf16[256,512]{1,0:T(8,128)(2,1)}, u32[]{:S(2)}) copy-start(bf16[256,512]{1,0:T(8,128)(2,1)} %feat.3) | copy-start | bytes 786436
  72.0 20.3 %copy-start.12 = (bf16[2,128,128]{2,1,0:T(8,128)(2,1)S(1)}, bf16[2,128,128]{2,1,0:T(8,128)(2,1)}, u32[]{:S(2)}) copy-start(bf16[2,128,128]{2,1,0:T(8,128)(2,1)} %skip_weight.1) | copy-start | bytes 196612
  72.1 20.3 %copy-start.17 = (f32[8,128]{1,0:T(8,128)S(1)}, f32[8,128]{1,0:T(8,128)}, u32[]{:S(2)}) copy-start(f32[8,128]{1,0:T(8,128)} %field_weight.1) | copy-start | bytes 12292
  72.1 20.3 %copy-start.25 = (bf16[768,512]{1,0:T(8,128)(2,1)S(1)}, bf16[768,512]{1,0:T(8,128)(2,1)}, u32[]{:S(2)}) copy-start(bf16[768,512]{1,0:T(8,128)(2,1)} %copy-done.24) | copy-start | bytes 2359300
  72.1 20.3 %copy-start.27 = (bf16[768,512]{1,0:T(8,128)(2,1)S(1)}, bf16[768,512]{1,0:T(8,128)(2,1)}, u32[]{:S(2)}) copy-start(bf16[768,512]{1,0:T(8,128)(2,1)} %copy-done.26) | copy-start | bytes 2359300
  87.2 11.9 %copy-start.6 = (s32[2]{0:T(128)S(1)}, s32[2]{0:T(128)}, u32[]{:S(2)}) copy-start(s32[2]{0:T(128)} %dest.3) | copy-start | bytes 28
  87.2 11.9 %copy-start.7 = (f32[16]{0:T(128)S(1)}, f32[16]{0:T(128)}, u32[]{:S(2)}) copy-start(f32[16]{0:T(128)} %param.40) | copy-start | bytes 196
  87.2 11.9 %all-to-all-start.1 = ((f32[16,24,128]{2,1,0:T(8,128)}), f32[16,24,128]{2,1,0:T(8,128)S(1)}, u32[]{:S(2)}, u32[]{:S(2)}) async-start(f32[16,24,128]{2,1,0:T(8,128)} %message.1), calls=%async_computation.1 | async-start | bytes 393216 | tf_op jit(solution)/shard_map/all_to_all | solution.py:675
  (10 other events, 7.3 us)
Sparse Core Ops, SparseCore 0:
  9.8 46.2 all-gather.1
